TPU v7x, 32 devices: a whole 2x2x4 slice. The times are simulated.
32 devices in a mesh: groups: 2 (over y), ctx: 4 (over z), heads: 2 (over x), rep: 2 (over core).
Axes of the slice: x: 2, y: 2, z: 4, core: 2. Of those that a mesh axis runs over, the one named last changes fastest.
Arguments:
- queries: bfloat16 [256, 128, 128], P(('groups', 'ctx', 'rep'), 'heads'), parts along dimension 0, may hold values from -10 to 10
- cache_keys: bfloat16 [16384, 8, 128], P(('groups', 'ctx'), 'heads'), parts along dimension 0, may hold values from -10 to 10
- cache_values: bfloat16 [16384, 8, 128], P(('groups', 'ctx'), 'heads'), parts along dimension 0, may hold values from -6 to 6
- new_keys: bfloat16 [256, 8, 128], P(('groups', 'ctx', 'rep'), 'heads'), parts along dimension 0, may hold values from -6 to 6
- new_values: bfloat16 [256, 8, 128], P(('groups', 'ctx', 'rep'), 'heads'), parts along dimension 0, may hold values from -6 to 6
- positions: int32 [256], P(('groups', 'ctx', 'rep')), parts along dimension 0, may hold values from 2 to 8191
- cached_length: int32 [2], P('groups'), parts along dimension 0, may hold values from 4096 to 8192
- out_weight: bfloat16 [16384, 16384], P('heads', ('ctx', 'rep')), may hold values from -0.046875 to 0.046875
Outputs:
- mixed: bfloat16 [256, 16384], P(('groups', 'heads'), ('ctx', 'rep')), parts along dimension 0
There are 2 independent parts, one for each index of `groups`. A program takes and returns all parts, laid end to end along the dimension named above; an argument that names none is the same for every part. Nothing has to cross between parts.
All inputs are finite; a program needn't handle non-finite values.
Results may differ from a plain program's by a relative error of at most 0.0052.
Values may be sent and summed in bfloat16 or wider, within the bound.
No kernel may reach another device: no remote copies, remote signals or barrier semaphores. Data moves between devices by JAX's collectives and lax.ppermute only.
A program may use at most 128 MiB of HBM per device.

v0:
```python
import jax
import jax.numpy as jnp
from jax import lax
from jax.sharding import PartitionSpec as P

NEG_FILL = -1e30


def shifted(value, axis, steps):
    count = lax.axis_size(axis)
    pairs = [(source, (source + steps) % count) for source in range(count)]
    return lax.ppermute(value, axis, pairs)


def combine(state, update):
    maxima, totals, values = state
    new_max, new_tot, new_val = update
    highest = jnp.maximum(maxima, new_max)
    keeping = jnp.exp(maxima - highest)
    taking = jnp.exp(new_max - highest)
    return (
        highest,
        keeping * totals + taking * new_tot,
        keeping[..., None] * values + taking[..., None] * new_val,
    )


def local(
    queries, cache_keys, cache_values, new_keys, new_values, positions, cached_length, out_weight
):
    token_rows, local_heads, head_size = queries.shape
    block_len, local_kv = (cache_keys.shape[0], cache_keys.shape[1])
    per_group = local_heads // local_kv
    scale_factor = head_size ** (-0.5)
    cycle_size = lax.axis_size("ctx")
    kv_start = lax.axis_index("ctx") * block_len
    limits = jnp.minimum(cached_length[0], positions)
    slot_index = kv_start + jnp.arange(block_len, dtype=jnp.int32)

    def attend(visitor, bounds):
        rows = visitor.shape[0]
        grouped = visitor.reshape(rows, local_kv, per_group, head_size)
        scores = (
            jnp.einsum("tkgd,jkd->tkgj", grouped, cache_keys, preferred_element_type=jnp.float32)
            * scale_factor
        )
        visible = (slot_index[None, :] < bounds[:, None])[:, None, None, :]
        scores = jnp.where(visible, scores, NEG_FILL)
        maxima = jnp.max(scores, axis=-1)
        weights = jnp.where(visible, jnp.exp(scores - maxima[..., None]), 0.0)
        totals = jnp.sum(weights, axis=-1)
        output = jnp.einsum(
            "tkgj,jkd->tkgd",
            weights.astype(jnp.bfloat16),
            cache_values,
            preferred_element_type=jnp.float32,
        )
        return (
            maxima.reshape(rows, local_heads),
            totals.reshape(rows, local_heads),
            output.reshape(rows, local_heads, head_size),
        )

    def partial_value(visitor, bounds):
        return attend(visitor, bounds)

    grouped_home = queries.reshape(token_rows, local_kv, per_group, head_size)
    own_score = (
        jnp.einsum("tkgd,tkd->tkg", grouped_home, new_keys, preferred_element_type=jnp.float32)
        * scale_factor
    )
    own_score = own_score.reshape(token_rows, local_heads)
    own_values = jnp.broadcast_to(
        new_values.astype(jnp.float32)[:, :, None, :], (token_rows, local_kv, per_group, head_size)
    ).reshape(token_rows, local_heads, head_size)
    start_state = (own_score, jnp.ones((token_rows, local_heads), jnp.float32), own_values)

    def travel(step, carry):
        visitor, bounds, state = carry
        state = combine(state, partial_value(visitor, bounds))
        visitor, bounds = shifted((visitor, bounds), "ctx", 1)
        state = shifted((state[0], state[1], state[2]), "ctx", 1)
        return (visitor, bounds, state)

    _, _, final = lax.fori_loop(0, cycle_size, travel, (queries, limits, start_state))
    attended = (
        (final[2] / final[1][..., None])
        .astype(jnp.bfloat16)
        .reshape(token_rows, local_heads * head_size)
    )
    terms = jnp.dot(
        lax.all_gather(attended, ("ctx", "rep"), axis=0, tiled=True),
        out_weight,
        preferred_element_type=jnp.float32,
    )
    return lax.psum_scatter(terms, "heads", scatter_dimension=0, tiled=True).astype(jnp.bfloat16)


def solution(mesh):
    return jax.shard_map(
        local,
        mesh=mesh,
        in_specs=(
            P(("groups", "ctx", "rep"), "heads", None),
            P(("groups", "ctx"), "heads", None),
            P(("groups", "ctx"), "heads", None),
            P(("groups", "ctx", "rep"), "heads", None),
            P(("groups", "ctx", "rep"), "heads", None),
            P(("groups", "ctx", "rep")),
            P("groups"),
            P("heads", ("ctx", "rep")),
        ),
        out_specs=P(("groups", "heads"), ("ctx", "rep")),
        check_vma=False,
    )
```

profile of v0, /device:TPU:0, one launch (start us, length us, event | category | flops | bytes accessed | tf_op | source)
XLA Modules:
  0.0 231.2 jit_solution(15120731785396124283)
XLA Ops:
  6.5 1.7 copy.71
  8.3 1.2 fusion.21
  9.5 0.1 reshape.53
  9.5 1.9 copy.27
  11.4 3.2 %copy.28 = bf16[2048,4,128]{2,0,1:T(8,128)(2,1)} copy(bf16[2048,4,128]{2,1,0:T(4,128)(2,1)} %param.12) | data formatting | bytes 4194304
  15.4 142.7 %while.19 = (s32[]{:T(128)}, bf16[16,64,128]{2,1,0:T(8,128)(2,1)}, s32[16]{0:T(128)S(1)}, f32[16,64]{1,0:T(8,128)S(1)}, f32[16,64]{1,0:T(8,128)S(1)}, /*index=5*...) while((s32[]{:T(128)}, bf16[16,64,128]{2,1,0:T(8,128)(2,1)}, ...), condition=%wide.region_3.4_spmd.clone, body=%wide.region_0.3_spmd.clone.sunk | while | flops 1101436928 | bytes 70263568 | solution.py:85
  15.4 1.0 copy.57
  16.4 0.1 broadcast_compare_fusion.2
  16.5 1.6 fusion.35
  18.1 3.2 %copy-done.1 = f32[4,2048,16,16]{1,3,2,0:T(8,128)} copy-done((f32[4,2048,16,16]{1,3,2,0:T(8,128)}, f32[4,2048,16,16]{1,3,2,0:T(8,128)S(1)}, u32[]{:S(2)}) %copy-start.1) | copy-done | bytes 8388632 | tf_op jit(solution)/shard_map/while
  21.3 2.7 %fusion.36 = f32[16,4,16]{2,0,1:T(8,128)S(1)} fusion(f32[4,2048,16,16]{1,3,2,0:T(8,128)S(1)} %get-tuple-element.197, f32[16,4,16]{2,0,1:T(8,128)S(1)} %get-tuple-element.198, pred[16,2048]{1,0:T(8,128)(4,1)S(1)} %broadcast_compare_fusion.2), kind=kLoop, calls=%fused_computation.5.clone.1 | loop fusion | flops 10484736 | bytes 8429568 | tf_op jit(solution)/shard_map/while/body/eval_jaxpr/reduce_sum | solution.py:51
  24.1 0.1 reshape.66
  24.1 0.1 reshape.67
  24.2 5.5 %fusion.37 = f32[16,4,16,128]{3,2,0,1:T(8,128)S(1)} fusion(bf16[2048,4,128]{2,0,1:T(8,128)(2,1)} %get-tuple-element.230, f32[4,2048,16,16]{1,3,2,0:T(8,128)} %copy-done.1, f32[16,4,16]{2,0,1:T(8,128)S(1)} %get-tuple-element.198, pred[16,2048]{1,0:T(8,128)(4,1)S(1)} %broadcast_compare_fusion.2), kind=kOutput, calls=%fused_computation.11.clone.1 | convolution fusion | flops 547356672 | bytes 11046912 | tf_op jit(solution)/shard_map/while/body/eval_jaxpr/tkgj,jkd->tkgd/dot_general | solution.py:52
  29.8 0.3 fusion.38
  30.1 3.1 %collective-permute-start.4 = (f32[16,64,128]{2,1,0:T(8,128)S(1)}, f32[16,64,128]{2,1,0:T(8,128)S(1)}, u32[]{:S(2)}, u32[]{:S(2)}) collective-permute-start(f32[16,64,128]{2,1,0:T(8,128)S(1)} %fusion.38), channel_id=1, source_target_pairs={{0,4},{4,8},{8,12},{12,0},{1,5},{5,9},{9,13},{13,1},{2,6},{6,10},{... | collective-permute-start | bytes 1572872 | tf_op jit(solution)/shard_map/while/body/eval_jaxpr/ppermute | solution.py:12
  33.2 1.6 collective-permute-start
  34.8 1.6 collective-permute-start.2
  36.4 0.1 collective-permute-start.3
  36.4 1.7 collective-permute-start.1
  38.2 15.1 %collective-permute-done.1 = s32[16]{0:T(128)S(1)} collective-permute-done((s32[16]{0:T(128)S(1)}, s32[16]{0:T(128)S(1)}, u32[]{:S(2)}, u32[]{:S(2)}) %collective-permute-start.1) | collective-permute-done | bytes 96 | tf_op jit(solution)/shard_map/while/body/eval_jaxpr/ppermute | solution.py:12
  53.3 1.0 copy.57
  54.2 0.1 broadcast_compare_fusion.2
  54.3 1.6 fusion.35
  56.0 3.2 %copy-done.1 = f32[4,2048,16,16]{1,3,2,0:T(8,128)} copy-done((f32[4,2048,16,16]{1,3,2,0:T(8,128)}, f32[4,2048,16,16]{1,3,2,0:T(8,128)S(1)}, u32[]{:S(2)}) %copy-start.1) | copy-done | bytes 8388632 | tf_op jit(solution)/shard_map/while
  59.2 2.7 %fusion.36 = f32[16,4,16]{2,0,1:T(8,128)S(1)} fusion(f32[4,2048,16,16]{1,3,2,0:T(8,128)S(1)} %get-tuple-element.197, f32[16,4,16]{2,0,1:T(8,128)S(1)} %get-tuple-element.198, pred[16,2048]{1,0:T(8,128)(4,1)S(1)} %broadcast_compare_fusion.2), kind=kLoop, calls=%fused_computation.5.clone.1 | loop fusion | flops 10484736 | bytes 8429568 | tf_op jit(solution)/shard_map/while/body/eval_jaxpr/reduce_sum | solution.py:51
  61.9 0.1 reshape.66
  62.0 0.1 reshape.67
  62.1 5.5 %fusion.37 = f32[16,4,16,128]{3,2,0,1:T(8,128)S(1)} fusion(bf16[2048,4,128]{2,0,1:T(8,128)(2,1)} %get-tuple-element.230, f32[4,2048,16,16]{1,3,2,0:T(8,128)} %copy-done.1, f32[16,4,16]{2,0,1:T(8,128)S(1)} %get-tuple-element.198, pred[16,2048]{1,0:T(8,128)(4,1)S(1)} %broadcast_compare_fusion.2), kind=kOutput, calls=%fused_computation.11.clone.1 | convolution fusion | flops 547356672 | bytes 11046912 | tf_op jit(solution)/shard_map/while/body/eval_jaxpr/tkgj,jkd->tkgd/dot_general | solution.py:52
  67.6 0.3 fusion.38
  68.0 1.3 collective-permute-start
  69.3 1.6 collective-permute-start.2
  70.9 2.1 collective-permute-start.3
  73.0 16.0 %collective-permute-done.1 = s32[16]{0:T(128)S(1)} collective-permute-done((s32[16]{0:T(128)S(1)}, s32[16]{0:T(128)S(1)}, u32[]{:S(2)}, u32[]{:S(2)}) %collective-permute-start.1) | collective-permute-done | bytes 96 | tf_op jit(solution)/shard_map/while/body/eval_jaxpr/ppermute | solution.py:12
  89.1 1.0 copy.57
  90.0 0.1 broadcast_compare_fusion.2
  90.1 1.6 fusion.35
  91.7 3.2 %copy-done.1 = f32[4,2048,16,16]{1,3,2,0:T(8,128)} copy-done((f32[4,2048,16,16]{1,3,2,0:T(8,128)}, f32[4,2048,16,16]{1,3,2,0:T(8,128)S(1)}, u32[]{:S(2)}) %copy-start.1) | copy-done | bytes 8388632 | tf_op jit(solution)/shard_map/while
  94.9 2.7 %fusion.36 = f32[16,4,16]{2,0,1:T(8,128)S(1)} fusion(f32[4,2048,16,16]{1,3,2,0:T(8,128)S(1)} %get-tuple-element.197, f32[16,4,16]{2,0,1:T(8,128)S(1)} %get-tuple-element.198, pred[16,2048]{1,0:T(8,128)(4,1)S(1)} %broadcast_compare_fusion.2), kind=kLoop, calls=%fused_computation.5.clone.1 | loop fusion | flops 10484736 | bytes 8429568 | tf_op jit(solution)/shard_map/while/body/eval_jaxpr/reduce_sum | solution.py:51
  97.7 0.1 reshape.66
  97.8 0.1 reshape.67
  97.9 5.5 %fusion.37 = f32[16,4,16,128]{3,2,0,1:T(8,128)S(1)} fusion(bf16[2048,4,128]{2,0,1:T(8,128)(2,1)} %get-tuple-element.230, f32[4,2048,16,16]{1,3,2,0:T(8,128)} %copy-done.1, f32[16,4,16]{2,0,1:T(8,128)S(1)} %get-tuple-element.198, pred[16,2048]{1,0:T(8,128)(4,1)S(1)} %broadcast_compare_fusion.2), kind=kOutput, calls=%fused_computation.11.clone.1 | convolution fusion | flops 547356672 | bytes 11046912 | tf_op jit(solution)/shard_map/while/body/eval_jaxpr/tkgj,jkd->tkgd/dot_general | solution.py:52
  103.4 0.3 fusion.38
  103.9 0.7 collective-permute-start.2
  104.6 4.2 %collective-permute-start.3 = (f32[16,64]{1,0:T(8,128)S(1)}, f32[16,64]{1,0:T(8,128)S(1)}, u32[]{:S(2)}, u32[]{:S(2)}) collective-permute-start(f32[16,64]{1,0:T(8,128)S(1)} %get-tuple-element.200), channel_id=1, source_target_pairs={{0,4},{4,8},{8,12},{12,0},{1,5},{5,9},{9,13},{13,1},{2,6},{6,10},{... | collective-permute-start | bytes 12296 | tf_op jit(solution)/shard_map/while/body/eval_jaxpr/ppermute | solution.py:12
  108.8 15.1 %collective-permute-done.1 = s32[16]{0:T(128)S(1)} collective-permute-done((s32[16]{0:T(128)S(1)}, s32[16]{0:T(128)S(1)}, u32[]{:S(2)}, u32[]{:S(2)}) %collective-permute-start.1) | collective-permute-done | bytes 96 | tf_op jit(solution)/shard_map/while/body/eval_jaxpr/ppermute | solution.py:12
  124.0 1.0 copy.57
  124.9 0.1 broadcast_compare_fusion.2
  125.0 1.6 fusion.35
  126.7 3.2 %copy-done.1 = f32[4,2048,16,16]{1,3,2,0:T(8,128)} copy-done((f32[4,2048,16,16]{1,3,2,0:T(8,128)}, f32[4,2048,16,16]{1,3,2,0:T(8,128)S(1)}, u32[]{:S(2)}) %copy-start.1) | copy-done | bytes 8388632 | tf_op jit(solution)/shard_map/while
  129.9 2.7 %fusion.36 = f32[16,4,16]{2,0,1:T(8,128)S(1)} fusion(f32[4,2048,16,16]{1,3,2,0:T(8,128)S(1)} %get-tuple-element.197, f32[16,4,16]{2,0,1:T(8,128)S(1)} %get-tuple-element.198, pred[16,2048]{1,0:T(8,128)(4,1)S(1)} %broadcast_compare_fusion.2), kind=kLoop, calls=%fused_computation.5.clone.1 | loop fusion | flops 10484736 | bytes 8429568 | tf_op jit(solution)/shard_map/while/body/eval_jaxpr/reduce_sum | solution.py:51
  132.6 0.1 reshape.66
  132.7 0.1 reshape.67
  132.8 5.5 %fusion.37 = f32[16,4,16,128]{3,2,0,1:T(8,128)S(1)} fusion(bf16[2048,4,128]{2,0,1:T(8,128)(2,1)} %get-tuple-element.230, f32[4,2048,16,16]{1,3,2,0:T(8,128)} %copy-done.1, f32[16,4,16]{2,0,1:T(8,128)S(1)} %get-tuple-element.198, pred[16,2048]{1,0:T(8,128)(4,1)S(1)} %broadcast_compare_fusion.2), kind=kOutput, calls=%fused_computation.11.clone.1 | convolution fusion | flops 547356672 | bytes 11046912 | tf_op jit(solution)/shard_map/while/body/eval_jaxpr/tkgj,jkd->tkgd/dot_general | solution.py:52
  138.3 0.3 fusion.38
  138.8 0.5 collective-permute-start.2
  139.4 4.3 %collective-permute-start.3 = (f32[16,64]{1,0:T(8,128)S(1)}, f32[16,64]{1,0:T(8,128)S(1)}, u32[]{:S(2)}, u32[]{:S(2)}) collective-permute-start(f32[16,64]{1,0:T(8,128)S(1)} %get-tuple-element.200), channel_id=1, source_target_pairs={{0,4},{4,8},{8,12},{12,0},{1,5},{5,9},{9,13},{13,1},{2,6},{6,10},{... | collective-permute-start | bytes 12296 | tf_op jit(solution)/shard_map/while/body/eval_jaxpr/ppermute | solution.py:12
  143.8 14.3 %collective-permute-done.1 = s32[16]{0:T(128)S(1)} collective-permute-done((s32[16]{0:T(128)S(1)}, s32[16]{0:T(128)S(1)}, u32[]{:S(2)}, u32[]{:S(2)}) %collective-permute-start.1) | collective-permute-done | bytes 96 | tf_op jit(solution)/shard_map/while/body/eval_jaxpr/ppermute | solution.py:12
  158.1 0.2 divide_convert_fusion
  158.3 0.9 copy.41
  159.2 26.8 %all-gather.2.cloned.1.call-done = bf16[128,8192]{1,0:T(8,128)(2,1)} async-done(((bf16[16,8192]{1,0:T(8,128)(2,1)}), bf16[128,8192]{1,0:T(8,128)(2,1)}) %all-gather.2.cloned.1.call-update) | async-done | bytes 2097168 | tf_op jit(solution)/shard_map/all_gather | solution.py:92
  186.0 16.7 %fusion.23 = f32[128,2048]{1,0:T(8,128)} fusion(bf16[128,8192]{1,0:T(8,128)(2,1)} %all-gather.2.cloned.1.call-done, bf16[8192,2048]{1,0:T(8,128)(2,1)} %param.17), kind=kOutput, calls=%fused_computation.29 | convolution fusion | flops 4294967296 | bytes 36700160 | tf_op jit(solution)/shard_map/dot_general | solution.py:91
  202.7 19.9 %reduce-scatter.2.cloned.1.call-done = f32[64,2048]{1,0:T(8,128)} async-done(((f32[128,2048]{1,0:T(8,128)}), f32[64,2048]{1,0:T(8,128)}) %reduce-scatter.2.cloned.1.call-update) | async-done | bytes 524304 | tf_op jit(solution)/shard_map/reduce_scatter | solution.py:96
  222.6 1.8 convert_element_type.14
  (66 shorter events, 1.2 us)
Async XLA Ops:
  6.5 1.7 copy-start
  6.5 8.8 %copy-start.2 = (bf16[16,4,128]{2,1,0:T(4,128)(2,1)S(1)}, bf16[16,4,128]{2,1,0:T(4,128)(2,1)}, u32[]{:S(2)}) copy-start(bf16[16,4,128]{2,1,0:T(4,128)(2,1)} %param.14) | copy-start | bytes 49156
  6.5 8.8 %copy-start.3 = (s32[16]{0:T(128)S(1)}, s32[16]{0:T(128)}, u32[]{:S(2)}) copy-start(s32[16]{0:T(128)} %param.15) | copy-start | bytes 196
  6.5 179.5 %all-gather.2.cloned.1.call-start = ((), (), s32[]{:S(2)}) async-start(), calls=%async_computation.1 | async-start | bytes 2359296 | tf_op jit(solution)/shard_map/all_gather | solution.py:92
  18.1 3.2 %copy-start.1 = (f32[4,2048,16,16]{1,3,2,0:T(8,128)}, f32[4,2048,16,16]{1,3,2,0:T(8,128)S(1)}, u32[]{:S(2)}) copy-start(f32[4,2048,16,16]{1,3,2,0:T(8,128)S(1)} %get-tuple-element.197) | copy-start | bytes 25165828 | tf_op jit(solution)/shard_map/while
  30.1 23.1 %collective-permute-start.4 = (f32[16,64,128]{2,1,0:T(8,128)S(1)}, f32[16,64,128]{2,1,0:T(8,128)S(1)}, u32[]{:S(2)}, u32[]{:S(2)}) collective-permute-start(f32[16,64,128]{2,1,0:T(8,128)S(1)} %fusion.38), channel_id=1, source_target_pairs={{0,4},{4,8},{8,12},{12,0},{1,5},{5,9},{9,13},{13,1},{2,6},{6,10},{... | collective-permute-start | bytes 1572872 | tf_op jit(solution)/shard_map/while/body/eval_jaxpr/ppermute | solution.py:12
  33.2 20.0 %collective-permute-start = (bf16[16,64,128]{2,1,0:T(8,128)(2,1)S(1)}, bf16[16,64,128]{2,1,0:T(8,128)(2,1)}, u32[]{:S(2)}, u32[]{:S(2)}) collective-permute-start(bf16[16,64,128]{2,1,0:T(8,128)(2,1)S(1)} %copy.57), channel_id=1, source_target_pairs={{0,4},{4,8},{8,12},{12,0},{1,5},{5,9},{9,13},{13,1},{2,6},{6,10},{... | collective-permute-start | bytes 786440 | tf_op jit(solution)/shard_map/while/body/eval_jaxpr/ppermute | solution.py:12
  34.8 18.4 %collective-permute-start.2 = (f32[16,64]{1,0:T(8,128)S(1)}, f32[16,64]{1,0:T(8,128)S(1)}, u32[]{:S(2)}, u32[]{:S(2)}) collective-permute-start(f32[16,64]{1,0:T(8,128)S(1)} %get-tuple-element.199), channel_id=1, source_target_pairs={{0,4},{4,8},{8,12},{12,0},{1,5},{5,9},{9,13},{13,1},{2,6},{6,10},{... | collective-permute-start | bytes 12296 | tf_op jit(solution)/shard_map/while/body/eval_jaxpr/ppermute | solution.py:12
  36.4 16.9 %collective-permute-start.3 = (f32[16,64]{1,0:T(8,128)S(1)}, f32[16,64]{1,0:T(8,128)S(1)}, u32[]{:S(2)}, u32[]{:S(2)}) collective-permute-start(f32[16,64]{1,0:T(8,128)S(1)} %get-tuple-element.200), channel_id=1, source_target_pairs={{0,4},{4,8},{8,12},{12,0},{1,5},{5,9},{9,13},{13,1},{2,6},{6,10},{... | collective-permute-start | bytes 12296 | tf_op jit(solution)/shard_map/while/body/eval_jaxpr/ppermute | solution.py:12
  36.4 16.8 %collective-permute-start.1 = (s32[16]{0:T(128)S(1)}, s32[16]{0:T(128)S(1)}, u32[]{:S(2)}, u32[]{:S(2)}) collective-permute-start(s32[16]{0:T(128)S(1)} %copy.58), channel_id=1, source_target_pairs={{0,4},{4,8},{8,12},{12,0},{1,5},{5,9},{9,13},{13,1},{2,6},{6,10},{... | collective-permute-start | bytes 200 | tf_op jit(solution)/shard_map/while/body/eval_jaxpr/ppermute | solution.py:12
  55.9 3.2 %copy-start.1 = (f32[4,2048,16,16]{1,3,2,0:T(8,128)}, f32[4,2048,16,16]{1,3,2,0:T(8,128)S(1)}, u32[]{:S(2)}) copy-start(f32[4,2048,16,16]{1,3,2,0:T(8,128)S(1)} %get-tuple-element.197) | copy-start | bytes 25165828 | tf_op jit(solution)/shard_map/while
  68.0 21.0 %collective-permute-start.4 = (f32[16,64,128]{2,1,0:T(8,128)S(1)}, f32[16,64,128]{2,1,0:T(8,128)S(1)}, u32[]{:S(2)}, u32[]{:S(2)}) collective-permute-start(f32[16,64,128]{2,1,0:T(8,128)S(1)} %fusion.38), channel_id=1, source_target_pairs={{0,4},{4,8},{8,12},{12,0},{1,5},{5,9},{9,13},{13,1},{2,6},{6,10},{... | collective-permute-start | bytes 1572872 | tf_op jit(solution)/shard_map/while/body/eval_jaxpr/ppermute | solution.py:12
  68.0 21.0 %collective-permute-start = (bf16[16,64,128]{2,1,0:T(8,128)(2,1)S(1)}, bf16[16,64,128]{2,1,0:T(8,128)(2,1)}, u32[]{:S(2)}, u32[]{:S(2)}) collective-permute-start(bf16[16,64,128]{2,1,0:T(8,128)(2,1)S(1)} %copy.57), channel_id=1, source_target_pairs={{0,4},{4,8},{8,12},{12,0},{1,5},{5,9},{9,13},{13,1},{2,6},{6,10},{... | collective-permute-start | bytes 786440 | tf_op jit(solution)/shard_map/while/body/eval_jaxpr/ppermute | solution.py:12
  69.3 19.7 %collective-permute-start.2 = (f32[16,64]{1,0:T(8,128)S(1)}, f32[16,64]{1,0:T(8,128)S(1)}, u32[]{:S(2)}, u32[]{:S(2)}) collective-permute-start(f32[16,64]{1,0:T(8,128)S(1)} %get-tuple-element.199), channel_id=1, source_target_pairs={{0,4},{4,8},{8,12},{12,0},{1,5},{5,9},{9,13},{13,1},{2,6},{6,10},{... | collective-permute-start | bytes 12296 | tf_op jit(solution)/shard_map/while/body/eval_jaxpr/ppermute | solution.py:12
  70.9 18.1 %collective-permute-start.3 = (f32[16,64]{1,0:T(8,128)S(1)}, f32[16,64]{1,0:T(8,128)S(1)}, u32[]{:S(2)}, u32[]{:S(2)}) collective-permute-start(f32[16,64]{1,0:T(8,128)S(1)} %get-tuple-element.200), channel_id=1, source_target_pairs={{0,4},{4,8},{8,12},{12,0},{1,5},{5,9},{9,13},{13,1},{2,6},{6,10},{... | collective-permute-start | bytes 12296 | tf_op jit(solution)/shard_map/while/body/eval_jaxpr/ppermute | solution.py:12
  73.0 16.0 %collective-permute-start.1 = (s32[16]{0:T(128)S(1)}, s32[16]{0:T(128)S(1)}, u32[]{:S(2)}, u32[]{:S(2)}) collective-permute-start(s32[16]{0:T(128)S(1)} %copy.58), channel_id=1, source_target_pairs={{0,4},{4,8},{8,12},{12,0},{1,5},{5,9},{9,13},{13,1},{2,6},{6,10},{... | collective-permute-start | bytes 200 | tf_op jit(solution)/shard_map/while/body/eval_jaxpr/ppermute | solution.py:12
  91.7 3.2 %copy-start.1 = (f32[4,2048,16,16]{1,3,2,0:T(8,128)}, f32[4,2048,16,16]{1,3,2,0:T(8,128)S(1)}, u32[]{:S(2)}) copy-start(f32[4,2048,16,16]{1,3,2,0:T(8,128)S(1)} %get-tuple-element.197) | copy-start | bytes 25165828 | tf_op jit(solution)/shard_map/while
  103.7 20.2 %collective-permute-start.4 = (f32[16,64,128]{2,1,0:T(8,128)S(1)}, f32[16,64,128]{2,1,0:T(8,128)S(1)}, u32[]{:S(2)}, u32[]{:S(2)}) collective-permute-start(f32[16,64,128]{2,1,0:T(8,128)S(1)} %fusion.38), channel_id=1, source_target_pairs={{0,4},{4,8},{8,12},{12,0},{1,5},{5,9},{9,13},{13,1},{2,6},{6,10},{... | collective-permute-start | bytes 1572872 | tf_op jit(solution)/shard_map/while/body/eval_jaxpr/ppermute | solution.py:12
  103.8 20.1 %collective-permute-start = (bf16[16,64,128]{2,1,0:T(8,128)(2,1)S(1)}, bf16[16,64,128]{2,1,0:T(8,128)(2,1)}, u32[]{:S(2)}, u32[]{:S(2)}) collective-permute-start(bf16[16,64,128]{2,1,0:T(8,128)(2,1)S(1)} %copy.57), channel_id=1, source_target_pairs={{0,4},{4,8},{8,12},{12,0},{1,5},{5,9},{9,13},{13,1},{2,6},{6,10},{... | collective-permute-start | bytes 786440 | tf_op jit(solution)/shard_map/while/body/eval_jaxpr/ppermute | solution.py:12
  103.9 20.1 %collective-permute-start.2 = (f32[16,64]{1,0:T(8,128)S(1)}, f32[16,64]{1,0:T(8,128)S(1)}, u32[]{:S(2)}, u32[]{:S(2)}) collective-permute-start(f32[16,64]{1,0:T(8,128)S(1)} %get-tuple-element.199), channel_id=1, source_target_pairs={{0,4},{4,8},{8,12},{12,0},{1,5},{5,9},{9,13},{13,1},{2,6},{6,10},{... | collective-permute-start | bytes 12296 | tf_op jit(solution)/shard_map/while/body/eval_jaxpr/ppermute | solution.py:12
  104.6 19.4 %collective-permute-start.3 = (f32[16,64]{1,0:T(8,128)S(1)}, f32[16,64]{1,0:T(8,128)S(1)}, u32[]{:S(2)}, u32[]{:S(2)}) collective-permute-start(f32[16,64]{1,0:T(8,128)S(1)} %get-tuple-element.200), channel_id=1, source_target_pairs={{0,4},{4,8},{8,12},{12,0},{1,5},{5,9},{9,13},{13,1},{2,6},{6,10},{... | collective-permute-start | bytes 12296 | tf_op jit(solution)/shard_map/while/body/eval_jaxpr/ppermute | solution.py:12
  108.8 15.2 %collective-permute-start.1 = (s32[16]{0:T(128)S(1)}, s32[16]{0:T(128)S(1)}, u32[]{:S(2)}, u32[]{:S(2)}) collective-permute-start(s32[16]{0:T(128)S(1)} %copy.58), channel_id=1, source_target_pairs={{0,4},{4,8},{8,12},{12,0},{1,5},{5,9},{9,13},{13,1},{2,6},{6,10},{... | collective-permute-start | bytes 200 | tf_op jit(solution)/shard_map/while/body/eval_jaxpr/ppermute | solution.py:12
  126.7 3.2 %copy-start.1 = (f32[4,2048,16,16]{1,3,2,0:T(8,128)}, f32[4,2048,16,16]{1,3,2,0:T(8,128)S(1)}, u32[]{:S(2)}) copy-start(f32[4,2048,16,16]{1,3,2,0:T(8,128)S(1)} %get-tuple-element.197) | copy-start | bytes 25165828 | tf_op jit(solution)/shard_map/while
  138.7 19.4 %collective-permute-start.4 = (f32[16,64,128]{2,1,0:T(8,128)S(1)}, f32[16,64,128]{2,1,0:T(8,128)S(1)}, u32[]{:S(2)}, u32[]{:S(2)}) collective-permute-start(f32[16,64,128]{2,1,0:T(8,128)S(1)} %fusion.38), channel_id=1, source_target_pairs={{0,4},{4,8},{8,12},{12,0},{1,5},{5,9},{9,13},{13,1},{2,6},{6,10},{... | collective-permute-start | bytes 1572872 | tf_op jit(solution)/shard_map/while/body/eval_jaxpr/ppermute | solution.py:12
  138.7 19.3 %collective-permute-start = (bf16[16,64,128]{2,1,0:T(8,128)(2,1)S(1)}, bf16[16,64,128]{2,1,0:T(8,128)(2,1)}, u32[]{:S(2)}, u32[]{:S(2)}) collective-permute-start(bf16[16,64,128]{2,1,0:T(8,128)(2,1)S(1)} %copy.57), channel_id=1, source_target_pairs={{0,4},{4,8},{8,12},{12,0},{1,5},{5,9},{9,13},{13,1},{2,6},{6,10},{... | collective-permute-start | bytes 786440 | tf_op jit(solution)/shard_map/while/body/eval_jaxpr/ppermute | solution.py:12
  138.8 19.2 %collective-permute-start.2 = (f32[16,64]{1,0:T(8,128)S(1)}, f32[16,64]{1,0:T(8,128)S(1)}, u32[]{:S(2)}, u32[]{:S(2)}) collective-permute-start(f32[16,64]{1,0:T(8,128)S(1)} %get-tuple-element.199), channel_id=1, source_target_pairs={{0,4},{4,8},{8,12},{12,0},{1,5},{5,9},{9,13},{13,1},{2,6},{6,10},{... | collective-permute-start | bytes 12296 | tf_op jit(solution)/shard_map/while/body/eval_jaxpr/ppermute | solution.py:12
  139.4 18.7 %collective-permute-start.3 = (f32[16,64]{1,0:T(8,128)S(1)}, f32[16,64]{1,0:T(8,128)S(1)}, u32[]{:S(2)}, u32[]{:S(2)}) collective-permute-start(f32[16,64]{1,0:T(8,128)S(1)} %get-tuple-element.200), channel_id=1, source_target_pairs={{0,4},{4,8},{8,12},{12,0},{1,5},{5,9},{9,13},{13,1},{2,6},{6,10},{... | collective-permute-start | bytes 12296 | tf_op jit(solution)/shard_map/while/body/eval_jaxpr/ppermute | solution.py:12
  143.7 14.4 %collective-permute-start.1 = (s32[16]{0:T(128)S(1)}, s32[16]{0:T(128)S(1)}, u32[]{:S(2)}, u32[]{:S(2)}) collective-permute-start(s32[16]{0:T(128)S(1)} %copy.58), channel_id=1, source_target_pairs={{0,4},{4,8},{8,12},{12,0},{1,5},{5,9},{9,13},{13,1},{2,6},{6,10},{... | collective-permute-start | bytes 200 | tf_op jit(solution)/shard_map/while/body/eval_jaxpr/ppermute | solution.py:12
  159.2 63.4 %reduce-scatter.2.cloned.1.call-start = ((), (), s32[]{:S(2)}) async-start(), calls=%async_computation.2 | async-start | bytes 1572864 | tf_op jit(solution)/shard_map/reduce_scatter | solution.py:96
Sparse Core Ops, SparseCore 0:
  159.3 26.6 all-gather.1
  202.8 19.7 reduce-scatter.1
where the time goes:
time: 232 us; the launch traced here: 231 us
  waiting for transfers between devices  107 us (46%)
  matrix products  46.1 us (20%)
  local copies, waits for them, and re-layouts  25.4 us (11%)
  starting transfers between devices  23.3 us (10%)
  other arithmetic  14.7 us (6%)
  between operations  14.1 us (6%)
    ppermute x20, waiting for transfers between devices, shifted(): return lax.ppermute(value, axis, pairs)  60.5 us
    all_gather x1, waiting for transfers between devices, local(): lax.all_gather(attended, ('ctx', 'rep'), axis=0, tiled=True)  26.8 us
    ppermute x20, starting transfers between devices, shifted(): return lax.ppermute(value, axis, pairs)  23.2 us
    dot_general x4, matrix products, attend(): jnp.einsum('tkgj,jkd->tkgd', weights.astype(jnp.bfloat16), cache_values,...  21.8 us
    reduce_scatter x1, waiting for transfers between devices, local(): lax.psum_scatter(terms, 'heads', scatter_dimension=0, tiled=True)  19.9 us
    dot_general x1, matrix products, local(): jnp.dot(lax.all_gather(attended, ('ctx', 'rep'), axis=0, tiled=True), out...  16.7 us
    while x16, local copies, waits for them, and re-layouts  16.6 us
    reduce_sum x4, other arithmetic, attend(): totals = jnp.sum(weights, axis=-1)  10.9 us
  transfers between devices with their start and end apart: 22, of which 6 were waited for; matrix products, arithmetic and copies ran while one was open for 0% of the time, Pallas kernels for 0%

commit v1 on v0

v1 whole, which is shorter than its diff:
```python
import functools
import math

import jax
import jax.numpy as jnp
from jax import lax
from jax.experimental import pallas as pl
from jax.experimental.pallas import tpu as pltpu
from jax.sharding import PartitionSpec as P

NEG_FILL = -1e30
NEG_FLOOR = -1e29
LANES = 128
PACK = 16
VMEM = pltpu.MemorySpace.VMEM
SMEM = pltpu.MemorySpace.SMEM


def round_up(value, step):
    return (value + step - 1) // step * step


def stat_rows(rows):
    return round_up(3 * (rows // LANES), PACK)


def attend_kernel(
    tokens, kv_heads, per_group, with_own, base_ref, q_ref, k_ref, v_ref, *rest
):
    if with_own:
        nk_ref, nv_ref, out_ref, bound_ref = rest
    else:
        out_ref, bound_ref = rest
    head_rows = tokens * per_group
    rows = kv_heads * head_rows
    block_len, size = k_ref.shape[1:]
    factor = size ** (-0.5) * math.log2(math.e)
    high = q_ref[rows : rows + tokens, :].astype(jnp.float32)
    low = q_ref[rows + tokens : rows + 2 * tokens, :].astype(jnp.float32)
    bound = high * 128.0 + low - base_ref[0].astype(jnp.float32)
    bound_ref[...] = jnp.broadcast_to(bound[:, None, :], (tokens, per_group, LANES)).reshape(
        head_rows, LANES
    )
    lane = lax.broadcasted_iota(jnp.int32, (1, LANES), 1).astype(jnp.float32)
    lane_id = lax.broadcasted_iota(jnp.int32, (LANES, LANES), 1)
    stats = jnp.zeros((LANES, LANES), jnp.float32)
    limit = bound_ref[...]
    for head in range(kv_heads):
        q = q_ref[head * head_rows : (head + 1) * head_rows, :]
        scores = lax.dot_general(
            q, k_ref[head], (((1,), (1,)), ((), ())), preferred_element_type=jnp.float32
        )
        pieces = []
        for start in range(0, block_len, LANES):
            seen = (lane + float(start)) < limit
            pieces.append(jnp.where(seen, scores[:, start : start + LANES], NEG_FILL))
        best = functools.reduce(jnp.maximum, pieces)
        top = jnp.max(best, axis=-1, keepdims=True)
        if with_own:
            nk = jnp.broadcast_to(
                nk_ref[head].astype(jnp.float32)[:, None, :], (tokens, per_group, size)
            ).reshape(head_rows, size)
            own = jnp.sum(q.astype(jnp.float32) * nk, axis=-1, keepdims=True)
            top = jnp.maximum(top, own)
        top = jnp.maximum(top, NEG_FLOOR)
        weights = [jnp.exp2((piece - top) * factor) for piece in pieces]
        total = jnp.sum(functools.reduce(jnp.add, weights), axis=-1, keepdims=True)
        rounded = jnp.concatenate([w.astype(jnp.bfloat16) for w in weights], axis=1)
        value = lax.dot_general(
            rounded, v_ref[head], (((1,), (0,)), ((), ())), preferred_element_type=jnp.float32
        )
        if with_own:
            nv = jnp.broadcast_to(
                nv_ref[head].astype(jnp.float32)[:, None, :], (tokens, per_group, size)
            ).reshape(head_rows, size)
            mine = jnp.exp2((own - top) * factor)
            total = total + mine
            value = value + mine * nv
        some = total > 0.0
        safe = jnp.where(some, total, 1.0)
        out_ref[head * head_rows : (head + 1) * head_rows, :] = (value / safe).astype(jnp.bfloat16)
        level = jnp.where(some, top * factor + jnp.log2(safe), NEG_FILL)
        for part in range(head_rows // LANES):
            column = level[part * LANES : (part + 1) * LANES, :]
            index = head * (head_rows // LANES) + part
            stats = jnp.where(lane_id == index, column, stats)
    flat = jnp.transpose(stats)
    first = flat.astype(jnp.bfloat16)
    rest_one = flat - first.astype(jnp.float32)
    second = rest_one.astype(jnp.bfloat16)
    third = (rest_one - second.astype(jnp.float32)).astype(jnp.bfloat16)
    count = rows // LANES
    extra = stat_rows(rows)
    joined = jnp.concatenate(
        [
            first.astype(jnp.float32)[:count],
            second.astype(jnp.float32)[:count],
            third.astype(jnp.float32)[:count],
            jnp.zeros((extra - 3 * count, LANES), jnp.float32),
        ],
        axis=0,
    )
    out_ref[rows : rows + extra, :] = joined.astype(jnp.bfloat16)


def attend(base, packed, keys, values, own, tokens, per_group):
    kv_heads, block_len, size = keys.shape
    rows = tokens * kv_heads * per_group
    body = functools.partial(attend_kernel, tokens, kv_heads, per_group, own is not None)
    spec = pl.BlockSpec(memory_space=VMEM)
    operands = (base, packed, keys, values) + (own if own is not None else ())
    return pl.pallas_call(
        body,
        out_shape=jax.ShapeDtypeStruct((rows + stat_rows(rows), size), jnp.bfloat16),
        in_specs=[pl.BlockSpec(memory_space=SMEM)] + [spec] * (len(operands) - 1),
        out_specs=spec,
        scratch_shapes=[pltpu.VMEM((tokens * per_group, LANES), jnp.float32)],
        compiler_params=pltpu.CompilerParams(vmem_limit_bytes=24 * 1024 * 1024),
        cost_estimate=pl.CostEstimate(
            flops=4 * rows * block_len * size,
            bytes_accessed=4 * kv_heads * block_len * size,
            transcendentals=rows * block_len,
        ),
        name="attend",
    )(*operands)


def merge_kernel(tokens, kv_heads, per_group, count, *refs):
    parts, out_ref, hold_ref = refs[:count], refs[count], refs[count + 1]
    head_rows = tokens * per_group
    rows = kv_heads * head_rows
    lines = rows // LANES
    levels = []
    for part in parts:
        tail = part[rows:, :].astype(jnp.float32)
        levels.append(tail[:lines] + tail[lines : 2 * lines] + tail[2 * lines : 3 * lines])
    top = functools.reduce(jnp.maximum, levels)
    shares = [jnp.exp2(level - top) for level in levels]
    whole = functools.reduce(jnp.add, shares)
    shares = [share / whole for share in shares]
    stacked = jnp.concatenate(
        shares + [jnp.zeros((LANES - count * lines, LANES), jnp.float32)], axis=0
    )
    columns = jnp.transpose(stacked)
    for head in range(kv_heads):
        for piece in range(head_rows // LANES):
            line = head * (head_rows // LANES) + piece
            start = line * LANES
            value = None
            for index, part in enumerate(parts):
                share = columns[:, index * lines + line : index * lines + line + 1]
                term = share * part[start : start + LANES, :].astype(jnp.float32)
                value = term if value is None else value + term
            hold_ref[piece * LANES : (piece + 1) * LANES, :] = value
        for member in range(per_group):
            column = (head * per_group + member) * LANES
            out_ref[:, column : column + LANES] = hold_ref[
                pl.ds(member, tokens, stride=per_group), :
            ].astype(jnp.bfloat16)


def merge(parts, tokens, kv_heads, per_group):
    rows = tokens * kv_heads * per_group
    spec = pl.BlockSpec(memory_space=VMEM)
    return pl.pallas_call(
        functools.partial(merge_kernel, tokens, kv_heads, per_group, len(parts)),
        out_shape=jax.ShapeDtypeStruct((tokens, kv_heads * per_group * LANES), jnp.bfloat16),
        in_specs=[spec] * len(parts),
        out_specs=spec,
        scratch_shapes=[pltpu.VMEM((tokens * per_group, LANES), jnp.float32)],
        compiler_params=pltpu.CompilerParams(vmem_limit_bytes=8 * 1024 * 1024),
        cost_estimate=pl.CostEstimate(
            flops=4 * len(parts) * rows * LANES,
            bytes_accessed=2 * len(parts) * rows * LANES,
            transcendentals=0,
        ),
        name="merge",
    )(*parts)


def project_kernel(count, near, place_ref, *refs):
    blocks, w_ref, near_ref, far_ref, left_ref = (
        refs[:count],
        refs[count],
        refs[count + 1],
        refs[count + 2],
        refs[count + 3],
    )

    @pl.when(pl.program_id(0) == 0)
    def _():
        for index, block in enumerate(blocks):
            tokens = block.shape[0]
            start = pl.multiple_of(place_ref[index], tokens)
            left_ref[pl.ds(start, tokens), :] = block[...]

    result = jnp.dot(left_ref[...], w_ref[...], preferred_element_type=jnp.float32)
    near_ref[...] = result[:near]
    far_ref[...] = result[near:].astype(jnp.bfloat16)


def project(places, blocks, weight, near, tile):
    depth, width = weight.shape
    total = sum(block.shape[0] for block in blocks)
    whole = [pl.BlockSpec(block.shape, lambda j: (0, 0)) for block in blocks]
    return pl.pallas_call(
        functools.partial(project_kernel, len(blocks), near),
        out_shape=(
            jax.ShapeDtypeStruct((near, width), jnp.float32),
            jax.ShapeDtypeStruct((total - near, width), jnp.bfloat16),
        ),
        grid=(width // tile,),
        in_specs=[pl.BlockSpec(memory_space=SMEM)]
        + whole
        + [pl.BlockSpec((depth, tile), lambda j: (0, j))],
        out_specs=(
            pl.BlockSpec((near, tile), lambda j: (0, j)),
            pl.BlockSpec((total - near, tile), lambda j: (0, j)),
        ),
        scratch_shapes=[pltpu.VMEM((total, depth), jnp.bfloat16)],
        compiler_params=pltpu.CompilerParams(vmem_limit_bytes=28 * 1024 * 1024),
        cost_estimate=pl.CostEstimate(
            flops=2 * total * depth * width,
            bytes_accessed=2 * depth * width,
            transcendentals=0,
        ),
        name="project",
    )(places, *blocks, weight)


def split_index(index, pair):
    return index // pair, index % pair


def ctx_routes(count):
    pair = 2 if count % 2 == 0 else 1
    return pair, count // pair


def moved(value, count, step, flip):
    pair, spans = ctx_routes(count)
    pairs = []
    for source in range(count):
        span, side = split_index(source, pair)
        pairs.append((source, ((span + step) % spans) * pair + (side + flip) % pair))
    return lax.ppermute(value, "ctx", pairs)


def gather_blocks(value, count):
    pair, spans = ctx_routes(count)
    blocks = [((0, 0), value)]
    if pair > 1:
        blocks.append(((0, 1), moved(value, count, 0, 1)))
    for step in range(1, spans):
        crossed = moved(value, count, -step, 0)
        blocks.append(((step, 0), crossed))
    for key, crossed in list(blocks):
        if pair > 1 and key[0] > 0:
            blocks.append(((key[0], 1), moved(crossed, count, 0, 1)))
    return blocks


def local(
    queries, cache_keys, cache_values, new_keys, new_values, positions, cached_length, out_weight
):
    tokens, local_heads, size = queries.shape
    block_len, kv_heads = cache_keys.shape[0], cache_keys.shape[1]
    per_group = local_heads // kv_heads
    n_ctx = lax.axis_size("ctx")
    n_rep = lax.axis_size("rep")
    n_heads = lax.axis_size("heads")
    ctx = lax.axis_index("ctx")
    rep = lax.axis_index("rep")
    side = lax.axis_index("heads")
    pair, spans = ctx_routes(n_ctx)
    base = (ctx * block_len).astype(jnp.int32).reshape(1)

    limits = jnp.minimum(cached_length[0], positions)
    marks = jnp.concatenate([limits // 128, limits % 128]).astype(jnp.bfloat16)
    marks = jnp.broadcast_to(marks[:, None], (2 * tokens, size))
    ordered = queries.reshape(tokens, kv_heads, per_group, size).transpose(1, 0, 2, 3)
    packed = jnp.concatenate([ordered.reshape(tokens * local_heads, size), marks], axis=0)

    keys = cache_keys.transpose(1, 0, 2)
    values = cache_values.transpose(1, 0, 2)
    own = (new_keys.transpose(1, 0, 2), new_values.transpose(1, 0, 2))

    parts = []
    for (step, flip), block in gather_blocks(packed, n_ctx):
        home = step == 0 and flip == 0
        part = attend(base, block, keys, values, own if home else None, tokens, per_group)
        parts.append(part if home else moved(part, n_ctx, step, flip))
    attended = merge(parts, tokens, kv_heads, per_group)

    group_tokens = n_ctx * n_rep * tokens
    near = group_tokens // n_heads
    span, which = ctx // pair, ctx % pair
    blocks, places = [], []
    for (step, flip), block in gather_blocks(attended, n_ctx):
        source = ((span + step) % spans) * pair + (which + flip) % pair
        for turn in range(n_rep):
            passed = block
            if turn:
                passed = lax.ppermute(
                    block, "rep", [(i, (i - turn) % n_rep) for i in range(n_rep)]
                )
            row = (source * n_rep + (rep + turn) % n_rep) * tokens
            places.append((row - side * near) % group_tokens)
            blocks.append(passed)
    places = jnp.stack(places).astype(jnp.int32)
    width = out_weight.shape[1]
    mine, others = project(places, blocks, out_weight, near, min(256, width))
    result = mine
    for step in range(1, n_heads):
        sent = others[(step - 1) * near : step * near]
        result = result + lax.ppermute(
            sent, "heads", [(i, (i + step) % n_heads) for i in range(n_heads)]
        ).astype(jnp.float32)
    return result.astype(jnp.bfloat16)


def solution(mesh):
    return jax.shard_map(
        local,
        mesh=mesh,
        in_specs=(
            P(("groups", "ctx", "rep"), "heads", None),
            P(("groups", "ctx"), "heads", None),
            P(("groups", "ctx"), "heads", None),
            P(("groups", "ctx", "rep"), "heads", None),
            P(("groups", "ctx", "rep"), "heads", None),
            P(("groups", "ctx", "rep")),
            P("groups"),
            P("heads", ("ctx", "rep")),
        ),
        out_specs=P(("groups", "heads"), ("ctx", "rep")),
        check_vma=False,
    )
```

time: 232 us -> 103 us (0.44)
  waiting for transfers between devices: 107 us -> 48.1 us
  matrix products: 46.1 us -> 0 us
  Pallas kernels: 0 us -> 30.2 us
  local copies, waits for them, and re-layouts: 25.4 us -> 6.76 us
  between operations: 14.1 us -> 0.79 us
  other arithmetic: 14.7 us -> 1.73 us
  starting transfers between devices: 23.3 us -> 15.6 us
    dot_general x10 -> x0, matrix products: 46.1 us -> none  [the longest x4 21.8 us: attend(): jnp.einsum('tkgj,jkd->tkgd', weights.astype(jnp.bfloat16), cache_values,...]
    pallas_call x0 -> x6, Pallas kernels: none -> 30.2 us  [the longest x4 15.5 us: attend(): pl.pallas_call(body, out_shape=jax.ShapeDtypeStruct((rows + stat_rows(row...]
    all_gather x1 -> x0, waiting for transfers between devices: 26.8 us -> none  [local(): lax.all_gather(attended, ('ctx', 'rep'), axis=0, tiled=True)]
    reduce_scatter x1 -> x0, waiting for transfers between devices: 19.9 us -> none  [local(): lax.psum_scatter(terms, 'heads', scatter_dimension=0, tiled=True)]
    while x16 -> x0, local copies, waits for them, and re-layouts: 16.6 us -> none
    ppermute x20 -> x14, waiting for transfers between devices: 60.5 us -> 48.1 us  [the longest x9 39.8 us: moved(): return lax.ppermute(value, 'ctx', pairs)]
    reduce_sum x4 -> x0, other arithmetic: 10.9 us -> none  [attend(): totals = jnp.sum(weights, axis=-1)]
    ppermute x20 -> x14, starting transfers between devices: 23.2 us -> 15.6 us  [the longest x9 13.5 us: moved(): return lax.ppermute(value, 'ctx', pairs)]
  transfers between devices with their start and end apart: 22 -> 14, of which waited for: 6 -> 6; matrix products, arithmetic and copies ran while one was open for 0% -> 4% of each run, Pallas kernels for 0% -> 15%
where the time goes in v1:
time: 103 us
  waiting for transfers between devices  48.1 us (47%)
  Pallas kernels  30.2 us (29%)
  starting transfers between devices  15.6 us (15%)
  local copies, waits for them, and re-layouts  6.76 us (7%)
  other arithmetic  1.73 us (2%)
    ppermute x9, waiting for transfers between devices, moved(): return lax.ppermute(value, 'ctx', pairs)  39.8 us
    pallas_call x4, Pallas kernels, attend(): pl.pallas_call(body, out_shape=jax.ShapeDtypeStruct((rows + stat_rows(row...  15.5 us
    pallas_call x1, Pallas kernels, project(): pl.pallas_call(functools.partial(project_kernel, len(blocks), near), out_...  13.8 us
    ppermute x9, starting transfers between devices, moved(): return lax.ppermute(value, 'ctx', pairs)  13.5 us
    ppermute x1, waiting for transfers between devices, local(): lax.ppermute(sent, 'heads', [(i, (i + step) % n_heads) for i in range(n_h...  6.87 us
    transpose x1, local copies, waits for them, and re-layouts, local(): values = cache_values.transpose(1, 0, 2)  4.09 us
  transfers between devices with their start and end apart: 14, of which 6 were waited for; matrix products, arithmetic and copies ran while one was open for 4% of the time, Pallas kernels for 15%

profile of v1, /device:TPU:0, one launch (start us, length us, event | category | flops | bytes accessed | tf_op | source)
XLA Modules:
  0.0 103.2 jit_solution(16946376556972127642)
XLA Ops:
  0.7 0.7 fusion.1
  1.3 1.0 copy.9
  2.3 0.1 pad_maximum_fusion.1
  2.4 0.2 pad_maximum_fusion.q_ref
  2.6 4.1 %collective-permute-start.2 = (bf16[1056,128]{1,0:T(8,128)(2,1)S(1)}, bf16[1056,128]{1,0:T(8,128)(2,1)S(1)}, u32[]{:S(2)}, u32[]{:S(2)}) collective-permute-start(bf16[1056,128]{1,0:T(8,128)(2,1)S(1)} %pad_maximum_fusion.q_ref), channel_id=1, source_target_pairs={{0,8},{4,12},{8,0},{12,4},{1,9},{5,13},{9,1},{13,5},{2,10},{6,14},... | collective-permute-start | bytes 811016 | tf_op jit(solution)/shard_map/ppermute | solution.py:246
  6.7 1.6 %collective-permute-start = (bf16[1056,128]{1,0:T(8,128)(2,1)S(1)}, bf16[1056,128]{1,0:T(8,128)(2,1)S(1)}, u32[]{:S(2)}, u32[]{:S(2)}) collective-permute-start(bf16[1056,128]{1,0:T(8,128)(2,1)S(1)} %pad_maximum_fusion.q_ref), channel_id=1, source_target_pairs={{0,4},{4,0},{8,12},{12,8},{1,5},{5,1},{9,13},{13,9},{2,6},{6,2},{1... | collective-permute-start | bytes 811016 | tf_op jit(solution)/shard_map/ppermute | solution.py:246
  8.3 10.8 %collective-permute-done.2.q_ref = bf16[1056,128]{1,0:T(8,128)(2,1)S(1)} collective-permute-done((bf16[1056,128]{1,0:T(8,128)(2,1)S(1)}, bf16[1056,128]{1,0:T(8,128)(2,1)S(1)}, u32[]{:S(2)}, u32[]{:S(2)}) %collective-permute-start.2) | collective-permute-done | bytes 270368 | tf_op jit(solution)/shard_map/ppermute | solution.py:246
  19.1 0.6 collective-permute-start.4
  19.7 4.1 %copy_bitcast_fusion = (bf16[4,2048,128]{2,1,0:T(8,128)(2,1)S(1)}, bf16[4,2048,128]{2,1,0:T(8,128)(2,1)}) fusion(bf16[2048,4,128]{2,1,0:T(4,128)(2,1)} %param.10, bf16[2048,4,128]{2,1,0:T(4,128)(2,1)} %param.9), kind=kLoop, calls=%fused_computation | loop fusion | bytes 8388608 | tf_op jit(solution)/shard_map/transpose | solution.py:285
  23.8 0.0 copy-start
  23.8 1.6 %copy-done = bf16[4,2048,128]{2,1,0:T(8,128)(2,1)S(1)} copy-done((bf16[4,2048,128]{2,1,0:T(8,128)(2,1)S(1)}, bf16[4,2048,128]{2,1,0:T(8,128)(2,1)}, u32[]{:S(2)}) %copy-start) | copy-done | bytes 2097176
  25.4 3.8 %attend.6 = bf16[1056,128]{1,0:T(8,128)(2,1)S(1)} custom-call(s32[1]{0:T(128)} %bitcast.8.base_ref, bf16[1056,128]{1,0:T(8,128)(2,1)S(1)} %collective-permute-done.2.q_ref, bf16[4,2048,128]{2,1,0:T(8,128)(2,1)S(1)} %copy-done, bf16[4,2048,128]{2,1,0:T(8,128)(2,1)S(1)} %get-tuple-element.11.v_ref), custom_call_target="tpu_custom_call" | custom-call | flops 1073741824 | bytes 4194304 | tf_op jit(solution)/shard_map/attend/pallas_call | solution.py:112
  29.2 3.4 %collective-permute-start.3 = (bf16[1056,128]{1,0:T(8,128)(2,1)S(1)}, bf16[1056,128]{1,0:T(8,128)(2,1)S(1)}, u32[]{:S(2)}, u32[]{:S(2)}) collective-permute-start(bf16[1056,128]{1,0:T(8,128)(2,1)S(1)} %attend.6), channel_id=1, source_target_pairs={{0,8},{4,12},{8,0},{12,4},{1,9},{5,13},{9,1},{13,5},{2,10},{6,14},... | collective-permute-start | bytes 811016 | tf_op jit(solution)/shard_map/ppermute | solution.py:246
  32.6 0.0 collective-permute-done.q_ref
  32.6 3.8 %attend.5 = bf16[1056,128]{1,0:T(8,128)(2,1)S(1)} custom-call(s32[1]{0:T(128)} %bitcast.8.base_ref, bf16[1056,128]{1,0:T(8,128)(2,1)S(1)} %collective-permute-done.q_ref, bf16[4,2048,128]{2,1,0:T(8,128)(2,1)S(1)} %copy-done, bf16[4,2048,128]{2,1,0:T(8,128)(2,1)S(1)} %get-tuple-element.11.v_ref), custom_call_target="tpu_custom_call" | custom-call | flops 1073741824 | bytes 4194304 | tf_op jit(solution)/shard_map/attend/pallas_call | solution.py:112
  36.4 0.0 copy-start.2
  36.5 0.0 copy-start.3
  36.5 0.0 copy-start.1
  36.5 0.1 collective-permute-start.1
  36.6 0.0 collective-permute-done.4.q_ref
  36.6 4.0 %attend.7 = bf16[1056,128]{1,0:T(8,128)(2,1)S(1)} custom-call(s32[1]{0:T(128)} %bitcast.8.base_ref, bf16[1056,128]{1,0:T(8,128)(2,1)S(1)} %collective-permute-done.4.q_ref, bf16[4,2048,128]{2,1,0:T(8,128)(2,1)S(1)} %copy-done, bf16[4,2048,128]{2,1,0:T(8,128)(2,1)S(1)} %get-tuple-element.11.v_ref), custom_call_target="tpu_custom_call" | custom-call | flops 1073741824 | bytes 4194304 | tf_op jit(solution)/shard_map/attend/pallas_call | solution.py:112
  40.5 1.5 %collective-permute-start.5 = (bf16[1056,128]{1,0:T(8,128)(2,1)S(1)}, bf16[1056,128]{1,0:T(8,128)(2,1)S(1)}, u32[]{:S(2)}, u32[]{:S(2)}) collective-permute-start(bf16[1056,128]{1,0:T(8,128)(2,1)S(1)} %attend.7), channel_id=1, source_target_pairs={{0,12},{4,8},{8,4},{12,0},{1,13},{5,9},{9,5},{13,1},{2,14},{6,10},... | collective-permute-start | bytes 811016 | tf_op jit(solution)/shard_map/ppermute | solution.py:246
  42.1 0.0 copy-done.2
  42.1 0.0 copy-done.3
  42.1 0.0 copy-done.1
  42.1 4.0 %attend.4.refs_0_ = bf16[1056,128]{1,0:T(8,128)(2,1)S(1)} custom-call(s32[1]{0:T(128)} %bitcast.8.base_ref, bf16[1056,128]{1,0:T(8,128)(2,1)S(1)} %pad_maximum_fusion.q_ref, bf16[4,2048,128]{2,1,0:T(8,128)(2,1)S(1)} %copy-done.1, bf16[4,2048,128]{2,1,0:T(8,128)(2,1)S(1)} %get-tuple-element.11.v_ref, bf16[4,16,128]{2,1,0:T(8,128)(2,1)S(1)} %get-tuple-element.14.rest_0_, ...), custom_call_target="tpu_custom_call" | custom-call | flops 1073741824 | bytes 4194304 | tf_op jit(solution)/shard_map/attend/pallas_call | solution.py:112
  46.1 0.0 collective-permute-done.3.refs_2_
  46.1 9.7 %collective-permute-done.1.refs_1_ = bf16[1056,128]{1,0:T(8,128)(2,1)S(1)} collective-permute-done((bf16[1056,128]{1,0:T(8,128)(2,1)S(1)}, bf16[1056,128]{1,0:T(8,128)(2,1)S(1)}, u32[]{:S(2)}, u32[]{:S(2)}) %collective-permute-start.1) | collective-permute-done | bytes 270368 | tf_op jit(solution)/shard_map/ppermute | solution.py:246
  55.8 0.0 collective-permute-done.5.refs_3_
  55.8 0.9 merge.1.refs_0_
  56.7 2.2 %collective-permute-start.9 = (bf16[16,8192]{1,0:T(8,128)(2,1)S(1)}, bf16[16,8192]{1,0:T(8,128)(2,1)S(1)}, u32[]{:S(2)}, u32[]{:S(2)}) collective-permute-start(bf16[16,8192]{1,0:T(8,128)(2,1)S(1)} %merge.1.refs_0_), channel_id=1, source_target_pairs={{0,8},{4,12},{8,0},{12,4},{1,9},{5,13},{9,1},{13,5},{2,10},{6,14},... | collective-permute-start | bytes 786440 | tf_op jit(solution)/shard_map/ppermute | solution.py:246
  58.8 0.0 collective-permute-start.7
  58.8 12.3 %collective-permute-done.9.refs_4_ = bf16[16,8192]{1,0:T(8,128)(2,1)S(1)} collective-permute-done((bf16[16,8192]{1,0:T(8,128)(2,1)S(1)}, bf16[16,8192]{1,0:T(8,128)(2,1)S(1)}, u32[]{:S(2)}, u32[]{:S(2)}) %collective-permute-start.9) | collective-permute-done | bytes 262176 | tf_op jit(solution)/shard_map/ppermute | solution.py:246
  71.1 0.0 collective-permute-start.11
  71.2 0.0 collective-permute-start.6
  71.2 0.5 collective-permute-start.10
  71.7 0.0 collective-permute-done.7.refs_2_
  71.7 0.0 collective-permute-start.8
  71.7 7.0 %collective-permute-done.11.refs_6_ = bf16[16,8192]{1,0:T(8,128)(2,1)S(1)} collective-permute-done((bf16[16,8192]{1,0:T(8,128)(2,1)S(1)}, bf16[16,8192]{1,0:T(8,128)(2,1)S(1)}, u32[]{:S(2)}, u32[]{:S(2)}) %collective-permute-start.11) | collective-permute-done | bytes 262176 | tf_op jit(solution)/shard_map/ppermute | solution.py:246
  78.7 0.0 collective-permute-start.12
  78.7 0.1 stack.35.place_ref
  78.8 0.0 collective-permute-done.6.refs_1_
  78.8 0.0 collective-permute-done.10.refs_5_
  78.8 0.0 collective-permute-done.8.refs_3_
  78.8 1.4 %collective-permute-done.12.refs_7_ = bf16[16,8192]{1,0:T(8,128)(2,1)S(1)} collective-permute-done((bf16[16,8192]{1,0:T(8,128)(2,1)S(1)}, bf16[16,8192]{1,0:T(8,128)(2,1)S(1)}, u32[]{:S(2)}, u32[]{:S(2)}) %collective-permute-start.12) | collective-permute-done | bytes 262176 | tf_op jit(solution)/shard_map/ppermute | solution.py:304
  80.2 13.8 %project.1 = (f32[64,2048]{1,0:T(8,128)S(1)}, bf16[64,2048]{1,0:T(8,128)(2,1)S(1)}) custom-call(s32[8]{0:T(128)S(1)} %stack.35.place_ref, bf16[16,8192]{1,0:T(8,128)(2,1)S(1)} %merge.1.refs_0_, bf16[16,8192]{1,0:T(8,128)(2,1)S(1)} %collective-permute-done.6.refs_1_, bf16[16,8192]{1,0:T(8,128)(2,1)S(1)} %collective-permute-done.7.refs_2_, ...), custom_call_target="tpu_custom_call" | custom-call | flops 4294967296 | bytes 33554432 | tf_op jit(solution)/shard_map/project/pallas_call | solution.py:206
  94.0 1.5 %collective-permute-start.13 = (bf16[64,2048]{1,0:T(8,128)(2,1)S(1)}, bf16[64,2048]{1,0:T(8,128)(2,1)S(1)}, u32[]{:S(2)}, u32[]{:S(2)}) collective-permute-start(bf16[64,2048]{1,0:T(8,128)(2,1)S(1)} %get-tuple-element.8), channel_id=1, source_target_pairs={{0,2},{2,0},{1,3},{3,1},{4,6},{6,4},{5,7},{7,5},{8,10},{10,8},{9,1... | collective-permute-start | bytes 786440 | tf_op jit(solution)/shard_map/ppermute | solution.py:316
  95.6 6.9 %collective-permute-done.13 = bf16[64,2048]{1,0:T(8,128)(2,1)S(1)} collective-permute-done((bf16[64,2048]{1,0:T(8,128)(2,1)S(1)}, bf16[64,2048]{1,0:T(8,128)(2,1)S(1)}, u32[]{:S(2)}, u32[]{:S(2)}) %collective-permute-start.13) | collective-permute-done | bytes 262176 | tf_op jit(solution)/shard_map/ppermute | solution.py:316
  102.4 0.8 add_convert_fusion
  (2 shorter events, 0.0 us)
Async XLA Ops:
  2.6 16.5 %collective-permute-start.2 = (bf16[1056,128]{1,0:T(8,128)(2,1)S(1)}, bf16[1056,128]{1,0:T(8,128)(2,1)S(1)}, u32[]{:S(2)}, u32[]{:S(2)}) collective-permute-start(bf16[1056,128]{1,0:T(8,128)(2,1)S(1)} %pad_maximum_fusion.q_ref), channel_id=1, source_target_pairs={{0,8},{4,12},{8,0},{12,4},{1,9},{5,13},{9,1},{13,5},{2,10},{6,14},... | collective-permute-start | bytes 811016 | tf_op jit(solution)/shard_map/ppermute | solution.py:246
  6.7 25.9 %collective-permute-start = (bf16[1056,128]{1,0:T(8,128)(2,1)S(1)}, bf16[1056,128]{1,0:T(8,128)(2,1)S(1)}, u32[]{:S(2)}, u32[]{:S(2)}) collective-permute-start(bf16[1056,128]{1,0:T(8,128)(2,1)S(1)} %pad_maximum_fusion.q_ref), channel_id=1, source_target_pairs={{0,4},{4,0},{8,12},{12,8},{1,5},{5,1},{9,13},{13,9},{2,6},{6,2},{1... | collective-permute-start | bytes 811016 | tf_op jit(solution)/shard_map/ppermute | solution.py:246
  19.1 17.5 %collective-permute-start.4 = (bf16[1056,128]{1,0:T(8,128)(2,1)S(1)}, bf16[1056,128]{1,0:T(8,128)(2,1)S(1)}, u32[]{:S(2)}, u32[]{:S(2)}) collective-permute-start(bf16[1056,128]{1,0:T(8,128)(2,1)S(1)} %collective-permute-done.2.q_ref), channel_id=1, source_target_pairs={{0,4},{4,0},{8,12},{12,8},{1,5},{5,1},{9,13},{13,9},{2,6},{6,2},{1... | collective-permute-start | bytes 811016 | tf_op jit(solution)/shard_map/ppermute | solution.py:246
  23.8 1.6 %copy-start = (bf16[4,2048,128]{2,1,0:T(8,128)(2,1)S(1)}, bf16[4,2048,128]{2,1,0:T(8,128)(2,1)}, u32[]{:S(2)}) copy-start(bf16[4,2048,128]{2,1,0:T(8,128)(2,1)} %get-tuple-element.12.k_ref) | copy-start | bytes 6291460
  29.2 16.9 %collective-permute-start.3 = (bf16[1056,128]{1,0:T(8,128)(2,1)S(1)}, bf16[1056,128]{1,0:T(8,128)(2,1)S(1)}, u32[]{:S(2)}, u32[]{:S(2)}) collective-permute-start(bf16[1056,128]{1,0:T(8,128)(2,1)S(1)} %attend.6), channel_id=1, source_target_pairs={{0,8},{4,12},{8,0},{12,4},{1,9},{5,13},{9,1},{13,5},{2,10},{6,14},... | collective-permute-start | bytes 811016 | tf_op jit(solution)/shard_map/ppermute | solution.py:246
  36.4 5.6 %copy-start.2 = (bf16[16,4,128]{2,1,0:T(4,128)(2,1)S(1)}, bf16[16,4,128]{2,1,0:T(4,128)(2,1)}, u32[]{:S(2)}) copy-start(bf16[16,4,128]{2,1,0:T(4,128)(2,1)} %param.12) | copy-start | bytes 49156
  36.5 5.6 %copy-start.3 = (bf16[16,4,128]{2,1,0:T(4,128)(2,1)S(1)}, bf16[16,4,128]{2,1,0:T(4,128)(2,1)}, u32[]{:S(2)}) copy-start(bf16[16,4,128]{2,1,0:T(4,128)(2,1)} %param.11) | copy-start | bytes 49156
  36.5 5.6 %copy-start.1 = (bf16[4,2048,128]{2,1,0:T(8,128)(2,1)S(1)}, bf16[4,2048,128]{2,1,0:T(8,128)(2,1)}, u32[]{:S(2)}) copy-start(bf16[4,2048,128]{2,1,0:T(8,128)(2,1)} %get-tuple-element.12.k_ref) | copy-start | bytes 6291460
  36.5 19.3 %collective-permute-start.1 = (bf16[1056,128]{1,0:T(8,128)(2,1)S(1)}, bf16[1056,128]{1,0:T(8,128)(2,1)S(1)}, u32[]{:S(2)}, u32[]{:S(2)}) collective-permute-start(bf16[1056,128]{1,0:T(8,128)(2,1)S(1)} %attend.5), channel_id=1, source_target_pairs={{0,4},{4,0},{8,12},{12,8},{1,5},{5,1},{9,13},{13,9},{2,6},{6,2},{1... | collective-permute-start | bytes 811016 | tf_op jit(solution)/shard_map/ppermute | solution.py:246
  40.5 15.3 %collective-permute-start.5 = (bf16[1056,128]{1,0:T(8,128)(2,1)S(1)}, bf16[1056,128]{1,0:T(8,128)(2,1)S(1)}, u32[]{:S(2)}, u32[]{:S(2)}) collective-permute-start(bf16[1056,128]{1,0:T(8,128)(2,1)S(1)} %attend.7), channel_id=1, source_target_pairs={{0,12},{4,8},{8,4},{12,0},{1,13},{5,9},{9,5},{13,1},{2,14},{6,10},... | collective-permute-start | bytes 811016 | tf_op jit(solution)/shard_map/ppermute | solution.py:246
  56.7 14.5 %collective-permute-start.9 = (bf16[16,8192]{1,0:T(8,128)(2,1)S(1)}, bf16[16,8192]{1,0:T(8,128)(2,1)S(1)}, u32[]{:S(2)}, u32[]{:S(2)}) collective-permute-start(bf16[16,8192]{1,0:T(8,128)(2,1)S(1)} %merge.1.refs_0_), channel_id=1, source_target_pairs={{0,8},{4,12},{8,0},{12,4},{1,9},{5,13},{9,1},{13,5},{2,10},{6,14},... | collective-permute-start | bytes 786440 | tf_op jit(solution)/shard_map/ppermute | solution.py:246
  58.8 12.8 %collective-permute-start.7 = (bf16[16,8192]{1,0:T(8,128)(2,1)S(1)}, bf16[16,8192]{1,0:T(8,128)(2,1)S(1)}, u32[]{:S(2)}, u32[]{:S(2)}) collective-permute-start(bf16[16,8192]{1,0:T(8,128)(2,1)S(1)} %merge.1.refs_0_), channel_id=1, source_target_pairs={{0,4},{4,0},{8,12},{12,8},{1,5},{5,1},{9,13},{13,9},{2,6},{6,2},{1... | collective-permute-start | bytes 786440 | tf_op jit(solution)/shard_map/ppermute | solution.py:246
  71.1 7.5 %collective-permute-start.11 = (bf16[16,8192]{1,0:T(8,128)(2,1)S(1)}, bf16[16,8192]{1,0:T(8,128)(2,1)S(1)}, u32[]{:S(2)}, u32[]{:S(2)}) collective-permute-start(bf16[16,8192]{1,0:T(8,128)(2,1)S(1)} %collective-permute-done.9.refs_4_), channel_id=1, source_target_pairs={{0,4},{4,0},{8,12},{12,8},{1,5},{5,1},{9,13},{13,9},{2,6},{6,2},{1... | collective-permute-start | bytes 786440 | tf_op jit(solution)/shard_map/ppermute | solution.py:246
  71.2 7.6 %collective-permute-start.6 = (bf16[16,8192]{1,0:T(8,128)(2,1)S(1)}, bf16[16,8192]{1,0:T(8,128)(2,1)S(1)}, u32[]{:S(2)}, u32[]{:S(2)}) collective-permute-start(bf16[16,8192]{1,0:T(8,128)(2,1)S(1)} %merge.1.refs_0_), channel_id=1, source_target_pairs={{0,1},{1,0},{2,3},{3,2},{4,5},{5,4},{6,7},{7,6},{8,9},{9,8},{10,11... | collective-permute-start | bytes 786440 | tf_op jit(solution)/shard_map/ppermute | solution.py:304
  71.2 7.6 %collective-permute-start.10 = (bf16[16,8192]{1,0:T(8,128)(2,1)S(1)}, bf16[16,8192]{1,0:T(8,128)(2,1)S(1)}, u32[]{:S(2)}, u32[]{:S(2)}) collective-permute-start(bf16[16,8192]{1,0:T(8,128)(2,1)S(1)} %collective-permute-done.9.refs_4_), channel_id=1, source_target_pairs={{0,1},{1,0},{2,3},{3,2},{4,5},{5,4},{6,7},{7,6},{8,9},{9,8},{10,11... | collective-permute-start | bytes 786440 | tf_op jit(solution)/shard_map/ppermute | solution.py:304
  71.7 7.1 %collective-permute-start.8 = (bf16[16,8192]{1,0:T(8,128)(2,1)S(1)}, bf16[16,8192]{1,0:T(8,128)(2,1)S(1)}, u32[]{:S(2)}, u32[]{:S(2)}) collective-permute-start(bf16[16,8192]{1,0:T(8,128)(2,1)S(1)} %collective-permute-done.7.refs_2_), channel_id=1, source_target_pairs={{0,1},{1,0},{2,3},{3,2},{4,5},{5,4},{6,7},{7,6},{8,9},{9,8},{10,11... | collective-permute-start | bytes 786440 | tf_op jit(solution)/shard_map/ppermute | solution.py:304
  78.7 1.5 %collective-permute-start.12 = (bf16[16,8192]{1,0:T(8,128)(2,1)S(1)}, bf16[16,8192]{1,0:T(8,128)(2,1)S(1)}, u32[]{:S(2)}, u32[]{:S(2)}) collective-permute-start(bf16[16,8192]{1,0:T(8,128)(2,1)S(1)} %collective-permute-done.11.refs_6_), channel_id=1, source_target_pairs={{0,1},{1,0},{2,3},{3,2},{4,5},{5,4},{6,7},{7,6},{8,9},{9,8},{10,11... | collective-permute-start | bytes 786440 | tf_op jit(solution)/shard_map/ppermute | solution.py:304
  94.0 8.4 %collective-permute-start.13 = (bf16[64,2048]{1,0:T(8,128)(2,1)S(1)}, bf16[64,2048]{1,0:T(8,128)(2,1)S(1)}, u32[]{:S(2)}, u32[]{:S(2)}) collective-permute-start(bf16[64,2048]{1,0:T(8,128)(2,1)S(1)} %get-tuple-element.8), channel_id=1, source_target_pairs={{0,2},{2,0},{1,3},{3,1},{4,6},{6,4},{5,7},{7,5},{8,10},{10,8},{9,1... | collective-permute-start | bytes 786440 | tf_op jit(solution)/shard_map/ppermute | solution.py:316

commit v2 on v1

--- a/solution.py
+++ b/solution.py
@@ -13,7 +13,6 @@
 LANES = 128
 PACK = 16
 VMEM = pltpu.MemorySpace.VMEM
-SMEM = pltpu.MemorySpace.SMEM
 
 
 def round_up(value, step):
@@ -25,19 +24,30 @@
 
 
 def attend_kernel(
-    tokens, kv_heads, per_group, with_own, base_ref, q_ref, k_ref, v_ref, *rest
+    tokens, heads, per_group, with_own, load_rows, q_ref, k_ref, v_ref, *rest
 ):
+    rest = list(rest)
     if with_own:
-        nk_ref, nv_ref, out_ref, bound_ref = rest
-    else:
-        out_ref, bound_ref = rest
+        nk_ref, nv_ref = rest.pop(0), rest.pop(0)
+    if load_rows is not None:
+        w_ref = rest.pop(0)
+    out_ref = rest.pop(0)
+    copy = None
+    if load_rows is not None:
+        copy = pltpu.make_async_copy(
+            w_ref.at[load_rows[0] : load_rows[1], :], rest.pop(0), rest.pop()
+        )
+        copy.start()
+    bound_ref = rest.pop(0)
     head_rows = tokens * per_group
-    rows = kv_heads * head_rows
-    block_len, size = k_ref.shape[1:]
+    kv_heads, block_len, size = k_ref.shape
+    rows = len(heads) * head_rows
+    local_heads = kv_heads * per_group
     factor = size ** (-0.5) * math.log2(math.e)
-    high = q_ref[rows : rows + tokens, :].astype(jnp.float32)
-    low = q_ref[rows + tokens : rows + 2 * tokens, :].astype(jnp.float32)
-    bound = high * 128.0 + low - base_ref[0].astype(jnp.float32)
+    high = q_ref[tokens * local_heads : tokens * local_heads + tokens, :].astype(jnp.float32)
+    low = q_ref[tokens * local_heads + tokens :, :].astype(jnp.float32)
+    base = lax.axis_index("ctx").astype(jnp.int32) * block_len
+    bound = high * 128.0 + low - base.astype(jnp.float32)
     bound_ref[...] = jnp.broadcast_to(bound[:, None, :], (tokens, per_group, LANES)).reshape(
         head_rows, LANES
     )
@@ -45,8 +55,14 @@
     lane_id = lax.broadcasted_iota(jnp.int32, (LANES, LANES), 1)
     stats = jnp.zeros((LANES, LANES), jnp.float32)
     limit = bound_ref[...]
-    for head in range(kv_heads):
-        q = q_ref[head * head_rows : (head + 1) * head_rows, :]
+    for order, head in enumerate(heads):
+        q = jnp.concatenate(
+            [
+                q_ref[t * local_heads + head * per_group : t * local_heads + (head + 1) * per_group, :]
+                for t in range(tokens)
+            ],
+            axis=0,
+        )
         scores = lax.dot_general(
             q, k_ref[head], (((1,), (1,)), ((), ())), preferred_element_type=jnp.float32
         )
@@ -78,11 +94,11 @@
             value = value + mine * nv
         some = total > 0.0
         safe = jnp.where(some, total, 1.0)
-        out_ref[head * head_rows : (head + 1) * head_rows, :] = (value / safe).astype(jnp.bfloat16)
+        out_ref[order * head_rows : (order + 1) * head_rows, :] = (value / safe).astype(jnp.bfloat16)
         level = jnp.where(some, top * factor + jnp.log2(safe), NEG_FILL)
         for part in range(head_rows // LANES):
             column = level[part * LANES : (part + 1) * LANES, :]
-            index = head * (head_rows // LANES) + part
+            index = order * (head_rows // LANES) + part
             stats = jnp.where(lane_id == index, column, stats)
     flat = jnp.transpose(stats)
     first = flat.astype(jnp.bfloat16)
@@ -101,24 +117,38 @@
         axis=0,
     )
     out_ref[rows : rows + extra, :] = joined.astype(jnp.bfloat16)
-
-
-def attend(base, packed, keys, values, own, tokens, per_group):
+    if copy is not None:
+        copy.wait()
+
+
+def attend(packed, keys, values, own, weight, load_rows, tokens, per_group, heads):
     kv_heads, block_len, size = keys.shape
-    rows = tokens * kv_heads * per_group
-    body = functools.partial(attend_kernel, tokens, kv_heads, per_group, own is not None)
+    rows = tokens * len(heads) * per_group
+    body = functools.partial(
+        attend_kernel, tokens, heads, per_group, own is not None, load_rows
+    )
     spec = pl.BlockSpec(memory_space=VMEM)
-    operands = (base, packed, keys, values) + (own if own is not None else ())
+    operands = (packed, keys, values) + (own if own is not None else ())
+    in_specs = [spec] * len(operands)
+    shapes = [jax.ShapeDtypeStruct((rows + stat_rows(rows), size), jnp.bfloat16)]
+    scratch = [pltpu.VMEM((tokens * per_group, LANES), jnp.float32)]
+    if load_rows is not None:
+        operands += (pltpu.with_memory_space_constraint(weight, pltpu.MemorySpace.HBM),)
+        in_specs.append(pl.BlockSpec(memory_space=pltpu.MemorySpace.HBM))
+        shapes.append(
+            jax.ShapeDtypeStruct((load_rows[1] - load_rows[0], weight.shape[1]), weight.dtype)
+        )
+        scratch.append(pltpu.SemaphoreType.DMA)
     return pl.pallas_call(
         body,
-        out_shape=jax.ShapeDtypeStruct((rows + stat_rows(rows), size), jnp.bfloat16),
-        in_specs=[pl.BlockSpec(memory_space=SMEM)] + [spec] * (len(operands) - 1),
-        out_specs=spec,
-        scratch_shapes=[pltpu.VMEM((tokens * per_group, LANES), jnp.float32)],
-        compiler_params=pltpu.CompilerParams(vmem_limit_bytes=24 * 1024 * 1024),
+        out_shape=shapes,
+        in_specs=in_specs,
+        out_specs=[spec] * len(shapes),
+        scratch_shapes=scratch,
+        compiler_params=pltpu.CompilerParams(vmem_limit_bytes=12 * 1024 * 1024),
         cost_estimate=pl.CostEstimate(
             flops=4 * rows * block_len * size,
-            bytes_accessed=4 * kv_heads * block_len * size,
+            bytes_accessed=4 * len(heads) * block_len * size,
             transcendentals=rows * block_len,
         ),
         name="attend",
@@ -178,54 +208,82 @@
     )(*parts)
 
 
-def project_kernel(count, near, place_ref, *refs):
-    blocks, w_ref, near_ref, far_ref, left_ref = (
-        refs[:count],
-        refs[count],
-        refs[count + 1],
-        refs[count + 2],
-        refs[count + 3],
-    )
-
-    @pl.when(pl.program_id(0) == 0)
-    def _():
-        for index, block in enumerate(blocks):
-            tokens = block.shape[0]
-            start = pl.multiple_of(place_ref[index], tokens)
-            left_ref[pl.ds(start, tokens), :] = block[...]
-
-    result = jnp.dot(left_ref[...], w_ref[...], preferred_element_type=jnp.float32)
-    near_ref[...] = result[:near]
-    far_ref[...] = result[near:].astype(jnp.bfloat16)
-
-
-def project(places, blocks, weight, near, tile):
-    depth, width = weight.shape
+def project_kernel(origins, strips, near, columns_from, with_sum, last, *refs):
+    count = len(origins)
+    blocks, w_refs = refs[:count], refs[count : count + strips]
+    rest = refs[count + strips :]
+    sum_ref = None
+    if with_sum:
+        sum_ref, rest = rest[0], rest[1:]
+    left_ref = rest[-1]
+    n_ctx, n_rep = lax.axis_size("ctx"), lax.axis_size("rep")
+    pair, spans = ctx_routes(n_ctx)
+    ctx, rep, side = (lax.axis_index(name).astype(jnp.int32) for name in ("ctx", "rep", "heads"))
+    group_tokens = left_ref.shape[0]
+    for (step, flip, turn), block in zip(origins, blocks):
+        tokens = block.shape[0]
+        source = lax.rem(lax.div(ctx, pair) + step, spans) * pair + lax.rem(ctx + flip, pair)
+        row = (source * n_rep + lax.rem(rep + turn, n_rep)) * tokens
+        row = lax.rem(row - side * near + group_tokens, group_tokens)
+        start = pl.multiple_of(row, tokens)
+        left_ref[pl.ds(start, tokens), :] = block[...]
+    depth = left_ref.shape[1]
+    width = rest[0].shape[1]
+    tile = min(256, width)
+    strip = depth // strips
+    for start in range(0, width, tile):
+        result = None
+        for index, w_ref in enumerate(w_refs):
+            term = jnp.dot(
+                left_ref[:, index * strip : (index + 1) * strip],
+                w_ref[:, columns_from + start : columns_from + start + tile],
+                preferred_element_type=jnp.float32,
+            )
+            result = term if result is None else result + term
+        if with_sum:
+            result = result + sum_ref[:, columns_from + start : columns_from + start + tile]
+        if last:
+            rest[0][:, start : start + tile] = result[:near]
+            rest[1][:, start : start + tile] = result[near:].astype(jnp.bfloat16)
+        else:
+            rest[0][:, start : start + tile] = result
+
+
+def project(origins, blocks, weights, partial_sum, near, columns, last):
+    depth = blocks[0].shape[1]
+    width = columns[1] - columns[0]
     total = sum(block.shape[0] for block in blocks)
-    whole = [pl.BlockSpec(block.shape, lambda j: (0, 0)) for block in blocks]
-    return pl.pallas_call(
-        functools.partial(project_kernel, len(blocks), near),
-        out_shape=(
+    spec = pl.BlockSpec(memory_space=VMEM)
+    if last:
+        shapes = (
             jax.ShapeDtypeStruct((near, width), jnp.float32),
             jax.ShapeDtypeStruct((total - near, width), jnp.bfloat16),
+        )
+    else:
+        shapes = (jax.ShapeDtypeStruct((total, width), jnp.float32),)
+    operands = tuple(blocks) + tuple(weights) + (() if partial_sum is None else (partial_sum,))
+    return pl.pallas_call(
+        functools.partial(
+            project_kernel,
+            origins,
+            len(weights),
+            near,
+            columns[0],
+            partial_sum is not None,
+            last,
         ),
-        grid=(width // tile,),
-        in_specs=[pl.BlockSpec(memory_space=SMEM)]
-        + whole
-        + [pl.BlockSpec((depth, tile), lambda j: (0, j))],
-        out_specs=(
-            pl.BlockSpec((near, tile), lambda j: (0, j)),
-            pl.BlockSpec((total - near, tile), lambda j: (0, j)),
-        ),
+        out_shape=shapes,
+        in_specs=[spec] * len(operands),
+        out_specs=tuple(spec for _ in shapes),
         scratch_shapes=[pltpu.VMEM((total, depth), jnp.bfloat16)],
-        compiler_params=pltpu.CompilerParams(vmem_limit_bytes=28 * 1024 * 1024),
+        compiler_params=pltpu.CompilerParams(vmem_limit_bytes=8 * 1024 * 1024),
         cost_estimate=pl.CostEstimate(
             flops=2 * total * depth * width,
             bytes_accessed=2 * depth * width,
             transcendentals=0,
         ),
         name="project",
-    )(places, *blocks, weight)
+    )(*operands)
 
 
 def split_index(index, pair):
@@ -246,17 +304,27 @@
     return lax.ppermute(value, "ctx", pairs)
 
 
+def after(value, *others):
+    return lax.optimization_barrier((value,) + others)[0]
+
+
+def gather_keys(count):
+    pair, spans = ctx_routes(count)
+    crossed = [(step, 0) for step in range(1, spans)]
+    near = [(0, 1)] if pair > 1 else []
+    far = [(step, 1) for step in range(1, spans)] if pair > 1 else []
+    return crossed, near, far
+
+
 def gather_blocks(value, count):
-    pair, spans = ctx_routes(count)
-    blocks = [((0, 0), value)]
-    if pair > 1:
-        blocks.append(((0, 1), moved(value, count, 0, 1)))
-    for step in range(1, spans):
-        crossed = moved(value, count, -step, 0)
-        blocks.append(((step, 0), crossed))
-    for key, crossed in list(blocks):
-        if pair > 1 and key[0] > 0:
-            blocks.append(((key[0], 1), moved(crossed, count, 0, 1)))
+    crossed, near, far = gather_keys(count)
+    blocks = {(0, 0): value}
+    for step, flip in crossed:
+        blocks[(step, flip)] = moved(value, count, -step, 0)
+    for step, flip in near:
+        blocks[(step, flip)] = moved(value, count, 0, 1)
+    for step, flip in far:
+        blocks[(step, flip)] = moved(blocks[(step, 0)], count, 0, 1)
     return blocks
 
 
@@ -269,54 +337,97 @@
     n_ctx = lax.axis_size("ctx")
     n_rep = lax.axis_size("rep")
     n_heads = lax.axis_size("heads")
-    ctx = lax.axis_index("ctx")
-    rep = lax.axis_index("rep")
-    side = lax.axis_index("heads")
-    pair, spans = ctx_routes(n_ctx)
-    base = (ctx * block_len).astype(jnp.int32).reshape(1)
-
     limits = jnp.minimum(cached_length[0], positions)
     marks = jnp.concatenate([limits // 128, limits % 128]).astype(jnp.bfloat16)
     marks = jnp.broadcast_to(marks[:, None], (2 * tokens, size))
-    ordered = queries.reshape(tokens, kv_heads, per_group, size).transpose(1, 0, 2, 3)
-    packed = jnp.concatenate([ordered.reshape(tokens * local_heads, size), marks], axis=0)
+    packed = jnp.concatenate([queries.reshape(tokens * local_heads, size), marks], axis=0)
 
     keys = cache_keys.transpose(1, 0, 2)
     values = cache_values.transpose(1, 0, 2)
     own = (new_keys.transpose(1, 0, 2), new_values.transpose(1, 0, 2))
-
-    parts = []
-    for (step, flip), block in gather_blocks(packed, n_ctx):
-        home = step == 0 and flip == 0
-        part = attend(base, block, keys, values, own if home else None, tokens, per_group)
-        parts.append(part if home else moved(part, n_ctx, step, flip))
-    attended = merge(parts, tokens, kv_heads, per_group)
+    chunks = 2 if kv_heads % 2 == 0 else 1
+    chunk_heads = kv_heads // chunks
+    ranges = [tuple(range(c * chunk_heads, (c + 1) * chunk_heads)) for c in range(chunks)]
+
+    calls = chunks * n_ctx
+    strips = max(s for s in range(1, min(calls, 8) + 1) if s % chunks == 0)
+    strip = out_weight.shape[0] // strips
+    loaded = []
+
+    def run(block, mine):
+        found = []
+        for heads in ranges:
+            index = len(loaded)
+            load = (index * strip, (index + 1) * strip) if index < strips else None
+            made = attend(
+                block,
+                keys,
+                values,
+                own if mine else None,
+                out_weight,
+                load,
+                tokens,
+                per_group,
+                heads,
+            )
+            found.append(made[0])
+            if load is not None:
+                loaded.append(made[1])
+        return found
+
+    crossed, close, far = gather_keys(n_ctx)
+    visitors = {key: moved(packed, n_ctx, -key[0], 0) for key in crossed}
+    visitors.update({key: moved(packed, n_ctx, 0, 1) for key in close})
+    parts = [[part] for part in run(packed, True)]
+    last = [part[0] for part in parts]
+    for key in far:
+        visitors[(key[0], 0)] = after(visitors[(key[0], 0)], *last)
+        visitors[key] = moved(visitors[(key[0], 0)], n_ctx, 0, 1)
+    for key in crossed + close + far:
+        block = after(visitors[key], *last)
+        last = run(block, False)
+        for index, part in enumerate(last):
+            parts[index].append(moved(part, n_ctx, key[0], key[1]))
 
     group_tokens = n_ctx * n_rep * tokens
     near = group_tokens // n_heads
-    span, which = ctx // pair, ctx % pair
-    blocks, places = [], []
-    for (step, flip), block in gather_blocks(attended, n_ctx):
-        source = ((span + step) % spans) * pair + (which + flip) % pair
-        for turn in range(n_rep):
-            passed = block
-            if turn:
-                passed = lax.ppermute(
-                    block, "rep", [(i, (i - turn) % n_rep) for i in range(n_rep)]
-                )
-            row = (source * n_rep + (rep + turn) % n_rep) * tokens
-            places.append((row - side * near) % group_tokens)
-            blocks.append(passed)
-    places = jnp.stack(places).astype(jnp.int32)
     width = out_weight.shape[1]
-    mine, others = project(places, blocks, out_weight, near, min(256, width))
-    result = mine
-    for step in range(1, n_heads):
-        sent = others[(step - 1) * near : step * near]
-        result = result + lax.ppermute(
-            sent, "heads", [(i, (i + step) % n_heads) for i in range(n_heads)]
-        ).astype(jnp.float32)
-    return result.astype(jnp.bfloat16)
+    origins = []
+    held = []
+    for index in range(chunks):
+        attended = merge(parts[index], tokens, chunk_heads, per_group)
+        blocks = []
+        for (step, flip), block in gather_blocks(attended, n_ctx).items():
+            for turn in range(n_rep):
+                passed = block
+                if turn:
+                    passed = lax.ppermute(
+                        block, "rep", [(i, (i - turn) % n_rep) for i in range(n_rep)]
+                    )
+                blocks.append(passed)
+                if index == 0:
+                    origins.append((step, flip, turn))
+        held.append(blocks)
+    so_far = None
+    each = strips // chunks
+    for index in range(chunks - 1):
+        so_far = project(
+            origins, held[index], loaded[index * each : (index + 1) * each], so_far, near, (0, width), False
+        )[0]
+    pieces = 2 if width % (2 * LANES) == 0 else 1
+    results = []
+    for piece in range(pieces):
+        columns = (piece * width // pieces, (piece + 1) * width // pieces)
+        mine, others = project(
+            origins, held[-1], loaded[-each:], so_far, near, columns, True
+        )
+        for step in range(1, n_heads):
+            sent = others[(step - 1) * near : step * near]
+            mine = mine + lax.ppermute(
+                sent, "heads", [(i, (i + step) % n_heads) for i in range(n_heads)]
+            ).astype(jnp.float32)
+        results.append(mine.astype(jnp.bfloat16))
+    return jnp.concatenate(results, axis=1)
 
 
 def solution(mesh):

time: 103 us -> 87.1 us (0.85)
  waiting for transfers between devices: 48.1 us -> 16.9 us
  starting transfers between devices: 15.6 us -> 35.6 us
  local copies, waits for them, and re-layouts: 6.76 us -> 2.78 us
  Pallas kernels: 30.2 us -> 27.9 us
    ppermute x9 -> x15, waiting for transfers between devices: 39.8 us -> 11.6 us  [moved(): return lax.ppermute(value, 'ctx', pairs)]
    ppermute x9 -> x15, starting transfers between devices: 13.5 us -> 32.3 us  [moved(): return lax.ppermute(value, 'ctx', pairs)]
    pallas_call x5 -> x11, Pallas kernels: 29.4 us -> 26.8 us  [the longest x8 21.7 us: attend(): pl.pallas_call(body, out_shape=shapes, in_specs=in_specs, out_specs=[spec...]
    concatenate x1 -> x2, other arithmetic: 0.21 us -> 1.87 us  [the longest x1 1.15 us: local(): jnp.concatenate([queries.reshape(tokens * local_heads, size), marks], axi...]
    ppermute x1 -> x2, waiting for transfers between devices: 6.87 us -> 5.22 us  [local(): lax.ppermute(sent, 'heads', [(i, (i + step) % n_heads) for i in range(n_h...]
    unnamed x8 -> x4, local copies, waits for them, and re-layouts: 1.61 us -> 0.01 us
    ppermute x4 -> x8, waiting for transfers between devices: 1.43 us -> 0.02 us  [local(): lax.ppermute(block, 'rep', [(i, (i - turn) % n_rep) for i in range(n_rep)])]
    transpose x1, local copies, waits for them, and re-layouts: 4.09 us -> 2.76 us  [local(): values = cache_values.transpose(1, 0, 2)]
  transfers between devices with their start and end apart: 14 -> 25, of which waited for: 6 -> 8; matrix products, arithmetic and copies ran while one was open for 4% -> 3% of each run, Pallas kernels for 15% -> 31%
where the time goes in v2:
time: 87.1 us; the launch traced here: 86.7 us
  starting transfers between devices  35.6 us (41%)
  Pallas kernels  27.9 us (32%)
  waiting for transfers between devices  16.9 us (19%)
  local copies, waits for them, and re-layouts  2.78 us (3%)
  other arithmetic  2.68 us (3%)
  between operations  0.9 us (1%)
    ppermute x15, starting transfers between devices, moved(): return lax.ppermute(value, 'ctx', pairs)  32.3 us
    pallas_call x8, Pallas kernels, attend(): pl.pallas_call(body, out_shape=shapes, in_specs=in_specs, out_specs=[spec...  21.7 us
    ppermute x15, waiting for transfers between devices, moved(): return lax.ppermute(value, 'ctx', pairs)  11.6 us
    ppermute x2, waiting for transfers between devices, local(): lax.ppermute(sent, 'heads', [(i, (i + step) % n_heads) for i in range(n_h...  5.22 us
    pallas_call x3, Pallas kernels, project(): pl.pallas_call(functools.partial(project_kernel, origins, len(weights), n...  5.1 us
    transpose x1, local copies, waits for them, and re-layouts, local(): values = cache_values.transpose(1, 0, 2)  2.76 us
    ppermute x2, starting transfers between devices, local(): lax.ppermute(sent, 'heads', [(i, (i + step) % n_heads) for i in range(n_h...  2.16 us
  transfers between devices with their start and end apart: 25, of which 8 were waited for; matrix products, arithmetic and copies ran while one was open for 3% of the time, Pallas kernels for 31%

profile of v2, /device:TPU:0, one launch (start us, length us, event | category | flops | bytes accessed | tf_op | source)
XLA Modules:
  0.0 86.7 jit_solution(17716249871961831210)
XLA Ops:
  0.7 0.7 fusion.1
  1.3 0.1 pad_maximum_fusion.2
  1.4 1.2 %pad_maximum_fusion.q_ref = bf16[1056,128]{1,0:T(8,128)(2,1)S(1)} fusion(bf16[1024,128]{1,0:T(8,128)(2,1)} %bitcast.11, bf16[1056]{0:T(1024)(128)(2,1)S(1)} %pad_maximum_fusion.2), kind=kLoop, calls=%fused_computation.2 | loop fusion | flops 540672 | bytes 534592 | tf_op jit(solution)/shard_map/concatenate | solution.py:343
  2.6 0.0 copy-start
  2.6 0.0 copy-start.1
  2.6 4.1 %collective-permute-start = (bf16[1056,128]{1,0:T(8,128)(2,1)S(1)}, bf16[1056,128]{1,0:T(8,128)(2,1)S(1)}, u32[]{:S(2)}, u32[]{:S(2)}) collective-permute-start(bf16[1056,128]{1,0:T(8,128)(2,1)S(1)} %pad_maximum_fusion.q_ref), channel_id=1, source_target_pairs={{0,8},{4,12},{8,0},{12,4},{1,9},{5,13},{9,1},{13,5},{2,10},{6,14},... | collective-permute-start | bytes 811016 | tf_op jit(solution)/shard_map/ppermute | solution.py:304
  6.7 1.6 %collective-permute-start.2 = (bf16[1056,128]{1,0:T(8,128)(2,1)S(1)}, bf16[1056,128]{1,0:T(8,128)(2,1)S(1)}, u32[]{:S(2)}, u32[]{:S(2)}) collective-permute-start(bf16[1056,128]{1,0:T(8,128)(2,1)S(1)} %pad_maximum_fusion.q_ref), channel_id=1, source_target_pairs={{0,4},{4,0},{8,12},{12,8},{1,5},{5,1},{9,13},{13,9},{2,6},{6,2},{1... | collective-permute-start | bytes 811016 | tf_op jit(solution)/shard_map/ppermute | solution.py:304
  8.3 2.8 %copy_bitcast_fusion = (bf16[4,2048,128]{2,1,0:T(8,128)(2,1)S(1)}, bf16[4,2048,128]{2,1,0:T(8,128)(2,1)S(1)}) fusion(bf16[2048,4,128]{2,1,0:T(4,128)(2,1)} %param.10, bf16[2048,4,128]{2,1,0:T(4,128)(2,1)} %param.9), kind=kLoop, calls=%fused_computation | loop fusion | bytes 8388608 | tf_op jit(solution)/shard_map/transpose | solution.py:346
  11.1 4.2 %attend.9 = (bf16[528,128]{1,0:T(8,128)(2,1)S(1)}, bf16[1024,2048]{1,0:T(8,128)(2,1)S(1)}) custom-call(bf16[1056,128]{1,0:T(8,128)(2,1)S(1)} %pad_maximum_fusion.q_ref, bf16[4,2048,128]{2,1,0:T(8,128)(2,1)S(1)} %get-tuple-element.56.k_ref, bf16[4,2048,128]{2,1,0:T(8,128)(2,1)S(1)} %get-tuple-element.55.v_ref, ...), custom_call_target="tpu_custom_call" | custom-call | flops 536870912 | bytes 2097152 | tf_op jit(solution)/shard_map/attend/pallas_call | solution.py:142
  15.3 4.2 %attend.8 = (bf16[528,128]{1,0:T(8,128)(2,1)S(1)}, bf16[1024,2048]{1,0:T(8,128)(2,1)S(1)}) custom-call(bf16[1056,128]{1,0:T(8,128)(2,1)S(1)} %pad_maximum_fusion.q_ref, bf16[4,2048,128]{2,1,0:T(8,128)(2,1)S(1)} %get-tuple-element.56.k_ref, bf16[4,2048,128]{2,1,0:T(8,128)(2,1)S(1)} %get-tuple-element.55.v_ref, ...), custom_call_target="tpu_custom_call" | custom-call | flops 536870912 | bytes 2097152 | tf_op jit(solution)/shard_map/attend/pallas_call | solution.py:142
  19.5 0.0 collective-permute-done.q_ref
  19.5 0.5 collective-permute-start.4
  20.0 2.2 %attend.11 = (bf16[528,128]{1,0:T(8,128)(2,1)S(1)}, bf16[1024,2048]{1,0:T(8,128)(2,1)S(1)}) custom-call(bf16[1056,128]{1,0:T(8,128)(2,1)S(1)} %collective-permute-done.q_ref, bf16[4,2048,128]{2,1,0:T(8,128)(2,1)S(1)} %get-tuple-element.56.k_ref, bf16[4,2048,128]{2,1,0:T(8,128)(2,1)S(1)} %get-tuple-element.55.v_ref, bf16[8192,2048]{1,0:T(8,128)(2,1)} %rest_0_.11), custom_call_target="tpu_custom_call" | custom-call | flops 536870912 | bytes 2097152 | tf_op jit(solution)/shard_map/attend/pallas_call | solution.py:142
  22.2 3.2 %collective-permute-start.13 = (bf16[528,128]{1,0:T(8,128)(2,1)S(1)}, bf16[528,128]{1,0:T(8,128)(2,1)S(1)}, u32[]{:S(2)}, u32[]{:S(2)}) collective-permute-start(bf16[528,128]{1,0:T(8,128)(2,1)S(1)} %get-tuple-element.34), channel_id=1, source_target_pairs={{0,8},{4,12},{8,0},{12,4},{1,9},{5,13},{9,1},{13,5},{2,10},{6,14},... | collective-permute-start | bytes 405512 | tf_op jit(solution)/shard_map/ppermute | solution.py:304
  25.4 2.2 %attend.10 = (bf16[528,128]{1,0:T(8,128)(2,1)S(1)}, bf16[1024,2048]{1,0:T(8,128)(2,1)S(1)}) custom-call(bf16[1056,128]{1,0:T(8,128)(2,1)S(1)} %collective-permute-done.q_ref, bf16[4,2048,128]{2,1,0:T(8,128)(2,1)S(1)} %get-tuple-element.56.k_ref, bf16[4,2048,128]{2,1,0:T(8,128)(2,1)S(1)} %get-tuple-element.55.v_ref, bf16[8192,2048]{1,0:T(8,128)(2,1)} %rest_0_.11), custom_call_target="tpu_custom_call" | custom-call | flops 536870912 | bytes 2097152 | tf_op jit(solution)/shard_map/attend/pallas_call | solution.py:142
  27.6 0.0 collective-permute-done.2.q_ref
  27.6 2.2 %attend.13 = (bf16[528,128]{1,0:T(8,128)(2,1)S(1)}, bf16[1024,2048]{1,0:T(8,128)(2,1)S(1)}) custom-call(bf16[1056,128]{1,0:T(8,128)(2,1)S(1)} %collective-permute-done.2.q_ref, bf16[4,2048,128]{2,1,0:T(8,128)(2,1)S(1)} %get-tuple-element.56.k_ref, bf16[4,2048,128]{2,1,0:T(8,128)(2,1)S(1)} %get-tuple-element.55.v_ref, bf16[8192,2048]{1,0:T(8,128)(2,1)} %rest_0_.11), custom_call_target="tpu_custom_call" | custom-call | flops 536870912 | bytes 2097152 | tf_op jit(solution)/shard_map/attend/pallas_call | solution.py:142
  29.8 0.1 collective-permute-start.14
  29.9 2.3 %attend.12 = (bf16[528,128]{1,0:T(8,128)(2,1)S(1)}, bf16[1024,2048]{1,0:T(8,128)(2,1)S(1)}) custom-call(bf16[1056,128]{1,0:T(8,128)(2,1)S(1)} %collective-permute-done.2.q_ref, bf16[4,2048,128]{2,1,0:T(8,128)(2,1)S(1)} %get-tuple-element.56.k_ref, bf16[4,2048,128]{2,1,0:T(8,128)(2,1)S(1)} %get-tuple-element.55.v_ref, bf16[8192,2048]{1,0:T(8,128)(2,1)} %rest_0_.11), custom_call_target="tpu_custom_call" | custom-call | flops 536870912 | bytes 2097152 | tf_op jit(solution)/shard_map/attend/pallas_call | solution.py:142
  32.2 0.0 collective-permute-done.4.q_ref
  32.2 2.2 %attend.15 = (bf16[528,128]{1,0:T(8,128)(2,1)S(1)}, bf16[1024,2048]{1,0:T(8,128)(2,1)S(1)}) custom-call(bf16[1056,128]{1,0:T(8,128)(2,1)S(1)} %collective-permute-done.4.q_ref, bf16[4,2048,128]{2,1,0:T(8,128)(2,1)S(1)} %get-tuple-element.56.k_ref, bf16[4,2048,128]{2,1,0:T(8,128)(2,1)S(1)} %get-tuple-element.55.v_ref, bf16[8192,2048]{1,0:T(8,128)(2,1)} %rest_0_.11), custom_call_target="tpu_custom_call" | custom-call | flops 536870912 | bytes 2097152 | tf_op jit(solution)/shard_map/attend/pallas_call | solution.py:142
  34.5 2.2 %collective-permute-start.15 = (bf16[528,128]{1,0:T(8,128)(2,1)S(1)}, bf16[528,128]{1,0:T(8,128)(2,1)S(1)}, u32[]{:S(2)}, u32[]{:S(2)}) collective-permute-start(bf16[528,128]{1,0:T(8,128)(2,1)S(1)} %get-tuple-element.44), channel_id=1, source_target_pairs={{0,12},{4,8},{8,4},{12,0},{1,13},{5,9},{9,5},{13,1},{2,14},{6,10},... | collective-permute-start | bytes 405512 | tf_op jit(solution)/shard_map/ppermute | solution.py:304
  36.7 0.0 collective-permute-start.3
  36.7 2.2 %collective-permute-start.1 = (bf16[528,128]{1,0:T(8,128)(2,1)S(1)}, bf16[528,128]{1,0:T(8,128)(2,1)S(1)}, u32[]{:S(2)}, u32[]{:S(2)}) collective-permute-start(bf16[528,128]{1,0:T(8,128)(2,1)S(1)} %get-tuple-element.33), channel_id=1, source_target_pairs={{0,8},{4,12},{8,0},{12,4},{1,9},{5,13},{9,1},{13,5},{2,10},{6,14},... | collective-permute-start | bytes 405512 | tf_op jit(solution)/shard_map/ppermute | solution.py:304
  38.9 2.2 %attend.14 = (bf16[528,128]{1,0:T(8,128)(2,1)S(1)}, bf16[1024,2048]{1,0:T(8,128)(2,1)S(1)}) custom-call(bf16[1056,128]{1,0:T(8,128)(2,1)S(1)} %collective-permute-done.4.q_ref, bf16[4,2048,128]{2,1,0:T(8,128)(2,1)S(1)} %get-tuple-element.56.k_ref, bf16[4,2048,128]{2,1,0:T(8,128)(2,1)S(1)} %get-tuple-element.55.v_ref, bf16[8192,2048]{1,0:T(8,128)(2,1)} %rest_0_.11), custom_call_target="tpu_custom_call" | custom-call | flops 536870912 | bytes 2097152 | tf_op jit(solution)/shard_map/attend/pallas_call | solution.py:142
  41.1 2.2 %collective-permute-start.5 = (bf16[528,128]{1,0:T(8,128)(2,1)S(1)}, bf16[528,128]{1,0:T(8,128)(2,1)S(1)}, u32[]{:S(2)}, u32[]{:S(2)}) collective-permute-start(bf16[528,128]{1,0:T(8,128)(2,1)S(1)} %get-tuple-element.39), channel_id=1, source_target_pairs={{0,12},{4,8},{8,4},{12,0},{1,13},{5,9},{9,5},{13,1},{2,14},{6,10},... | collective-permute-start | bytes 405512 | tf_op jit(solution)/shard_map/ppermute | solution.py:304
  43.4 0.0 collective-permute-done.13.refs_1_
  43.4 0.0 collective-permute-done.15.refs_3_
  43.4 0.5 merge.3.refs_0_
  43.9 8.0 %collective-permute-start.17 = (bf16[16,4096]{1,0:T(8,128)(2,1)S(1)}, bf16[16,4096]{1,0:T(8,128)(2,1)S(1)}, u32[]{:S(2)}, u32[]{:S(2)}) collective-permute-start(bf16[16,4096]{1,0:T(8,128)(2,1)S(1)} %merge.3.refs_0_), channel_id=1, source_target_pairs={{0,8},{4,12},{8,0},{12,4},{1,9},{5,13},{9,1},{13,5},{2,10},{6,14},... | collective-permute-start | bytes 393224 | tf_op jit(solution)/shard_map/ppermute | solution.py:304
  51.9 0.8 collective-permute-start.19
  52.7 0.0 collective-permute-done.3.refs_2_
  52.7 0.0 collective-permute-start.16
  52.7 1.6 %collective-permute-done.1.refs_1_ = bf16[528,128]{1,0:T(8,128)(2,1)S(1)} collective-permute-done((bf16[528,128]{1,0:T(8,128)(2,1)S(1)}, bf16[528,128]{1,0:T(8,128)(2,1)S(1)}, u32[]{:S(2)}, u32[]{:S(2)}) %collective-permute-start.1) | collective-permute-done | bytes 135200 | tf_op jit(solution)/shard_map/ppermute | solution.py:304
  54.4 0.5 merge.2.refs_0_
  54.9 4.9 %collective-permute-start.7 = (bf16[16,4096]{1,0:T(8,128)(2,1)S(1)}, bf16[16,4096]{1,0:T(8,128)(2,1)S(1)}, u32[]{:S(2)}, u32[]{:S(2)}) collective-permute-start(bf16[16,4096]{1,0:T(8,128)(2,1)S(1)} %merge.2.refs_0_), channel_id=1, source_target_pairs={{0,8},{4,12},{8,0},{12,4},{1,9},{5,13},{9,1},{13,5},{2,10},{6,14},... | collective-permute-start | bytes 393224 | tf_op jit(solution)/shard_map/ppermute | solution.py:304
  59.8 3.0 %collective-permute-done.17.refs_2_ = bf16[16,4096]{1,0:T(8,128)(2,1)S(1)} collective-permute-done((bf16[16,4096]{1,0:T(8,128)(2,1)S(1)}, bf16[16,4096]{1,0:T(8,128)(2,1)S(1)}, u32[]{:S(2)}, u32[]{:S(2)}) %collective-permute-start.17) | collective-permute-done | bytes 131104 | tf_op jit(solution)/shard_map/ppermute | solution.py:304
  62.9 0.0 collective-permute-start.21
  62.9 2.0 %collective-permute-start.9 = (bf16[16,4096]{1,0:T(8,128)(2,1)S(1)}, bf16[16,4096]{1,0:T(8,128)(2,1)S(1)}, u32[]{:S(2)}, u32[]{:S(2)}) collective-permute-start(bf16[16,4096]{1,0:T(8,128)(2,1)S(1)} %merge.2.refs_0_), channel_id=1, source_target_pairs={{0,4},{4,0},{8,12},{12,8},{1,5},{5,1},{9,13},{13,9},{2,6},{6,2},{1... | collective-permute-start | bytes 393224 | tf_op jit(solution)/shard_map/ppermute | solution.py:304
  64.9 0.0 collective-permute-done.19.refs_4_
  64.9 0.0 collective-permute-start.18
  64.9 0.0 collective-permute-done.16.refs_1_
  64.9 0.5 collective-permute-start.20
  65.4 0.9 %collective-permute-done.7.refs_2_ = bf16[16,4096]{1,0:T(8,128)(2,1)S(1)} collective-permute-done((bf16[16,4096]{1,0:T(8,128)(2,1)S(1)}, bf16[16,4096]{1,0:T(8,128)(2,1)S(1)}, u32[]{:S(2)}, u32[]{:S(2)}) %collective-permute-start.7) | collective-permute-done | bytes 131104 | tf_op jit(solution)/shard_map/ppermute | solution.py:304
  66.4 0.5 collective-permute-start.11
  66.8 2.4 %collective-permute-done.21.refs_6_ = bf16[16,4096]{1,0:T(8,128)(2,1)S(1)} collective-permute-done((bf16[16,4096]{1,0:T(8,128)(2,1)S(1)}, bf16[16,4096]{1,0:T(8,128)(2,1)S(1)}, u32[]{:S(2)}, u32[]{:S(2)}) %collective-permute-start.21) | collective-permute-done | bytes 131104 | tf_op jit(solution)/shard_map/ppermute | solution.py:304
  69.3 2.7 %collective-permute-done.9.refs_4_ = bf16[16,4096]{1,0:T(8,128)(2,1)S(1)} collective-permute-done((bf16[16,4096]{1,0:T(8,128)(2,1)S(1)}, bf16[16,4096]{1,0:T(8,128)(2,1)S(1)}, u32[]{:S(2)}, u32[]{:S(2)}) %collective-permute-start.9) | collective-permute-done | bytes 131104 | tf_op jit(solution)/shard_map/ppermute | solution.py:304
  72.0 0.0 collective-permute-start.6
  72.0 0.0 collective-permute-done.18.refs_3_
  72.0 0.5 collective-permute-start.8
  72.5 0.0 collective-permute-done.20.refs_5_
  72.5 0.1 collective-permute-start.10
  72.6 0.8 collective-permute-done.11.refs_6_
  73.4 2.4 %project.3.refs_12_ = f32[128,2048]{1,0:T(8,128)S(1)} custom-call(bf16[16,4096]{1,0:T(8,128)(2,1)S(1)} %merge.3.refs_0_, bf16[16,4096]{1,0:T(8,128)(2,1)S(1)} %collective-permute-done.16.refs_1_, bf16[16,4096]{1,0:T(8,128)(2,1)S(1)} %collective-permute-done.17.refs_2_, bf16[16,4096]{1,0:T(8,128)(2,1)S(1)} %collective-permute-done.18.refs_3_, ...), custom_call_target="tpu_custom_call" | custom-call | flops 2147483648 | bytes 16777216 | tf_op jit(solution)/shard_map/project/pallas_call | solution.py:265
  75.8 0.0 collective-permute-done.6.refs_1_
  75.8 0.0 collective-permute-done.10.refs_5_
  75.8 0.0 collective-permute-done.12.refs_7_
  75.8 1.4 %project.4 = (f32[64,1024]{1,0:T(8,128)S(1)}, bf16[64,1024]{1,0:T(8,128)(2,1)S(1)}) custom-call(bf16[16,4096]{1,0:T(8,128)(2,1)S(1)} %merge.2.refs_0_, bf16[16,4096]{1,0:T(8,128)(2,1)S(1)} %collective-permute-done.6.refs_1_, bf16[16,4096]{1,0:T(8,128)(2,1)S(1)} %collective-permute-done.7.refs_2_, bf16[16,4096]{1,0:T(8,128)(2,1)S(1)} %collective-permute-done.8.refs_3_, ...), custom_call_target="tpu_custom_call" | custom-call | flops 1073741824 | bytes 8388608 | tf_op jit(solution)/shard_map/project/pallas_call | solution.py:265
  77.2 1.5 %collective-permute-start.23 = (bf16[64,1024]{1,0:T(8,128)(2,1)S(1)}, bf16[64,1024]{1,0:T(8,128)(2,1)S(1)}, u32[]{:S(2)}, u32[]{:S(2)}) collective-permute-start(bf16[64,1024]{1,0:T(8,128)(2,1)S(1)} %get-tuple-element.50), channel_id=1, source_target_pairs={{0,2},{2,0},{1,3},{3,1},{4,6},{6,4},{5,7},{7,5},{8,10},{10,8},{9,1... | collective-permute-start | bytes 393224 | tf_op jit(solution)/shard_map/ppermute | solution.py:426
  78.7 1.3 %project.5 = (f32[64,1024]{1,0:T(8,128)S(1)}, bf16[64,1024]{1,0:T(8,128)(2,1)S(1)}) custom-call(bf16[16,4096]{1,0:T(8,128)(2,1)S(1)} %merge.2.refs_0_, bf16[16,4096]{1,0:T(8,128)(2,1)S(1)} %collective-permute-done.6.refs_1_, bf16[16,4096]{1,0:T(8,128)(2,1)S(1)} %collective-permute-done.7.refs_2_, bf16[16,4096]{1,0:T(8,128)(2,1)S(1)} %collective-permute-done.8.refs_3_, ...), custom_call_target="tpu_custom_call" | custom-call | flops 1073741824 | bytes 8388608 | tf_op jit(solution)/shard_map/project/pallas_call | solution.py:265
  80.1 0.6 collective-permute-start.24
  80.7 2.6 %collective-permute-done.23 = bf16[64,1024]{1,0:T(8,128)(2,1)S(1)} collective-permute-done((bf16[64,1024]{1,0:T(8,128)(2,1)S(1)}, bf16[64,1024]{1,0:T(8,128)(2,1)S(1)}, u32[]{:S(2)}, u32[]{:S(2)}) %collective-permute-start.23) | collective-permute-done | bytes 131104 | tf_op jit(solution)/shard_map/ppermute | solution.py:426
  83.4 2.6 %collective-permute-done.24 = bf16[64,1024]{1,0:T(8,128)(2,1)S(1)} collective-permute-done((bf16[64,1024]{1,0:T(8,128)(2,1)S(1)}, bf16[64,1024]{1,0:T(8,128)(2,1)S(1)}, u32[]{:S(2)}, u32[]{:S(2)}) %collective-permute-start.24) | collective-permute-done | bytes 131104 | tf_op jit(solution)/shard_map/ppermute | solution.py:426
  86.0 0.7 pad_maximum_fusion.1
  (12 shorter events, 0.1 us)
Async XLA Ops:
  2.6 8.5 %copy-start = (bf16[16,4,128]{2,1,0:T(4,128)(2,1)S(1)}, bf16[16,4,128]{2,1,0:T(4,128)(2,1)}, u32[]{:S(2)}) copy-start(bf16[16,4,128]{2,1,0:T(4,128)(2,1)} %param.12) | copy-start | bytes 49156
  2.6 8.5 %copy-start.1 = (bf16[16,4,128]{2,1,0:T(4,128)(2,1)S(1)}, bf16[16,4,128]{2,1,0:T(4,128)(2,1)}, u32[]{:S(2)}) copy-start(bf16[16,4,128]{2,1,0:T(4,128)(2,1)} %param.11) | copy-start | bytes 49156
  2.6 16.9 %collective-permute-start = (bf16[1056,128]{1,0:T(8,128)(2,1)S(1)}, bf16[1056,128]{1,0:T(8,128)(2,1)S(1)}, u32[]{:S(2)}, u32[]{:S(2)}) collective-permute-start(bf16[1056,128]{1,0:T(8,128)(2,1)S(1)} %pad_maximum_fusion.q_ref), channel_id=1, source_target_pairs={{0,8},{4,12},{8,0},{12,4},{1,9},{5,13},{9,1},{13,5},{2,10},{6,14},... | collective-permute-start | bytes 811016 | tf_op jit(solution)/shard_map/ppermute | solution.py:304
  6.7 20.9 %collective-permute-start.2 = (bf16[1056,128]{1,0:T(8,128)(2,1)S(1)}, bf16[1056,128]{1,0:T(8,128)(2,1)S(1)}, u32[]{:S(2)}, u32[]{:S(2)}) collective-permute-start(bf16[1056,128]{1,0:T(8,128)(2,1)S(1)} %pad_maximum_fusion.q_ref), channel_id=1, source_target_pairs={{0,4},{4,0},{8,12},{12,8},{1,5},{5,1},{9,13},{13,9},{2,6},{6,2},{1... | collective-permute-start | bytes 811016 | tf_op jit(solution)/shard_map/ppermute | solution.py:304
  19.5 12.8 %collective-permute-start.4 = (bf16[1056,128]{1,0:T(8,128)(2,1)S(1)}, bf16[1056,128]{1,0:T(8,128)(2,1)S(1)}, u32[]{:S(2)}, u32[]{:S(2)}) collective-permute-start(bf16[1056,128]{1,0:T(8,128)(2,1)S(1)} %collective-permute-done.q_ref), channel_id=1, source_target_pairs={{0,4},{4,0},{8,12},{12,8},{1,5},{5,1},{9,13},{13,9},{2,6},{6,2},{1... | collective-permute-start | bytes 811016 | tf_op jit(solution)/shard_map/ppermute | solution.py:304
  22.2 21.2 %collective-permute-start.13 = (bf16[528,128]{1,0:T(8,128)(2,1)S(1)}, bf16[528,128]{1,0:T(8,128)(2,1)S(1)}, u32[]{:S(2)}, u32[]{:S(2)}) collective-permute-start(bf16[528,128]{1,0:T(8,128)(2,1)S(1)} %get-tuple-element.34), channel_id=1, source_target_pairs={{0,8},{4,12},{8,0},{12,4},{1,9},{5,13},{9,1},{13,5},{2,10},{6,14},... | collective-permute-start | bytes 405512 | tf_op jit(solution)/shard_map/ppermute | solution.py:304
  29.8 11.3 %collective-permute-start.14 = (bf16[528,128]{1,0:T(8,128)(2,1)S(1)}, bf16[528,128]{1,0:T(8,128)(2,1)S(1)}, u32[]{:S(2)}, u32[]{:S(2)}) collective-permute-start(bf16[528,128]{1,0:T(8,128)(2,1)S(1)} %get-tuple-element.37), channel_id=1, source_target_pairs={{0,4},{4,0},{8,12},{12,8},{1,5},{5,1},{9,13},{13,9},{2,6},{6,2},{1... | collective-permute-start | bytes 405512 | tf_op jit(solution)/shard_map/ppermute | solution.py:304
  34.5 8.9 %collective-permute-start.15 = (bf16[528,128]{1,0:T(8,128)(2,1)S(1)}, bf16[528,128]{1,0:T(8,128)(2,1)S(1)}, u32[]{:S(2)}, u32[]{:S(2)}) collective-permute-start(bf16[528,128]{1,0:T(8,128)(2,1)S(1)} %get-tuple-element.44), channel_id=1, source_target_pairs={{0,12},{4,8},{8,4},{12,0},{1,13},{5,9},{9,5},{13,1},{2,14},{6,10},... | collective-permute-start | bytes 405512 | tf_op jit(solution)/shard_map/ppermute | solution.py:304
  36.7 16.0 %collective-permute-start.3 = (bf16[528,128]{1,0:T(8,128)(2,1)S(1)}, bf16[528,128]{1,0:T(8,128)(2,1)S(1)}, u32[]{:S(2)}, u32[]{:S(2)}) collective-permute-start(bf16[528,128]{1,0:T(8,128)(2,1)S(1)} %get-tuple-element.36), channel_id=1, source_target_pairs={{0,4},{4,0},{8,12},{12,8},{1,5},{5,1},{9,13},{13,9},{2,6},{6,2},{1... | collective-permute-start | bytes 405512 | tf_op jit(solution)/shard_map/ppermute | solution.py:304
  36.7 17.7 %collective-permute-start.1 = (bf16[528,128]{1,0:T(8,128)(2,1)S(1)}, bf16[528,128]{1,0:T(8,128)(2,1)S(1)}, u32[]{:S(2)}, u32[]{:S(2)}) collective-permute-start(bf16[528,128]{1,0:T(8,128)(2,1)S(1)} %get-tuple-element.33), channel_id=1, source_target_pairs={{0,8},{4,12},{8,0},{12,4},{1,9},{5,13},{9,1},{13,5},{2,10},{6,14},... | collective-permute-start | bytes 405512 | tf_op jit(solution)/shard_map/ppermute | solution.py:304
  41.1 13.2 %collective-permute-start.5 = (bf16[528,128]{1,0:T(8,128)(2,1)S(1)}, bf16[528,128]{1,0:T(8,128)(2,1)S(1)}, u32[]{:S(2)}, u32[]{:S(2)}) collective-permute-start(bf16[528,128]{1,0:T(8,128)(2,1)S(1)} %get-tuple-element.39), channel_id=1, source_target_pairs={{0,12},{4,8},{8,4},{12,0},{1,13},{5,9},{9,5},{13,1},{2,14},{6,10},... | collective-permute-start | bytes 405512 | tf_op jit(solution)/shard_map/ppermute | solution.py:304
  43.9 19.0 %collective-permute-start.17 = (bf16[16,4096]{1,0:T(8,128)(2,1)S(1)}, bf16[16,4096]{1,0:T(8,128)(2,1)S(1)}, u32[]{:S(2)}, u32[]{:S(2)}) collective-permute-start(bf16[16,4096]{1,0:T(8,128)(2,1)S(1)} %merge.3.refs_0_), channel_id=1, source_target_pairs={{0,8},{4,12},{8,0},{12,4},{1,9},{5,13},{9,1},{13,5},{2,10},{6,14},... | collective-permute-start | bytes 393224 | tf_op jit(solution)/shard_map/ppermute | solution.py:304
  51.9 13.0 %collective-permute-start.19 = (bf16[16,4096]{1,0:T(8,128)(2,1)S(1)}, bf16[16,4096]{1,0:T(8,128)(2,1)S(1)}, u32[]{:S(2)}, u32[]{:S(2)}) collective-permute-start(bf16[16,4096]{1,0:T(8,128)(2,1)S(1)} %merge.3.refs_0_), channel_id=1, source_target_pairs={{0,4},{4,0},{8,12},{12,8},{1,5},{5,1},{9,13},{13,9},{2,6},{6,2},{1... | collective-permute-start | bytes 393224 | tf_op jit(solution)/shard_map/ppermute | solution.py:304
  52.7 12.2 %collective-permute-start.16 = (bf16[16,4096]{1,0:T(8,128)(2,1)S(1)}, bf16[16,4096]{1,0:T(8,128)(2,1)S(1)}, u32[]{:S(2)}, u32[]{:S(2)}) collective-permute-start(bf16[16,4096]{1,0:T(8,128)(2,1)S(1)} %merge.3.refs_0_), channel_id=1, source_target_pairs={{0,1},{1,0},{2,3},{3,2},{4,5},{5,4},{6,7},{7,6},{8,9},{9,8},{10,11... | collective-permute-start | bytes 393224 | tf_op jit(solution)/shard_map/ppermute | solution.py:404
  54.9 11.4 %collective-permute-start.7 = (bf16[16,4096]{1,0:T(8,128)(2,1)S(1)}, bf16[16,4096]{1,0:T(8,128)(2,1)S(1)}, u32[]{:S(2)}, u32[]{:S(2)}) collective-permute-start(bf16[16,4096]{1,0:T(8,128)(2,1)S(1)} %merge.2.refs_0_), channel_id=1, source_target_pairs={{0,8},{4,12},{8,0},{12,4},{1,9},{5,13},{9,1},{13,5},{2,10},{6,14},... | collective-permute-start | bytes 393224 | tf_op jit(solution)/shard_map/ppermute | solution.py:304
  62.9 6.4 %collective-permute-start.21 = (bf16[16,4096]{1,0:T(8,128)(2,1)S(1)}, bf16[16,4096]{1,0:T(8,128)(2,1)S(1)}, u32[]{:S(2)}, u32[]{:S(2)}) collective-permute-start(bf16[16,4096]{1,0:T(8,128)(2,1)S(1)} %collective-permute-done.17.refs_2_), channel_id=1, source_target_pairs={{0,4},{4,0},{8,12},{12,8},{1,5},{5,1},{9,13},{13,9},{2,6},{6,2},{1... | collective-permute-start | bytes 393224 | tf_op jit(solution)/shard_map/ppermute | solution.py:304
  62.9 9.1 %collective-permute-start.9 = (bf16[16,4096]{1,0:T(8,128)(2,1)S(1)}, bf16[16,4096]{1,0:T(8,128)(2,1)S(1)}, u32[]{:S(2)}, u32[]{:S(2)}) collective-permute-start(bf16[16,4096]{1,0:T(8,128)(2,1)S(1)} %merge.2.refs_0_), channel_id=1, source_target_pairs={{0,4},{4,0},{8,12},{12,8},{1,5},{5,1},{9,13},{13,9},{2,6},{6,2},{1... | collective-permute-start | bytes 393224 | tf_op jit(solution)/shard_map/ppermute | solution.py:304
  64.9 7.1 %collective-permute-start.18 = (bf16[16,4096]{1,0:T(8,128)(2,1)S(1)}, bf16[16,4096]{1,0:T(8,128)(2,1)S(1)}, u32[]{:S(2)}, u32[]{:S(2)}) collective-permute-start(bf16[16,4096]{1,0:T(8,128)(2,1)S(1)} %collective-permute-done.17.refs_2_), channel_id=1, source_target_pairs={{0,1},{1,0},{2,3},{3,2},{4,5},{5,4},{6,7},{7,6},{8,9},{9,8},{10,11... | collective-permute-start | bytes 393224 | tf_op jit(solution)/shard_map/ppermute | solution.py:404
  64.9 7.6 %collective-permute-start.20 = (bf16[16,4096]{1,0:T(8,128)(2,1)S(1)}, bf16[16,4096]{1,0:T(8,128)(2,1)S(1)}, u32[]{:S(2)}, u32[]{:S(2)}) collective-permute-start(bf16[16,4096]{1,0:T(8,128)(2,1)S(1)} %collective-permute-done.19.refs_4_), channel_id=1, source_target_pairs={{0,1},{1,0},{2,3},{3,2},{4,5},{5,4},{6,7},{7,6},{8,9},{9,8},{10,11... | collective-permute-start | bytes 393224 | tf_op jit(solution)/shard_map/ppermute | solution.py:404
  66.4 7.0 %collective-permute-start.11 = (bf16[16,4096]{1,0:T(8,128)(2,1)S(1)}, bf16[16,4096]{1,0:T(8,128)(2,1)S(1)}, u32[]{:S(2)}, u32[]{:S(2)}) collective-permute-start(bf16[16,4096]{1,0:T(8,128)(2,1)S(1)} %collective-permute-done.7.refs_2_), channel_id=1, source_target_pairs={{0,4},{4,0},{8,12},{12,8},{1,5},{5,1},{9,13},{13,9},{2,6},{6,2},{1... | collective-permute-start | bytes 393224 | tf_op jit(solution)/shard_map/ppermute | solution.py:304
  69.3 4.1 %collective-permute-start.22 = (bf16[16,4096]{1,0:T(8,128)(2,1)S(1)}, bf16[16,4096]{1,0:T(8,128)(2,1)S(1)}, u32[]{:S(2)}, u32[]{:S(2)}) collective-permute-start(bf16[16,4096]{1,0:T(8,128)(2,1)S(1)} %collective-permute-done.21.refs_6_), channel_id=1, source_target_pairs={{0,1},{1,0},{2,3},{3,2},{4,5},{5,4},{6,7},{7,6},{8,9},{9,8},{10,11... | collective-permute-start | bytes 393224 | tf_op jit(solution)/shard_map/ppermute | solution.py:404
  72.0 3.8 %collective-permute-start.6 = (bf16[16,4096]{1,0:T(8,128)(2,1)S(1)}, bf16[16,4096]{1,0:T(8,128)(2,1)S(1)}, u32[]{:S(2)}, u32[]{:S(2)}) collective-permute-start(bf16[16,4096]{1,0:T(8,128)(2,1)S(1)} %merge.2.refs_0_), channel_id=1, source_target_pairs={{0,1},{1,0},{2,3},{3,2},{4,5},{5,4},{6,7},{7,6},{8,9},{9,8},{10,11... | collective-permute-start | bytes 393224 | tf_op jit(solution)/shard_map/ppermute | solution.py:404
  72.0 3.9 %collective-permute-start.8 = (bf16[16,4096]{1,0:T(8,128)(2,1)S(1)}, bf16[16,4096]{1,0:T(8,128)(2,1)S(1)}, u32[]{:S(2)}, u32[]{:S(2)}) collective-permute-start(bf16[16,4096]{1,0:T(8,128)(2,1)S(1)} %collective-permute-done.7.refs_2_), channel_id=1, source_target_pairs={{0,1},{1,0},{2,3},{3,2},{4,5},{5,4},{6,7},{7,6},{8,9},{9,8},{10,11... | collective-permute-start | bytes 393224 | tf_op jit(solution)/shard_map/ppermute | solution.py:404
  72.5 3.3 %collective-permute-start.10 = (bf16[16,4096]{1,0:T(8,128)(2,1)S(1)}, bf16[16,4096]{1,0:T(8,128)(2,1)S(1)}, u32[]{:S(2)}, u32[]{:S(2)}) collective-permute-start(bf16[16,4096]{1,0:T(8,128)(2,1)S(1)} %collective-permute-done.9.refs_4_), channel_id=1, source_target_pairs={{0,1},{1,0},{2,3},{3,2},{4,5},{5,4},{6,7},{7,6},{8,9},{9,8},{10,11... | collective-permute-start | bytes 393224 | tf_op jit(solution)/shard_map/ppermute | solution.py:404
  73.4 2.5 %collective-permute-start.12 = (bf16[16,4096]{1,0:T(8,128)(2,1)S(1)}, bf16[16,4096]{1,0:T(8,128)(2,1)S(1)}, u32[]{:S(2)}, u32[]{:S(2)}) collective-permute-start(bf16[16,4096]{1,0:T(8,128)(2,1)S(1)} %collective-permute-done.11.refs_6_), channel_id=1, source_target_pairs={{0,1},{1,0},{2,3},{3,2},{4,5},{5,4},{6,7},{7,6},{8,9},{9,8},{10,11... | collective-permute-start | bytes 393224 | tf_op jit(solution)/shard_map/ppermute | solution.py:404
  77.2 6.1 %collective-permute-start.23 = (bf16[64,1024]{1,0:T(8,128)(2,1)S(1)}, bf16[64,1024]{1,0:T(8,128)(2,1)S(1)}, u32[]{:S(2)}, u32[]{:S(2)}) collective-permute-start(bf16[64,1024]{1,0:T(8,128)(2,1)S(1)} %get-tuple-element.50), channel_id=1, source_target_pairs={{0,2},{2,0},{1,3},{3,1},{4,6},{6,4},{5,7},{7,5},{8,10},{10,8},{9,1... | collective-permute-start | bytes 393224 | tf_op jit(solution)/shard_map/ppermute | solution.py:426
  80.1 5.9 %collective-permute-start.24 = (bf16[64,1024]{1,0:T(8,128)(2,1)S(1)}, bf16[64,1024]{1,0:T(8,128)(2,1)S(1)}, u32[]{:S(2)}, u32[]{:S(2)}) collective-permute-start(bf16[64,1024]{1,0:T(8,128)(2,1)S(1)} %get-tuple-element.52), channel_id=1, source_target_pairs={{0,2},{2,0},{1,3},{3,1},{4,6},{6,4},{5,7},{7,5},{8,10},{10,8},{9,1... | collective-permute-start | bytes 393224 | tf_op jit(solution)/shard_map/ppermute | solution.py:426

commit v3 on v2

v3 whole, which is shorter than its diff:
```python
import functools
import math

import jax
import jax.numpy as jnp
from jax import lax
from jax.experimental import pallas as pl
from jax.experimental.pallas import tpu as pltpu
from jax.sharding import PartitionSpec as P


NEG_FILL = -1e30
NEG_FLOOR = -1e29
LANES = 128
PACK = 16
STREAMS = 4
VMEM = pltpu.MemorySpace.VMEM
SMEM = pltpu.MemorySpace.SMEM
HBM = pltpu.MemorySpace.HBM


def round_up(value, step):
    return (value + step - 1) // step * step


def stat_rows(rows):
    return round_up(3 * (rows // LANES), PACK)


def start_strips(w_ref, strips, strip_refs, sem_ref):
    copies = []
    for index, (strip, strip_ref) in enumerate(zip(strips, strip_refs)):
        rows = strip_ref.shape[0]
        part = rows // STREAMS
        for stream in range(STREAMS):
            copies.append(
                pltpu.make_async_copy(
                    w_ref.at[strip * rows + stream * part : strip * rows + (stream + 1) * part, :],
                    strip_ref.at[stream * part : (stream + 1) * part, :],
                    sem_ref.at[index * STREAMS + stream],
                )
            )
            copies[-1].start()
    return copies


def load_kernel(strips, w_ref, *rest):
    for copy in start_strips(w_ref, strips, rest[:-1], rest[-1]):
        copy.wait()


def load(weight, strips, rows):
    spec = pl.BlockSpec(memory_space=VMEM)
    shape = jax.ShapeDtypeStruct((rows, weight.shape[1]), weight.dtype)
    return pl.pallas_call(
        functools.partial(load_kernel, strips),
        out_shape=[shape] * len(strips),
        in_specs=[pl.BlockSpec(memory_space=HBM)],
        out_specs=[spec] * len(strips),
        scratch_shapes=[pltpu.SemaphoreType.DMA((len(strips) * STREAMS,))],
        compiler_params=pltpu.CompilerParams(vmem_limit_bytes=2 * 1024 * 1024),
        cost_estimate=pl.CostEstimate(
            flops=0, bytes_accessed=len(strips) * rows * weight.shape[1] * 2, transcendentals=0
        ),
        name="load",
    )(pltpu.with_memory_space_constraint(weight, HBM))


def put_levels(out_ref, begin, level):
    first = level.astype(jnp.bfloat16).astype(jnp.float32)
    second = (level - first).astype(jnp.bfloat16).astype(jnp.float32)
    third = level - first - second
    count = level.shape[0]
    extra = stat_rows(count * LANES)
    blank = jnp.zeros((extra - 3 * count, LANES), jnp.float32)
    joined = jnp.concatenate([first, second, third, blank], axis=0)
    out_ref[begin : begin + extra, :] = joined.astype(jnp.bfloat16)


def pack_kernel(positions_ref, length_ref, q_ref, out_ref, mark_ref, sem_ref):
    rows, size = q_ref.shape
    tokens = mark_ref.shape[0] // 2
    copy = pltpu.make_async_copy(q_ref, out_ref.at[:rows, :], sem_ref)
    copy.start()
    for t in range(tokens):
        limit = jnp.minimum(length_ref[0], positions_ref[t])
        high = lax.shift_right_logical(limit, 7).astype(jnp.float32)
        low = lax.bitwise_and(limit, 127).astype(jnp.float32)
        mark_ref[t : t + 1, :] = jnp.full((1, size), high, jnp.float32)
        mark_ref[tokens + t : tokens + t + 1, :] = jnp.full((1, size), low, jnp.float32)
    out_ref[rows:, :] = mark_ref[...].astype(jnp.bfloat16)
    copy.wait()


def pack(queries, positions, length):
    tokens, local_heads, size = queries.shape
    rows = tokens * local_heads
    return pl.pallas_call(
        pack_kernel,
        out_shape=jax.ShapeDtypeStruct((rows + 2 * tokens, size), jnp.bfloat16),
        in_specs=[pl.BlockSpec(memory_space=SMEM)] * 2 + [pl.BlockSpec(memory_space=HBM)],
        out_specs=pl.BlockSpec(memory_space=VMEM),
        scratch_shapes=[pltpu.VMEM((2 * tokens, size), jnp.float32), pltpu.SemaphoreType.DMA],
        compiler_params=pltpu.CompilerParams(vmem_limit_bytes=4 * 1024 * 1024),
        name="pack",
    )(positions, length, pltpu.with_memory_space_constraint(queries.reshape(rows, size), HBM))


def attend_kernel(
    tokens, keep, per_group, with_own, with_prev, strips, q_ref, k_ref, v_ref, *rest
):
    rest = list(rest)
    side = lax.rem(lax.axis_index("ctx").astype(jnp.int32), 2)
    if with_own:
        nk_ref, nv_ref = rest.pop(0), rest.pop(0)
    if with_prev:
        prev_ref = rest.pop(0)
    if strips:
        w_ref = rest.pop(0)
    out_ref = rest.pop(0)
    strip_refs = [rest.pop(0) for _ in strips]
    bound_ref = rest.pop(0)
    copies = start_strips(w_ref, strips, strip_refs, rest.pop(0)) if strips else []
    head_rows = tokens * per_group
    kv_heads, block_len, size = k_ref.shape
    half = kv_heads // 2
    origin = (side if keep else 1 - side) * half
    rows = half * head_rows
    begin = 0
    if with_prev:
        begin = prev_ref.shape[0]
        out_ref[:begin, :] = prev_ref[...]
    local_heads = (q_ref.shape[0] - 2 * tokens) // tokens
    factor = size ** (-0.5) * math.log2(math.e)
    high = q_ref[tokens * local_heads : tokens * local_heads + tokens, :].astype(jnp.float32)
    low = q_ref[tokens * local_heads + tokens :, :].astype(jnp.float32)
    base = lax.axis_index("ctx").astype(jnp.int32) * block_len
    bound = high * 128.0 + low - base.astype(jnp.float32)
    bound_ref[...] = jnp.broadcast_to(bound[:, None, :], (tokens, per_group, LANES)).reshape(
        head_rows, LANES
    )
    lane = lax.broadcasted_iota(jnp.int32, (1, LANES), 1).astype(jnp.float32)
    lane_id = lax.broadcasted_iota(jnp.int32, (LANES, LANES), 1)
    stats = jnp.zeros((LANES, LANES), jnp.float32)
    limit = bound_ref[...]
    for order in range(half):
        head = origin + order
        q = jnp.concatenate(
            [
                q_ref[
                    pl.ds(
                        pl.multiple_of(t * local_heads + head * per_group, per_group), per_group
                    ),
                    :,
                ]
                for t in range(tokens)
            ],
            axis=0,
        )
        scores = lax.dot_general(
            q, k_ref[head], (((1,), (1,)), ((), ())), preferred_element_type=jnp.float32
        )
        pieces = []
        for start in range(0, block_len, LANES):
            seen = (lane + float(start)) < limit
            pieces.append(jnp.where(seen, scores[:, start : start + LANES], NEG_FILL))
        best = functools.reduce(jnp.maximum, pieces)
        top = jnp.max(best, axis=-1, keepdims=True)
        if with_own:
            nk = jnp.broadcast_to(
                nk_ref[head].astype(jnp.float32)[:, None, :], (tokens, per_group, size)
            ).reshape(head_rows, size)
            own = jnp.sum(q.astype(jnp.float32) * nk, axis=-1, keepdims=True)
            top = jnp.maximum(top, own)
        top = jnp.maximum(top, NEG_FLOOR)
        weights = [jnp.exp2((piece - top) * factor) for piece in pieces]
        total = jnp.sum(functools.reduce(jnp.add, weights), axis=-1, keepdims=True)
        rounded = jnp.concatenate([w.astype(jnp.bfloat16) for w in weights], axis=1)
        value = lax.dot_general(
            rounded, v_ref[head], (((1,), (0,)), ((), ())), preferred_element_type=jnp.float32
        )
        if with_own:
            nv = jnp.broadcast_to(
                nv_ref[head].astype(jnp.float32)[:, None, :], (tokens, per_group, size)
            ).reshape(head_rows, size)
            mine = jnp.exp2((own - top) * factor)
            total = total + mine
            value = value + mine * nv
        some = total > 0.0
        safe = jnp.where(some, total, 1.0)
        start = begin + order * head_rows
        out_ref[start : start + head_rows, :] = (value / safe).astype(jnp.bfloat16)
        level = jnp.where(some, top * factor + jnp.log2(safe), NEG_FILL)
        for part in range(head_rows // LANES):
            column = level[part * LANES : (part + 1) * LANES, :]
            index = order * (head_rows // LANES) + part
            stats = jnp.where(lane_id == index, column, stats)
    count = rows // LANES
    put_levels(out_ref, begin + rows, jnp.transpose(stats)[:count])
    for copy in copies:
        copy.wait()


def attend(packed, keep, keys, values, own, prev, weight, strips, rows_each, tokens, per_group):
    kv_heads, block_len, size = keys.shape
    rows = tokens * (kv_heads // 2) * per_group
    body = functools.partial(
        attend_kernel, tokens, keep, per_group, own is not None, prev is not None, strips
    )
    spec = pl.BlockSpec(memory_space=VMEM)
    operands = (packed, keys, values) + (own if own is not None else ())
    length = rows + stat_rows(rows)
    if prev is not None:
        operands += (prev,)
        length += prev.shape[0]
    in_specs = [spec] * len(operands)
    shapes = [jax.ShapeDtypeStruct((length, size), jnp.bfloat16)]
    scratch = [pltpu.VMEM((tokens * per_group, LANES), jnp.float32)]
    if strips:
        operands += (pltpu.with_memory_space_constraint(weight, HBM),)
        in_specs.append(pl.BlockSpec(memory_space=HBM))
        shapes += [jax.ShapeDtypeStruct((rows_each, weight.shape[1]), weight.dtype)] * len(strips)
        scratch.append(pltpu.SemaphoreType.DMA((len(strips) * STREAMS,)))
    return pl.pallas_call(
        body,
        out_shape=shapes,
        in_specs=in_specs,
        out_specs=[spec] * len(shapes),
        scratch_shapes=scratch,
        compiler_params=pltpu.CompilerParams(vmem_limit_bytes=12 * 1024 * 1024),
        cost_estimate=pl.CostEstimate(
            flops=4 * rows * block_len * size,
            bytes_accessed=2 * kv_heads * block_len * size,
            transcendentals=rows * block_len,
        ),
        name="attend",
    )(*operands)


def block_rows(heads, head_rows):
    return heads * head_rows + stat_rows(heads * head_rows)


def blend(refs, sources, heads, head_rows):
    lines = heads * head_rows // LANES
    levels = []
    for index, block, total, first in sources:
        base = block * block_rows(total, head_rows) + total * head_rows
        every = total * head_rows // LANES
        tail = refs[index][base : base + stat_rows(total * head_rows), :].astype(jnp.float32)
        level = tail[:every] + tail[every : 2 * every] + tail[2 * every : 3 * every]
        levels.append(level[first * head_rows // LANES : first * head_rows // LANES + lines])
    top = functools.reduce(jnp.maximum, levels)
    shares = [jnp.exp2(level - top) for level in levels]
    whole = functools.reduce(jnp.add, shares)
    shares = [share / whole for share in shares]
    blank = jnp.zeros((LANES - len(sources) * lines, LANES), jnp.float32)
    columns = jnp.transpose(jnp.concatenate(shares + [blank], axis=0))
    values = []
    for line in range(lines):
        value = None
        for order, (index, block, total, first) in enumerate(sources):
            start = block * block_rows(total, head_rows) + first * head_rows + line * LANES
            share = columns[:, order * lines + line : order * lines + line + 1]
            term = share * refs[index][start : start + LANES, :].astype(jnp.float32)
            value = term if value is None else value + term
        values.append(value)
    return values, top + jnp.log2(whole)


def combine_kernel(count, plan, head_rows, *refs):
    for out_ref, (heads, blocks) in zip(refs[count:], plan):
        begin = 0
        for sources in blocks:
            values, level = blend(refs, sources, heads, head_rows)
            for line, value in enumerate(values):
                start = begin + line * LANES
                out_ref[start : start + LANES, :] = value.astype(jnp.bfloat16)
            put_levels(out_ref, begin + heads * head_rows, level)
            begin += block_rows(heads, head_rows)


def combine(arrays, plan, head_rows):
    spec = pl.BlockSpec(memory_space=VMEM)
    size = arrays[0].shape[1]
    shapes = [
        jax.ShapeDtypeStruct((len(blocks) * block_rows(heads, head_rows), size), jnp.bfloat16)
        for heads, blocks in plan
    ]
    return pl.pallas_call(
        functools.partial(combine_kernel, len(arrays), plan, head_rows),
        out_shape=shapes,
        in_specs=[spec] * len(arrays),
        out_specs=[spec] * len(shapes),
        compiler_params=pltpu.CompilerParams(vmem_limit_bytes=8 * 1024 * 1024),
        cost_estimate=pl.CostEstimate(
            flops=4 * sum(array.size for array in arrays),
            bytes_accessed=2 * sum(array.size for array in arrays),
            transcendentals=0,
        ),
        name="combine",
    )(*arrays)


def merge_kernel(count, plan, tokens, per_group, *refs):
    out_ref, hold_ref = refs[count], refs[count + 1]
    head_rows = tokens * per_group
    for block, column, heads, sources in plan:
        values, _ = blend(refs, sources, heads, head_rows)
        for line, value in enumerate(values):
            hold_ref[line * LANES : (line + 1) * LANES, :] = value
        for member in range(heads * per_group):
            start = (column * per_group + member) * LANES
            row = member // per_group * head_rows + member % per_group
            out_ref[block * tokens : (block + 1) * tokens, start : start + LANES] = hold_ref[
                pl.ds(row, tokens, stride=per_group), :
            ].astype(jnp.bfloat16)


def merge(arrays, plan, tokens, heads, per_group):
    spec = pl.BlockSpec(memory_space=VMEM)
    return pl.pallas_call(
        functools.partial(merge_kernel, len(arrays), plan, tokens, per_group),
        out_shape=jax.ShapeDtypeStruct((2 * tokens, heads * per_group * LANES), jnp.bfloat16),
        in_specs=[spec] * len(arrays),
        out_specs=spec,
        scratch_shapes=[pltpu.VMEM((heads * tokens * per_group, LANES), jnp.float32)],
        compiler_params=pltpu.CompilerParams(vmem_limit_bytes=8 * 1024 * 1024),
        cost_estimate=pl.CostEstimate(
            flops=4 * sum(array.size for array in arrays),
            bytes_accessed=2 * sum(array.size for array in arrays),
            transcendentals=0,
        ),
        name="merge",
    )(*arrays)


def project_kernel(origins, tokens, strips, near, columns_from, with_sum, last, *refs):
    count = len(origins)
    blocks, w_refs = refs[:count], refs[count : count + strips]
    rest = refs[count + strips :]
    sum_ref = None
    if with_sum:
        sum_ref, rest = rest[0], rest[1:]
    left_ref = rest[-1]
    n_ctx, n_rep = lax.axis_size("ctx"), lax.axis_size("rep")
    spans = n_ctx // 2
    ctx, rep, side = (lax.axis_index(name).astype(jnp.int32) for name in ("ctx", "rep", "heads"))
    group_tokens, depth = left_ref.shape
    for (step, flip, turn, offset), block in zip(origins, blocks):
        column = pl.multiple_of(lax.rem(ctx + flip, 2) * (depth // 2), LANES)
        for order in range(2):
            source = lax.rem(lax.div(ctx, 2) + step, spans) * 2 + lax.rem(ctx + flip + order, 2)
            row = (source * n_rep + lax.rem(rep + turn, n_rep)) * tokens
            row = lax.rem(row - side * near + group_tokens, group_tokens)
            left_ref[pl.ds(pl.multiple_of(row, tokens), tokens), pl.ds(column, depth // 2)] = block[
                order * tokens : (order + 1) * tokens, offset : offset + depth // 2
            ]
    width = rest[0].shape[1]
    tile = min(256, width)
    strip = depth // strips
    for start in range(0, width, tile):
        result = None
        for index, w_ref in enumerate(w_refs):
            term = jnp.dot(
                left_ref[:, index * strip : (index + 1) * strip],
                w_ref[:, columns_from + start : columns_from + start + tile],
                preferred_element_type=jnp.float32,
            )
            result = term if result is None else result + term
        if with_sum:
            result = result + sum_ref[:, columns_from + start : columns_from + start + tile]
        if last:
            rest[0][:, start : start + tile] = result[:near]
            rest[1][:, start : start + tile] = result[near:].astype(jnp.bfloat16)
        else:
            rest[0][:, start : start + tile] = result


def project(origins, blocks, weights, partial_sum, tokens, total, near, columns, last):
    depth = sum(weight.shape[0] for weight in weights)
    width = columns[1] - columns[0]
    spec = pl.BlockSpec(memory_space=VMEM)
    if last:
        shapes = (
            jax.ShapeDtypeStruct((near, width), jnp.float32),
            jax.ShapeDtypeStruct((total - near, width), jnp.bfloat16),
        )
    else:
        shapes = (jax.ShapeDtypeStruct((total, width), jnp.float32),)
    operands = tuple(blocks) + tuple(weights) + (() if partial_sum is None else (partial_sum,))
    return pl.pallas_call(
        functools.partial(
            project_kernel,
            tuple(origins),
            tokens,
            len(weights),
            near,
            columns[0],
            partial_sum is not None,
            last,
        ),
        out_shape=shapes,
        in_specs=[spec] * len(operands),
        out_specs=tuple(spec for _ in shapes),
        scratch_shapes=[pltpu.VMEM((total, depth), jnp.bfloat16)],
        compiler_params=pltpu.CompilerParams(vmem_limit_bytes=8 * 1024 * 1024),
        cost_estimate=pl.CostEstimate(
            flops=2 * total * depth * width,
            bytes_accessed=2 * depth * width,
            transcendentals=0,
        ),
        name="project",
    )(*operands)


def after(value, *others):
    return lax.optimization_barrier((value,) + others)[0]


def moved(value, count, step, flip):
    spans = count // 2
    pairs = [
        (i, ((i // 2 + step) % spans) * 2 + (i % 2 + flip) % 2) for i in range(count)
    ]
    return lax.ppermute(value, "ctx", pairs)


def local(
    queries, cache_keys, cache_values, new_keys, new_values, positions, cached_length, out_weight
):
    tokens, local_heads, size = queries.shape
    kv_heads = cache_keys.shape[1]
    per_group = local_heads // kv_heads
    head_rows = tokens * per_group
    n_ctx = lax.axis_size("ctx")
    n_rep = lax.axis_size("rep")
    n_heads = lax.axis_size("heads")
    spans = n_ctx // 2
    half = kv_heads // 2
    units = 2 if half % 2 == 0 else 1
    per_unit = half // units

    packed = pack(queries, positions, cached_length)
    keys = cache_keys.transpose(1, 0, 2)
    values = cache_values.transpose(1, 0, 2)
    own = (new_keys.transpose(1, 0, 2), new_values.transpose(1, 0, 2))

    strips = 2 * kv_heads
    rows_each = out_weight.shape[0] // strips

    def strips_of(unit):
        found = []
        for owner in range(2):
            for head in range(unit * per_unit, (unit + 1) * per_unit):
                found += [2 * (owner * half + head), 2 * (owner * half + head) + 1]
        return found

    pending = [strip for unit in range(units) for strip in strips_of(unit)]
    in_attend = strips // 2
    loaded = {}

    def run(block, keep, mine=False, busy=True, prev=None):
        take = 0 if mine or busy or len(loaded) >= in_attend else 1
        wanted = tuple(pending.pop(0) for _ in range(take))
        made = attend(
            block,
            keep,
            keys,
            values,
            own if mine else None,
            prev,
            out_weight,
            wanted,
            rows_each,
            tokens,
            per_group,
        )
        loaded.update(zip(wanted, made[1:]))
        return made[0]

    near_q = moved(packed, n_ctx, 0, 1)
    cross_q = {j: moved(packed, n_ctx, -j, 0) for j in range(1, spans)}
    own_send = run(packed, False, mine=True)
    back_own = moved(own_send, n_ctx, 0, 1)
    own_keep = run(after(packed, own_send), True, mine=True)
    near_q = after(near_q, own_keep)
    pair_a = run(near_q, False)
    back_a = moved(pair_a, n_ctx, 0, 1)
    far_q = {}
    for j in range(1, spans):
        cross_q[j] = after(cross_q[j], pair_a)
        far_q[j] = moved(cross_q[j], n_ctx, 0, 1)
    p_keep = run(after(near_q, pair_a), True, busy=False)

    def source(index, block, total, first):
        return (index, block, total, first)

    def both(heads, unit):
        first = unit * heads
        return (
            (source(0, 0, half, first), source(2, 0, half, first)),
            (source(1, 0, half, first), source(3, 0, half, first)),
        )

    chunks = {}
    last = p_keep
    done_a = False
    for j in range(1, spans):
        c_send = run(after(cross_q[j], last), False, busy=False)
        back_c = moved(c_send, n_ctx, 0, 1)
        last = c_send
        if not done_a:
            done_a = True
            (made,) = combine(
                (own_keep, p_keep, after(back_a, last), back_own),
                ((half, both(half, 0)),),
                head_rows,
            )
            chunks[0] = [(made, half, unit * per_unit) for unit in range(units)]
            got_a = {s: moved(made, n_ctx, s, 0) for s in range(1, spans)}
            last = made
        block_f = after(far_q[j], last)
        pair_b = run(block_f, False)
        back_b = moved(pair_b, n_ctx, 0, 1)
        c_keep = run(after(cross_q[j], pair_b), True, busy=False)
        f_keep = run(after(block_f, c_keep), True, busy=False)
        made = combine(
            (c_keep, f_keep, after(back_b, f_keep), back_c),
            tuple((per_unit, both(per_unit, unit)) for unit in range(units)),
            head_rows,
        )
        chunks[j] = [(piece, per_unit, 0) for piece in made]
        last = made[0]
    if not done_a:
        (made,) = combine((own_keep, p_keep, back_a, back_own), ((half, both(half, 0)),), head_rows)
        chunks[0] = [(made, half, unit * per_unit) for unit in range(units)]
        got_a = {}
        last = made
    got = {}
    for s in range(1, spans):
        got[s, 0] = [(got_a[s], half, unit * per_unit) for unit in range(units)]
        for j in range(1, spans):
            got[s, j] = [
                (moved(piece, n_ctx, s, 0), total, first)
                for piece, total, first in chunks[j]
            ]

    def fetch(count, gate):
        wanted = tuple(pending.pop(0) for _ in range(min(count, len(pending))))
        if wanted:
            made = load(after(out_weight, gate), wanted, rows_each)
            loaded.update(zip(wanted, made))

    def merged(j, wanted):
        arrays, plan = [], []
        for column, unit in enumerate(wanted):
            for block in range(2):
                picked = []
                for piece, total, first in [chunks[j][unit]] + [
                    got[s, (j + s) % spans][unit] for s in range(1, spans)
                ]:
                    index = next((i for i, seen in enumerate(arrays) if seen is piece), len(arrays))
                    if index == len(arrays):
                        arrays.append(piece)
                    picked.append(source(index, block, total, first))
                plan.append((block, column * per_unit, per_unit, tuple(picked)))
        return merge(tuple(arrays), tuple(plan), tokens, per_unit * len(wanted), per_group)

    def spread(array):
        entries = []
        for flip, block in ((0, array), (1, moved(array, n_ctx, 0, 1))):
            for turn in range(n_rep):
                passed = block
                if turn:
                    passed = lax.ppermute(
                        block, "rep", [(i, (i - turn) % n_rep) for i in range(n_rep)]
                    )
                entries.append((flip, turn, passed))
        return entries

    depth = per_unit * per_group * size
    held = [[] for _ in range(units)]
    fetch(len(pending) // 2, last)
    for j in range(1, spans):
        array = merged(j, range(units))
        for flip, turn, passed in spread(array):
            for unit in range(units):
                held[unit].append(((j, flip, turn, unit * depth), passed))
    for unit in range(units):
        array = merged(0, (unit,))
        if unit == 0:
            fetch(len(pending), array)
        for flip, turn, passed in spread(array):
            held[unit].append(((0, flip, turn, 0), passed))

    total = n_ctx * n_rep * tokens
    near = total // n_heads
    width = out_weight.shape[1]
    so_far = None
    for unit in range(units - 1):
        so_far = project(
            [entry[0] for entry in held[unit]],
            [entry[1] for entry in held[unit]],
            [loaded[strip] for strip in strips_of(unit)],
            so_far,
            tokens,
            total,
            near,
            (0, width),
            False,
        )[0]
    pieces = 2 if width % (2 * LANES) == 0 else 1
    results = []
    for piece in range(pieces):
        columns = (piece * width // pieces, (piece + 1) * width // pieces)
        mine, others = project(
            [entry[0] for entry in held[-1]],
            [entry[1] for entry in held[-1]],
            [loaded[strip] for strip in strips_of(units - 1)],
            so_far,
            tokens,
            total,
            near,
            columns,
            True,
        )
        for step in range(1, n_heads):
            sent = others[(step - 1) * near : step * near]
            mine = mine + lax.ppermute(
                sent, "heads", [(i, (i + step) % n_heads) for i in range(n_heads)]
            ).astype(jnp.float32)
        results.append(mine.astype(jnp.bfloat16))
    return jnp.concatenate(results, axis=1)


def solution(mesh):
    return jax.shard_map(
        local,
        mesh=mesh,
        in_specs=(
            P(("groups", "ctx", "rep"), "heads", None),
            P(("groups", "ctx"), "heads", None),
            P(("groups", "ctx"), "heads", None),
            P(("groups", "ctx", "rep"), "heads", None),
            P(("groups", "ctx", "rep"), "heads", None),
            P(("groups", "ctx", "rep")),
            P("groups"),
            P("heads", ("ctx", "rep")),
        ),
        out_specs=P(("groups", "heads"), ("ctx", "rep")),
        check_vma=False,
    )
```

time: 87.1 us -> 88.7 us (1.018)
  starting transfers between devices: 35.6 us -> 17.8 us
  Pallas kernels: 27.9 us -> 38.4 us
  waiting for transfers between devices: 16.9 us -> 27.2 us
  other arithmetic: 2.68 us -> 0.77 us
    ppermute x15 -> x13, starting transfers between devices: 32.3 us -> 14.9 us  [moved(): return lax.ppermute(value, 'ctx', pairs)]
    ppermute x15 -> x13, waiting for transfers between devices: 11.6 us -> 21.9 us  [moved(): return lax.ppermute(value, 'ctx', pairs)]
    pallas_call x5 -> x11, Pallas kernels: 6.2 us -> 15.9 us  [the longest x2 6.95 us: load(): pl.pallas_call(functools.partial(load_kernel, strips), out_shape=[shape]...]
    concatenate x2 -> x0, other arithmetic: 1.23 us -> none  [the longest x1 1.15 us: local(): jnp.concatenate([queries.reshape(tokens * local_heads, size), marks], axi...]
  transfers between devices with their start and end apart: 25 -> 21, of which waited for: 8 -> 12; matrix products, arithmetic and copies ran while one was open for 3% -> 3% of each run, Pallas kernels for 31% -> 39%
where the time goes in v3:
time: 88.7 us; the launch traced here: 88.5 us
  Pallas kernels  38.4 us (43%)
  waiting for transfers between devices  27.2 us (31%)
  starting transfers between devices  17.8 us (20%)
  local copies, waits for them, and re-layouts  3.43 us (4%)
  between operations  0.91 us (1%)
    pallas_call x8, Pallas kernels, attend(): pl.pallas_call(body, out_shape=shapes, in_specs=in_specs, out_specs=[spec...  22.5 us
    ppermute x13, waiting for transfers between devices, moved(): return lax.ppermute(value, 'ctx', pairs)  21.9 us
    ppermute x13, starting transfers between devices, moved(): return lax.ppermute(value, 'ctx', pairs)  14.9 us
    pallas_call x2, Pallas kernels, load(): pl.pallas_call(functools.partial(load_kernel, strips), out_shape=[shape]...  6.95 us
    ppermute x2, waiting for transfers between devices, local(): lax.ppermute(sent, 'heads', [(i, (i + step) % n_heads) for i in range(n_h...  5.29 us
    pallas_call x3, Pallas kernels, project(): pl.pallas_call(functools.partial(project_kernel, tuple(origins), tokens,...  5.08 us
    transpose x1, local copies, waits for them, and re-layouts, local(): values = cache_values.transpose(1, 0, 2)  2.76 us
    ppermute x2, starting transfers between devices, local(): lax.ppermute(sent, 'heads', [(i, (i + step) % n_heads) for i in range(n_h...  2.16 us
  transfers between devices with their start and end apart: 21, of which 12 were waited for; matrix products, arithmetic and copies ran while one was open for 3% of the time, Pallas kernels for 39%

profile of v3, /device:TPU:0, one launch (start us, length us, event | category | flops | bytes accessed | tf_op | source)
XLA Modules:
  0.0 88.5 jit_solution(4322894105548698549)
XLA Ops:
  0.7 0.6 copy-done
  1.3 1.5 %pack.1.q_ref = bf16[1056,128]{1,0:T(8,128)(2,1)S(1)} custom-call(s32[16]{0:T(128)S(1)} %copy-done, s32[1]{0:T(128)S(6)} %copy.17.length_ref, bf16[1024,128]{1,0:T(8,128)(2,1)} %bitcast.9), custom_call_target="tpu_custom_call" | custom-call | tf_op jit(solution)/shard_map/pack/pallas_call | solution.py:98
  2.8 0.0 copy-start.1
  2.8 0.0 copy-start.2
  2.8 3.1 %collective-permute-start.1 = (bf16[1056,128]{1,0:T(8,128)(2,1)S(1)}, bf16[1056,128]{1,0:T(8,128)(2,1)S(1)}, u32[]{:S(2)}, u32[]{:S(2)}) collective-permute-start(bf16[1056,128]{1,0:T(8,128)(2,1)S(1)} %pack.1.q_ref), channel_id=1, source_target_pairs={{0,4},{4,0},{8,12},{12,8},{1,5},{5,1},{9,13},{13,9},{2,6},{6,2},{1... | collective-permute-start | bytes 811016 | tf_op jit(solution)/shard_map/ppermute | solution.py:426
  6.0 2.6 %collective-permute-start = (bf16[1056,128]{1,0:T(8,128)(2,1)S(1)}, bf16[1056,128]{1,0:T(8,128)(2,1)S(1)}, u32[]{:S(2)}, u32[]{:S(2)}) collective-permute-start(bf16[1056,128]{1,0:T(8,128)(2,1)S(1)} %pack.1.q_ref), channel_id=1, source_target_pairs={{0,8},{4,12},{8,0},{12,4},{1,9},{5,13},{9,1},{13,5},{2,10},{6,14},... | collective-permute-start | bytes 811016 | tf_op jit(solution)/shard_map/ppermute | solution.py:426
  8.5 2.8 %copy_bitcast_fusion = (bf16[4,2048,128]{2,1,0:T(8,128)(2,1)S(1)}, bf16[4,2048,128]{2,1,0:T(8,128)(2,1)S(1)}) fusion(bf16[2048,4,128]{2,1,0:T(4,128)(2,1)} %param.10, bf16[2048,4,128]{2,1,0:T(4,128)(2,1)} %param.9), kind=kLoop, calls=%fused_computation | loop fusion | bytes 8388608 | tf_op jit(solution)/shard_map/transpose | solution.py:446
  11.3 2.2 %attend.8 = bf16[528,128]{1,0:T(8,128)(2,1)S(1)} custom-call(bf16[1056,128]{1,0:T(8,128)(2,1)S(1)} %pack.1.q_ref, bf16[4,2048,128]{2,1,0:T(8,128)(2,1)S(1)} %get-tuple-element.66.k_ref, bf16[4,2048,128]{2,1,0:T(8,128)(2,1)S(1)} %get-tuple-element.65.v_ref, bf16[4,16,128]{2,1,0:T(8,128)(2,1)S(1)} %get-tuple-element.68.rest_0_, ...), custom_call_target="tpu_custom_call" | custom-call | flops 536870912 | bytes 2097152 | tf_op jit(solution)/shard_map/attend/pallas_call | solution.py:224
  13.6 2.2 %attend.9.refs_0_ = bf16[528,128]{1,0:T(8,128)(2,1)S(1)} custom-call(bf16[1056,128]{1,0:T(8,128)(2,1)S(1)} %pack.1.q_ref, bf16[4,2048,128]{2,1,0:T(8,128)(2,1)S(1)} %get-tuple-element.66.k_ref, bf16[4,2048,128]{2,1,0:T(8,128)(2,1)S(1)} %get-tuple-element.65.v_ref, bf16[4,16,128]{2,1,0:T(8,128)(2,1)S(1)} %get-tuple-element.68.rest_0_, ...), custom_call_target="tpu_custom_call" | custom-call | flops 536870912 | bytes 2097152 | tf_op jit(solution)/shard_map/attend/pallas_call | solution.py:224
  15.8 2.3 %collective-permute-done.1.q_ref = bf16[1056,128]{1,0:T(8,128)(2,1)S(1)} collective-permute-done((bf16[1056,128]{1,0:T(8,128)(2,1)S(1)}, bf16[1056,128]{1,0:T(8,128)(2,1)S(1)}, u32[]{:S(2)}, u32[]{:S(2)}) %collective-permute-start.1) | collective-permute-done | bytes 270368 | tf_op jit(solution)/shard_map/ppermute | solution.py:426
  18.1 2.1 %attend.10 = bf16[528,128]{1,0:T(8,128)(2,1)S(1)} custom-call(bf16[1056,128]{1,0:T(8,128)(2,1)S(1)} %collective-permute-done.1.q_ref, bf16[4,2048,128]{2,1,0:T(8,128)(2,1)S(1)} %get-tuple-element.66.k_ref, bf16[4,2048,128]{2,1,0:T(8,128)(2,1)S(1)} %get-tuple-element.65.v_ref), custom_call_target="tpu_custom_call" | custom-call | flops 536870912 | bytes 2097152 | tf_op jit(solution)/shard_map/attend/pallas_call | solution.py:224
  20.3 0.4 collective-permute-done.q_ref
  20.6 0.4 collective-permute-start.2
  21.1 1.6 %collective-permute-start.3 = (bf16[528,128]{1,0:T(8,128)(2,1)S(1)}, bf16[528,128]{1,0:T(8,128)(2,1)S(1)}, u32[]{:S(2)}, u32[]{:S(2)}) collective-permute-start(bf16[528,128]{1,0:T(8,128)(2,1)S(1)} %attend.10), channel_id=1, source_target_pairs={{0,4},{4,0},{8,12},{12,8},{1,5},{5,1},{9,13},{13,9},{2,6},{6,2},{1... | collective-permute-start | bytes 405512 | tf_op jit(solution)/shard_map/ppermute | solution.py:426
  22.7 0.4 collective-permute-start.4
  23.1 3.6 %attend.11 = (bf16[528,128]{1,0:T(8,128)(2,1)S(1)}, bf16[1024,2048]{1,0:T(8,128)(2,1)S(1)}) custom-call(bf16[1056,128]{1,0:T(8,128)(2,1)S(1)} %collective-permute-done.1.q_ref, bf16[4,2048,128]{2,1,0:T(8,128)(2,1)S(1)} %get-tuple-element.66.k_ref, bf16[4,2048,128]{2,1,0:T(8,128)(2,1)S(1)} %get-tuple-element.65.v_ref, bf16[8192,2048]{1,0:T(8,128)(2,1)} %w_ref.1), custom_call_target="tpu_custom_call" | custom-call | flops 536870912 | bytes 2097152 | tf_op jit(solution)/shard_map/attend/pallas_call | solution.py:224
  26.7 3.3 %attend.12 = (bf16[528,128]{1,0:T(8,128)(2,1)S(1)}, bf16[1024,2048]{1,0:T(8,128)(2,1)S(1)}) custom-call(bf16[1056,128]{1,0:T(8,128)(2,1)S(1)} %collective-permute-done.q_ref, bf16[4,2048,128]{2,1,0:T(8,128)(2,1)S(1)} %get-tuple-element.66.k_ref, bf16[4,2048,128]{2,1,0:T(8,128)(2,1)S(1)} %get-tuple-element.65.v_ref, bf16[8192,2048]{1,0:T(8,128)(2,1)} %w_ref.1), custom_call_target="tpu_custom_call" | custom-call | flops 536870912 | bytes 2097152 | tf_op jit(solution)/shard_map/attend/pallas_call | solution.py:224
  30.1 2.3 %collective-permute-done.3.refs_2_ = bf16[528,128]{1,0:T(8,128)(2,1)S(1)} collective-permute-done((bf16[528,128]{1,0:T(8,128)(2,1)S(1)}, bf16[528,128]{1,0:T(8,128)(2,1)S(1)}, u32[]{:S(2)}, u32[]{:S(2)}) %collective-permute-start.3) | collective-permute-done | bytes 135200 | tf_op jit(solution)/shard_map/ppermute | solution.py:426
  32.3 1.4 %collective-permute-done.4.refs_3_ = bf16[528,128]{1,0:T(8,128)(2,1)S(1)} collective-permute-done((bf16[528,128]{1,0:T(8,128)(2,1)S(1)}, bf16[528,128]{1,0:T(8,128)(2,1)S(1)}, u32[]{:S(2)}, u32[]{:S(2)}) %collective-permute-start.4) | collective-permute-done | bytes 135200 | tf_op jit(solution)/shard_map/ppermute | solution.py:426
  33.8 0.5 combine.2.refs_0_
  34.2 1.3 %collective-permute-start.7 = (bf16[1056,128]{1,0:T(8,128)(2,1)S(1)}, bf16[1056,128]{1,0:T(8,128)(2,1)S(1)}, u32[]{:S(2)}, u32[]{:S(2)}) collective-permute-start(bf16[1056,128]{1,0:T(8,128)(2,1)S(1)} %combine.2.refs_0_), channel_id=1, source_target_pairs={{0,8},{4,12},{8,0},{12,4},{1,9},{5,13},{9,1},{13,5},{2,10},{6,14},... | collective-permute-start | bytes 811016 | tf_op jit(solution)/shard_map/ppermute | solution.py:426
  35.5 0.0 collective-permute-done.2.q_ref
  35.5 2.3 %attend.13 = bf16[528,128]{1,0:T(8,128)(2,1)S(1)} custom-call(bf16[1056,128]{1,0:T(8,128)(2,1)S(1)} %collective-permute-done.2.q_ref, bf16[4,2048,128]{2,1,0:T(8,128)(2,1)S(1)} %get-tuple-element.66.k_ref, bf16[4,2048,128]{2,1,0:T(8,128)(2,1)S(1)} %get-tuple-element.65.v_ref), custom_call_target="tpu_custom_call" | custom-call | flops 536870912 | bytes 2097152 | tf_op jit(solution)/shard_map/attend/pallas_call | solution.py:224
  37.8 1.8 %collective-permute-start.5 = (bf16[528,128]{1,0:T(8,128)(2,1)S(1)}, bf16[528,128]{1,0:T(8,128)(2,1)S(1)}, u32[]{:S(2)}, u32[]{:S(2)}) collective-permute-start(bf16[528,128]{1,0:T(8,128)(2,1)S(1)} %attend.13), channel_id=1, source_target_pairs={{0,4},{4,0},{8,12},{12,8},{1,5},{5,1},{9,13},{13,9},{2,6},{6,2},{1... | collective-permute-start | bytes 405512 | tf_op jit(solution)/shard_map/ppermute | solution.py:426
  39.6 0.3 collective-permute-start.6
  39.9 3.3 %attend.14 = (bf16[528,128]{1,0:T(8,128)(2,1)S(1)}, bf16[1024,2048]{1,0:T(8,128)(2,1)S(1)}) custom-call(bf16[1056,128]{1,0:T(8,128)(2,1)S(1)} %collective-permute-done.q_ref, bf16[4,2048,128]{2,1,0:T(8,128)(2,1)S(1)} %get-tuple-element.66.k_ref, bf16[4,2048,128]{2,1,0:T(8,128)(2,1)S(1)} %get-tuple-element.65.v_ref, bf16[8192,2048]{1,0:T(8,128)(2,1)} %w_ref.1), custom_call_target="tpu_custom_call" | custom-call | flops 536870912 | bytes 2097152 | tf_op jit(solution)/shard_map/attend/pallas_call | solution.py:224
  43.2 3.3 %attend.15 = (bf16[528,128]{1,0:T(8,128)(2,1)S(1)}, bf16[1024,2048]{1,0:T(8,128)(2,1)S(1)}) custom-call(bf16[1056,128]{1,0:T(8,128)(2,1)S(1)} %collective-permute-done.2.q_ref, bf16[4,2048,128]{2,1,0:T(8,128)(2,1)S(1)} %get-tuple-element.66.k_ref, bf16[4,2048,128]{2,1,0:T(8,128)(2,1)S(1)} %get-tuple-element.65.v_ref, bf16[8192,2048]{1,0:T(8,128)(2,1)} %w_ref.1), custom_call_target="tpu_custom_call" | custom-call | flops 536870912 | bytes 2097152 | tf_op jit(solution)/shard_map/attend/pallas_call | solution.py:224
  46.6 1.9 %collective-permute-done.5.refs_2_ = bf16[528,128]{1,0:T(8,128)(2,1)S(1)} collective-permute-done((bf16[528,128]{1,0:T(8,128)(2,1)S(1)}, bf16[528,128]{1,0:T(8,128)(2,1)S(1)}, u32[]{:S(2)}, u32[]{:S(2)}) %collective-permute-start.5) | collective-permute-done | bytes 135200 | tf_op jit(solution)/shard_map/ppermute | solution.py:426
  48.5 1.4 %collective-permute-done.6.refs_3_ = bf16[528,128]{1,0:T(8,128)(2,1)S(1)} collective-permute-done((bf16[528,128]{1,0:T(8,128)(2,1)S(1)}, bf16[528,128]{1,0:T(8,128)(2,1)S(1)}, u32[]{:S(2)}, u32[]{:S(2)}) %collective-permute-start.6) | collective-permute-done | bytes 135200 | tf_op jit(solution)/shard_map/ppermute | solution.py:426
  50.0 0.6 combine.3
  50.5 0.0 collective-permute-done.7.refs_1_
  50.5 0.6 merge.3.refs_0_
  51.2 0.1 collective-permute-start.9
  51.2 1.9 %collective-permute-start.15 = (bf16[544,128]{1,0:T(8,128)(2,1)S(1)}, bf16[544,128]{1,0:T(8,128)(2,1)S(1)}, u32[]{:S(2)}, u32[]{:S(2)}) collective-permute-start(bf16[544,128]{1,0:T(8,128)(2,1)S(1)} %get-tuple-element.49.refs_0_), channel_id=1, source_target_pairs={{0,8},{4,12},{8,0},{12,4},{1,9},{5,13},{9,1},{13,5},{2,10},{6,14},... | collective-permute-start | bytes 417800 | tf_op jit(solution)/shard_map/ppermute | solution.py:426
  53.2 1.1 %collective-permute-start.11 = (bf16[544,128]{1,0:T(8,128)(2,1)S(1)}, bf16[544,128]{1,0:T(8,128)(2,1)S(1)}, u32[]{:S(2)}, u32[]{:S(2)}) collective-permute-start(bf16[544,128]{1,0:T(8,128)(2,1)S(1)} %get-tuple-element.50.refs_2_), channel_id=1, source_target_pairs={{0,8},{4,12},{8,0},{12,4},{1,9},{5,13},{9,1},{13,5},{2,10},{6,14},... | collective-permute-start | bytes 417800 | tf_op jit(solution)/shard_map/ppermute | solution.py:426
  54.2 0.0 collective-permute-start.8
  54.2 7.9 %collective-permute-done.15.refs_1_ = bf16[544,128]{1,0:T(8,128)(2,1)S(1)} collective-permute-done((bf16[544,128]{1,0:T(8,128)(2,1)S(1)}, bf16[544,128]{1,0:T(8,128)(2,1)S(1)}, u32[]{:S(2)}, u32[]{:S(2)}) %collective-permute-start.15) | collective-permute-done | bytes 139296 | tf_op jit(solution)/shard_map/ppermute | solution.py:426
  62.1 0.3 merge.5.refs_4_
  62.4 0.2 collective-permute-start.17
  62.6 1.7 %collective-permute-done.9.refs_2_ = bf16[32,4096]{1,0:T(8,128)(2,1)S(1)} collective-permute-done((bf16[32,4096]{1,0:T(8,128)(2,1)S(1)}, bf16[32,4096]{1,0:T(8,128)(2,1)S(1)}, u32[]{:S(2)}, u32[]{:S(2)}) %collective-permute-start.9) | collective-permute-done | bytes 262176 | tf_op jit(solution)/shard_map/ppermute | solution.py:426
  64.3 0.0 collective-permute-start.10
  64.3 0.6 collective-permute-done.11.refs_1_
  64.9 0.3 merge.4.refs_4_
  65.2 0.1 collective-permute-start.13
  65.4 0.0 collective-permute-start.16
  65.4 2.1 %collective-permute-done.17.refs_6_ = bf16[32,2048]{1,0:T(8,128)(2,1)S(1)} collective-permute-done((bf16[32,2048]{1,0:T(8,128)(2,1)S(1)}, bf16[32,2048]{1,0:T(8,128)(2,1)S(1)}, u32[]{:S(2)}, u32[]{:S(2)}) %collective-permute-start.17) | collective-permute-done | bytes 131104 | tf_op jit(solution)/shard_map/ppermute | solution.py:426
  67.5 0.0 collective-permute-start.18
  67.5 3.5 %load.2 = (bf16[1024,2048]{1,0:T(8,128)(2,1)S(1)}, bf16[1024,2048]{1,0:T(8,128)(2,1)S(1)}) custom-call(bf16[8192,2048]{1,0:T(8,128)(2,1)} %w_ref.1), custom_call_target="tpu_custom_call" | custom-call | bytes 8388608 | tf_op jit(solution)/shard_map/load/pallas_call | solution.py:55
  71.0 3.5 %load.3 = (bf16[1024,2048]{1,0:T(8,128)(2,1)S(1)}, bf16[1024,2048]{1,0:T(8,128)(2,1)S(1)}) custom-call(bf16[8192,2048]{1,0:T(8,128)(2,1)} %w_ref.1), custom_call_target="tpu_custom_call" | custom-call | bytes 8388608 | tf_op jit(solution)/shard_map/load/pallas_call | solution.py:55
  74.4 0.0 collective-permute-done.8.refs_1_
  74.5 0.6 collective-permute-start.12
  75.0 0.1 collective-permute-start.14
  75.1 0.0 collective-permute-done.18.refs_7_
  75.1 0.0 collective-permute-done.10.refs_3_
  75.1 2.4 %project.3.refs_12_ = f32[128,2048]{1,0:T(8,128)S(1)} custom-call(bf16[32,4096]{1,0:T(8,128)(2,1)S(1)} %merge.3.refs_0_, bf16[32,4096]{1,0:T(8,128)(2,1)S(1)} %collective-permute-done.8.refs_1_, bf16[32,4096]{1,0:T(8,128)(2,1)S(1)} %collective-permute-done.9.refs_2_, bf16[32,4096]{1,0:T(8,128)(2,1)S(1)} %collective-permute-done.10.refs_3_, ...), custom_call_target="tpu_custom_call" | custom-call | flops 2147483648 | bytes 16777216 | tf_op jit(solution)/shard_map/project/pallas_call | solution.py:392
  77.5 0.0 collective-permute-done.12.refs_5_
  77.6 0.0 collective-permute-done.14.refs_7_
  77.6 1.3 %project.4 = (f32[64,1024]{1,0:T(8,128)S(1)}, bf16[64,1024]{1,0:T(8,128)(2,1)S(1)}) custom-call(bf16[32,4096]{1,0:T(8,128)(2,1)S(1)} %merge.3.refs_0_, bf16[32,4096]{1,0:T(8,128)(2,1)S(1)} %collective-permute-done.8.refs_1_, bf16[32,4096]{1,0:T(8,128)(2,1)S(1)} %collective-permute-done.9.refs_2_, bf16[32,4096]{1,0:T(8,128)(2,1)S(1)} %collective-permute-done.10.refs_3_, ...), custom_call_target="tpu_custom_call" | custom-call | flops 1073741824 | bytes 8388608 | tf_op jit(solution)/shard_map/project/pallas_call | solution.py:392
  78.9 1.9 %collective-permute-start.19 = (bf16[64,1024]{1,0:T(8,128)(2,1)S(1)}, bf16[64,1024]{1,0:T(8,128)(2,1)S(1)}, u32[]{:S(2)}, u32[]{:S(2)}) collective-permute-start(bf16[64,1024]{1,0:T(8,128)(2,1)S(1)} %get-tuple-element.62), channel_id=1, source_target_pairs={{0,2},{2,0},{1,3},{3,1},{4,6},{6,4},{5,7},{7,5},{8,10},{10,8},{9,1... | collective-permute-start | bytes 393224 | tf_op jit(solution)/shard_map/ppermute | solution.py:630
  80.8 1.3 %project.5 = (f32[64,1024]{1,0:T(8,128)S(1)}, bf16[64,1024]{1,0:T(8,128)(2,1)S(1)}) custom-call(bf16[32,4096]{1,0:T(8,128)(2,1)S(1)} %merge.3.refs_0_, bf16[32,4096]{1,0:T(8,128)(2,1)S(1)} %collective-permute-done.8.refs_1_, bf16[32,4096]{1,0:T(8,128)(2,1)S(1)} %collective-permute-done.9.refs_2_, bf16[32,4096]{1,0:T(8,128)(2,1)S(1)} %collective-permute-done.10.refs_3_, ...), custom_call_target="tpu_custom_call" | custom-call | flops 1073741824 | bytes 8388608 | tf_op jit(solution)/shard_map/project/pallas_call | solution.py:392
  82.1 0.3 collective-permute-start.20
  82.4 2.5 %collective-permute-done.19 = bf16[64,1024]{1,0:T(8,128)(2,1)S(1)} collective-permute-done((bf16[64,1024]{1,0:T(8,128)(2,1)S(1)}, bf16[64,1024]{1,0:T(8,128)(2,1)S(1)}, u32[]{:S(2)}, u32[]{:S(2)}) %collective-permute-start.19) | collective-permute-done | bytes 131104 | tf_op jit(solution)/shard_map/ppermute | solution.py:630
  84.9 2.8 %collective-permute-done.20 = bf16[64,1024]{1,0:T(8,128)(2,1)S(1)} collective-permute-done((bf16[64,1024]{1,0:T(8,128)(2,1)S(1)}, bf16[64,1024]{1,0:T(8,128)(2,1)S(1)}, u32[]{:S(2)}, u32[]{:S(2)}) %collective-permute-start.20) | collective-permute-done | bytes 131104 | tf_op jit(solution)/shard_map/ppermute | solution.py:630
  87.8 0.7 pad_maximum_fusion
  (8 shorter events, 0.1 us)
Async XLA Ops:
  0.7 0.7 copy-start
  2.8 8.5 %copy-start.1 = (bf16[16,4,128]{2,1,0:T(4,128)(2,1)S(1)}, bf16[16,4,128]{2,1,0:T(4,128)(2,1)}, u32[]{:S(2)}) copy-start(bf16[16,4,128]{2,1,0:T(4,128)(2,1)} %param.12) | copy-start | bytes 49156
  2.8 8.5 %copy-start.2 = (bf16[16,4,128]{2,1,0:T(4,128)(2,1)S(1)}, bf16[16,4,128]{2,1,0:T(4,128)(2,1)}, u32[]{:S(2)}) copy-start(bf16[16,4,128]{2,1,0:T(4,128)(2,1)} %param.11) | copy-start | bytes 49156
  2.8 15.3 %collective-permute-start.1 = (bf16[1056,128]{1,0:T(8,128)(2,1)S(1)}, bf16[1056,128]{1,0:T(8,128)(2,1)S(1)}, u32[]{:S(2)}, u32[]{:S(2)}) collective-permute-start(bf16[1056,128]{1,0:T(8,128)(2,1)S(1)} %pack.1.q_ref), channel_id=1, source_target_pairs={{0,4},{4,0},{8,12},{12,8},{1,5},{5,1},{9,13},{13,9},{2,6},{6,2},{1... | collective-permute-start | bytes 811016 | tf_op jit(solution)/shard_map/ppermute | solution.py:426
  6.0 14.7 %collective-permute-start = (bf16[1056,128]{1,0:T(8,128)(2,1)S(1)}, bf16[1056,128]{1,0:T(8,128)(2,1)S(1)}, u32[]{:S(2)}, u32[]{:S(2)}) collective-permute-start(bf16[1056,128]{1,0:T(8,128)(2,1)S(1)} %pack.1.q_ref), channel_id=1, source_target_pairs={{0,8},{4,12},{8,0},{12,4},{1,9},{5,13},{9,1},{13,5},{2,10},{6,14},... | collective-permute-start | bytes 811016 | tf_op jit(solution)/shard_map/ppermute | solution.py:426
  20.6 14.9 %collective-permute-start.2 = (bf16[1056,128]{1,0:T(8,128)(2,1)S(1)}, bf16[1056,128]{1,0:T(8,128)(2,1)S(1)}, u32[]{:S(2)}, u32[]{:S(2)}) collective-permute-start(bf16[1056,128]{1,0:T(8,128)(2,1)S(1)} %collective-permute-done.q_ref), channel_id=1, source_target_pairs={{0,4},{4,0},{8,12},{12,8},{1,5},{5,1},{9,13},{13,9},{2,6},{6,2},{1... | collective-permute-start | bytes 811016 | tf_op jit(solution)/shard_map/ppermute | solution.py:426
  21.1 11.2 %collective-permute-start.3 = (bf16[528,128]{1,0:T(8,128)(2,1)S(1)}, bf16[528,128]{1,0:T(8,128)(2,1)S(1)}, u32[]{:S(2)}, u32[]{:S(2)}) collective-permute-start(bf16[528,128]{1,0:T(8,128)(2,1)S(1)} %attend.10), channel_id=1, source_target_pairs={{0,4},{4,0},{8,12},{12,8},{1,5},{5,1},{9,13},{13,9},{2,6},{6,2},{1... | collective-permute-start | bytes 405512 | tf_op jit(solution)/shard_map/ppermute | solution.py:426
  22.7 11.1 %collective-permute-start.4 = (bf16[528,128]{1,0:T(8,128)(2,1)S(1)}, bf16[528,128]{1,0:T(8,128)(2,1)S(1)}, u32[]{:S(2)}, u32[]{:S(2)}) collective-permute-start(bf16[528,128]{1,0:T(8,128)(2,1)S(1)} %attend.8), channel_id=1, source_target_pairs={{0,4},{4,0},{8,12},{12,8},{1,5},{5,1},{9,13},{13,9},{2,6},{6,2},{1... | collective-permute-start | bytes 405512 | tf_op jit(solution)/shard_map/ppermute | solution.py:426
  34.2 16.3 %collective-permute-start.7 = (bf16[1056,128]{1,0:T(8,128)(2,1)S(1)}, bf16[1056,128]{1,0:T(8,128)(2,1)S(1)}, u32[]{:S(2)}, u32[]{:S(2)}) collective-permute-start(bf16[1056,128]{1,0:T(8,128)(2,1)S(1)} %combine.2.refs_0_), channel_id=1, source_target_pairs={{0,8},{4,12},{8,0},{12,4},{1,9},{5,13},{9,1},{13,5},{2,10},{6,14},... | collective-permute-start | bytes 811016 | tf_op jit(solution)/shard_map/ppermute | solution.py:426
  37.8 10.7 %collective-permute-start.5 = (bf16[528,128]{1,0:T(8,128)(2,1)S(1)}, bf16[528,128]{1,0:T(8,128)(2,1)S(1)}, u32[]{:S(2)}, u32[]{:S(2)}) collective-permute-start(bf16[528,128]{1,0:T(8,128)(2,1)S(1)} %attend.13), channel_id=1, source_target_pairs={{0,4},{4,0},{8,12},{12,8},{1,5},{5,1},{9,13},{13,9},{2,6},{6,2},{1... | collective-permute-start | bytes 405512 | tf_op jit(solution)/shard_map/ppermute | solution.py:426
  39.6 10.3 %collective-permute-start.6 = (bf16[528,128]{1,0:T(8,128)(2,1)S(1)}, bf16[528,128]{1,0:T(8,128)(2,1)S(1)}, u32[]{:S(2)}, u32[]{:S(2)}) collective-permute-start(bf16[528,128]{1,0:T(8,128)(2,1)S(1)} %get-tuple-element.41), channel_id=1, source_target_pairs={{0,4},{4,0},{8,12},{12,8},{1,5},{5,1},{9,13},{13,9},{2,6},{6,2},{1... | collective-permute-start | bytes 405512 | tf_op jit(solution)/shard_map/ppermute | solution.py:426
  51.2 13.2 %collective-permute-start.9 = (bf16[32,4096]{1,0:T(8,128)(2,1)S(1)}, bf16[32,4096]{1,0:T(8,128)(2,1)S(1)}, u32[]{:S(2)}, u32[]{:S(2)}) collective-permute-start(bf16[32,4096]{1,0:T(8,128)(2,1)S(1)} %merge.3.refs_0_), channel_id=1, source_target_pairs={{0,4},{4,0},{8,12},{12,8},{1,5},{5,1},{9,13},{13,9},{2,6},{6,2},{1... | collective-permute-start | bytes 786440 | tf_op jit(solution)/shard_map/ppermute | solution.py:426
  51.2 10.9 %collective-permute-start.15 = (bf16[544,128]{1,0:T(8,128)(2,1)S(1)}, bf16[544,128]{1,0:T(8,128)(2,1)S(1)}, u32[]{:S(2)}, u32[]{:S(2)}) collective-permute-start(bf16[544,128]{1,0:T(8,128)(2,1)S(1)} %get-tuple-element.49.refs_0_), channel_id=1, source_target_pairs={{0,8},{4,12},{8,0},{12,4},{1,9},{5,13},{9,1},{13,5},{2,10},{6,14},... | collective-permute-start | bytes 417800 | tf_op jit(solution)/shard_map/ppermute | solution.py:426
  53.2 11.7 %collective-permute-start.11 = (bf16[544,128]{1,0:T(8,128)(2,1)S(1)}, bf16[544,128]{1,0:T(8,128)(2,1)S(1)}, u32[]{:S(2)}, u32[]{:S(2)}) collective-permute-start(bf16[544,128]{1,0:T(8,128)(2,1)S(1)} %get-tuple-element.50.refs_2_), channel_id=1, source_target_pairs={{0,8},{4,12},{8,0},{12,4},{1,9},{5,13},{9,1},{13,5},{2,10},{6,14},... | collective-permute-start | bytes 417800 | tf_op jit(solution)/shard_map/ppermute | solution.py:426
  54.2 20.2 %collective-permute-start.8 = (bf16[32,4096]{1,0:T(8,128)(2,1)S(1)}, bf16[32,4096]{1,0:T(8,128)(2,1)S(1)}, u32[]{:S(2)}, u32[]{:S(2)}) collective-permute-start(bf16[32,4096]{1,0:T(8,128)(2,1)S(1)} %merge.3.refs_0_), channel_id=1, source_target_pairs={{0,1},{1,0},{2,3},{3,2},{4,5},{5,4},{6,7},{7,6},{8,9},{9,8},{10,11... | collective-permute-start | bytes 786440 | tf_op jit(solution)/shard_map/ppermute | solution.py:576
  62.4 5.0 %collective-permute-start.17 = (bf16[32,2048]{1,0:T(8,128)(2,1)S(1)}, bf16[32,2048]{1,0:T(8,128)(2,1)S(1)}, u32[]{:S(2)}, u32[]{:S(2)}) collective-permute-start(bf16[32,2048]{1,0:T(8,128)(2,1)S(1)} %merge.5.refs_4_), channel_id=1, source_target_pairs={{0,4},{4,0},{8,12},{12,8},{1,5},{5,1},{9,13},{13,9},{2,6},{6,2},{1... | collective-permute-start | bytes 393224 | tf_op jit(solution)/shard_map/ppermute | solution.py:426
  64.3 10.8 %collective-permute-start.10 = (bf16[32,4096]{1,0:T(8,128)(2,1)S(1)}, bf16[32,4096]{1,0:T(8,128)(2,1)S(1)}, u32[]{:S(2)}, u32[]{:S(2)}) collective-permute-start(bf16[32,4096]{1,0:T(8,128)(2,1)S(1)} %collective-permute-done.9.refs_2_), channel_id=1, source_target_pairs={{0,1},{1,0},{2,3},{3,2},{4,5},{5,4},{6,7},{7,6},{8,9},{9,8},{10,11... | collective-permute-start | bytes 786440 | tf_op jit(solution)/shard_map/ppermute | solution.py:576
  65.2 9.8 %collective-permute-start.13 = (bf16[32,2048]{1,0:T(8,128)(2,1)S(1)}, bf16[32,2048]{1,0:T(8,128)(2,1)S(1)}, u32[]{:S(2)}, u32[]{:S(2)}) collective-permute-start(bf16[32,2048]{1,0:T(8,128)(2,1)S(1)} %merge.4.refs_4_), channel_id=1, source_target_pairs={{0,4},{4,0},{8,12},{12,8},{1,5},{5,1},{9,13},{13,9},{2,6},{6,2},{1... | collective-permute-start | bytes 393224 | tf_op jit(solution)/shard_map/ppermute | solution.py:426
  65.4 9.7 %collective-permute-start.16 = (bf16[32,2048]{1,0:T(8,128)(2,1)S(1)}, bf16[32,2048]{1,0:T(8,128)(2,1)S(1)}, u32[]{:S(2)}, u32[]{:S(2)}) collective-permute-start(bf16[32,2048]{1,0:T(8,128)(2,1)S(1)} %merge.5.refs_4_), channel_id=1, source_target_pairs={{0,1},{1,0},{2,3},{3,2},{4,5},{5,4},{6,7},{7,6},{8,9},{9,8},{10,11... | collective-permute-start | bytes 393224 | tf_op jit(solution)/shard_map/ppermute | solution.py:576
  67.5 7.6 %collective-permute-start.18 = (bf16[32,2048]{1,0:T(8,128)(2,1)S(1)}, bf16[32,2048]{1,0:T(8,128)(2,1)S(1)}, u32[]{:S(2)}, u32[]{:S(2)}) collective-permute-start(bf16[32,2048]{1,0:T(8,128)(2,1)S(1)} %collective-permute-done.17.refs_6_), channel_id=1, source_target_pairs={{0,1},{1,0},{2,3},{3,2},{4,5},{5,4},{6,7},{7,6},{8,9},{9,8},{10,11... | collective-permute-start | bytes 393224 | tf_op jit(solution)/shard_map/ppermute | solution.py:576
  74.5 3.1 %collective-permute-start.12 = (bf16[32,2048]{1,0:T(8,128)(2,1)S(1)}, bf16[32,2048]{1,0:T(8,128)(2,1)S(1)}, u32[]{:S(2)}, u32[]{:S(2)}) collective-permute-start(bf16[32,2048]{1,0:T(8,128)(2,1)S(1)} %merge.4.refs_4_), channel_id=1, source_target_pairs={{0,1},{1,0},{2,3},{3,2},{4,5},{5,4},{6,7},{7,6},{8,9},{9,8},{10,11... | collective-permute-start | bytes 393224 | tf_op jit(solution)/shard_map/ppermute | solution.py:576
  75.0 2.5 %collective-permute-start.14 = (bf16[32,2048]{1,0:T(8,128)(2,1)S(1)}, bf16[32,2048]{1,0:T(8,128)(2,1)S(1)}, u32[]{:S(2)}, u32[]{:S(2)}) collective-permute-start(bf16[32,2048]{1,0:T(8,128)(2,1)S(1)} %collective-permute-done.13.refs_6_), channel_id=1, source_target_pairs={{0,1},{1,0},{2,3},{3,2},{4,5},{5,4},{6,7},{7,6},{8,9},{9,8},{10,11... | collective-permute-start | bytes 393224 | tf_op jit(solution)/shard_map/ppermute | solution.py:576
  78.9 5.9 %collective-permute-start.19 = (bf16[64,1024]{1,0:T(8,128)(2,1)S(1)}, bf16[64,1024]{1,0:T(8,128)(2,1)S(1)}, u32[]{:S(2)}, u32[]{:S(2)}) collective-permute-start(bf16[64,1024]{1,0:T(8,128)(2,1)S(1)} %get-tuple-element.62), channel_id=1, source_target_pairs={{0,2},{2,0},{1,3},{3,1},{4,6},{6,4},{5,7},{7,5},{8,10},{10,8},{9,1... | collective-permute-start | bytes 393224 | tf_op jit(solution)/shard_map/ppermute | solution.py:630
  82.1 5.6 %collective-permute-start.20 = (bf16[64,1024]{1,0:T(8,128)(2,1)S(1)}, bf16[64,1024]{1,0:T(8,128)(2,1)S(1)}, u32[]{:S(2)}, u32[]{:S(2)}) collective-permute-start(bf16[64,1024]{1,0:T(8,128)(2,1)S(1)} %get-tuple-element.64), channel_id=1, source_target_pairs={{0,2},{2,0},{1,3},{3,1},{4,6},{6,4},{5,7},{7,5},{8,10},{10,8},{9,1... | collective-permute-start | bytes 393224 | tf_op jit(solution)/shard_map/ppermute | solution.py:630

commit v4 on v3

--- a/solution.py
+++ b/solution.py
@@ -457,11 +457,11 @@
         return found
 
     pending = [strip for unit in range(units) for strip in strips_of(unit)]
-    in_attend = strips // 2
+    in_attend = min(3, strips // 2)
     loaded = {}
 
     def run(block, keep, mine=False, busy=True, prev=None):
-        take = 0 if mine or busy or len(loaded) >= in_attend else 1
+        take = 0 if busy or len(loaded) >= in_attend else 1
         wanted = tuple(pending.pop(0) for _ in range(take))
         made = attend(
             block,
@@ -483,7 +483,7 @@
     cross_q = {j: moved(packed, n_ctx, -j, 0) for j in range(1, spans)}
     own_send = run(packed, False, mine=True)
     back_own = moved(own_send, n_ctx, 0, 1)
-    own_keep = run(after(packed, own_send), True, mine=True)
+    own_keep = run(after(packed, own_send), True, mine=True, busy=False)
     near_q = after(near_q, own_keep)
     pair_a = run(near_q, False)
     back_a = moved(pair_a, n_ctx, 0, 1)
@@ -491,7 +491,7 @@
     for j in range(1, spans):
         cross_q[j] = after(cross_q[j], pair_a)
         far_q[j] = moved(cross_q[j], n_ctx, 0, 1)
-    p_keep = run(after(near_q, pair_a), True, busy=False)
+    p_keep = run(after(near_q, pair_a), True)
 
     def source(index, block, total, first):
         return (index, block, total, first)
@@ -507,7 +507,7 @@
     last = p_keep
     done_a = False
     for j in range(1, spans):
-        c_send = run(after(cross_q[j], last), False, busy=False)
+        c_send = run(after(cross_q[j], last), False)
         back_c = moved(c_send, n_ctx, 0, 1)
         last = c_send
         if not done_a:
@@ -581,7 +581,7 @@
 
     depth = per_unit * per_group * size
     held = [[] for _ in range(units)]
-    fetch(len(pending) // 2, last)
+    fetch(2 if units > 1 else len(pending), last)
     for j in range(1, spans):
         array = merged(j, range(units))
         for flip, turn, passed in spread(array):
@@ -590,7 +590,7 @@
     for unit in range(units):
         array = merged(0, (unit,))
         if unit == 0:
-            fetch(len(pending), array)
+            fetch(2, array)
         for flip, turn, passed in spread(array):
             held[unit].append(((0, flip, turn, 0), passed))
 
@@ -610,10 +610,13 @@
             (0, width),
             False,
         )[0]
+        fetch(len(pending), so_far)
     pieces = 2 if width % (2 * LANES) == 0 else 1
+    first = width * 3 // 8 // 256 * 256 or width // 2
+    edges = (0, first, width) if pieces == 2 else (0, width)
     results = []
     for piece in range(pieces):
-        columns = (piece * width // pieces, (piece + 1) * width // pieces)
+        columns = (edges[piece], edges[piece + 1])
         mine, others = project(
             [entry[0] for entry in held[-1]],
             [entry[1] for entry in held[-1]],

time: 88.7 us -> 91.8 us (1.035)
  waiting for transfers between devices: 27.2 us -> 29.2 us
  Pallas kernels: 38.4 us -> 39.6 us
    pallas_call x2 -> x3, Pallas kernels: 6.95 us -> 9.16 us  [load(): pl.pallas_call(functools.partial(load_kernel, strips), out_shape=[shape]...]
    ppermute x13, waiting for transfers between devices: 21.9 us -> 23.1 us  [moved(): return lax.ppermute(value, 'ctx', pairs)]
    pallas_call x8, Pallas kernels: 22.5 us -> 21.5 us  [attend(): pl.pallas_call(body, out_shape=shapes, in_specs=in_specs, out_specs=[spec...]
  transfers between devices with their start and end apart: 21 -> 21, of which waited for: 12 -> 12; matrix products, arithmetic and copies ran while one was open for 3% -> 3% of each run, Pallas kernels for 39% -> 40%
where the time goes in v4:
time: 91.8 us; the launch traced here: 91.6 us
  Pallas kernels  39.6 us (43%)
  waiting for transfers between devices  29.2 us (32%)
  starting transfers between devices  17.7 us (19%)
  local copies, waits for them, and re-layouts  3.43 us (4%)
    ppermute x13, waiting for transfers between devices, moved(): return lax.ppermute(value, 'ctx', pairs)  23.1 us
    pallas_call x8, Pallas kernels, attend(): pl.pallas_call(body, out_shape=shapes, in_specs=in_specs, out_specs=[spec...  21.5 us
    ppermute x13, starting transfers between devices, moved(): return lax.ppermute(value, 'ctx', pairs)  14.9 us
    pallas_call x3, Pallas kernels, load(): pl.pallas_call(functools.partial(load_kernel, strips), out_shape=[shape]...  9.16 us
    ppermute x2, waiting for transfers between devices, local(): lax.ppermute(sent, 'heads', [(i, (i + step) % n_heads) for i in range(n_h...  6.14 us
    pallas_call x3, Pallas kernels, project(): pl.pallas_call(functools.partial(project_kernel, tuple(origins), tokens,...  5.11 us
    transpose x1, local copies, waits for them, and re-layouts, local(): values = cache_values.transpose(1, 0, 2)  2.76 us
    ppermute x2, starting transfers between devices, local(): lax.ppermute(sent, 'heads', [(i, (i + step) % n_heads) for i in range(n_h...  2.15 us
  transfers between devices with their start and end apart: 21, of which 12 were waited for; matrix products, arithmetic and copies ran while one was open for 3% of the time, Pallas kernels for 40%

profile of v4, /device:TPU:0, one launch (start us, length us, event | category | flops | bytes accessed | tf_op | source)
XLA Modules:
  0.0 91.6 jit_solution(17731375453205257820)
XLA Ops:
  0.7 0.6 copy-done
  1.3 1.5 %pack.1.q_ref = bf16[1056,128]{1,0:T(8,128)(2,1)S(1)} custom-call(s32[16]{0:T(128)S(1)} %copy-done, s32[1]{0:T(128)S(6)} %copy.17.length_ref, bf16[1024,128]{1,0:T(8,128)(2,1)} %bitcast.9), custom_call_target="tpu_custom_call" | custom-call | tf_op jit(solution)/shard_map/pack/pallas_call | solution.py:98
  2.8 0.0 copy-start.1
  2.8 0.0 copy-start.2
  2.8 3.1 %collective-permute-start.1 = (bf16[1056,128]{1,0:T(8,128)(2,1)S(1)}, bf16[1056,128]{1,0:T(8,128)(2,1)S(1)}, u32[]{:S(2)}, u32[]{:S(2)}) collective-permute-start(bf16[1056,128]{1,0:T(8,128)(2,1)S(1)} %pack.1.q_ref), channel_id=1, source_target_pairs={{0,4},{4,0},{8,12},{12,8},{1,5},{5,1},{9,13},{13,9},{2,6},{6,2},{1... | collective-permute-start | bytes 811016 | tf_op jit(solution)/shard_map/ppermute | solution.py:426
  6.0 2.6 %collective-permute-start = (bf16[1056,128]{1,0:T(8,128)(2,1)S(1)}, bf16[1056,128]{1,0:T(8,128)(2,1)S(1)}, u32[]{:S(2)}, u32[]{:S(2)}) collective-permute-start(bf16[1056,128]{1,0:T(8,128)(2,1)S(1)} %pack.1.q_ref), channel_id=1, source_target_pairs={{0,8},{4,12},{8,0},{12,4},{1,9},{5,13},{9,1},{13,5},{2,10},{6,14},... | collective-permute-start | bytes 811016 | tf_op jit(solution)/shard_map/ppermute | solution.py:426
  8.5 2.8 %copy_bitcast_fusion = (bf16[4,2048,128]{2,1,0:T(8,128)(2,1)S(1)}, bf16[4,2048,128]{2,1,0:T(8,128)(2,1)S(1)}) fusion(bf16[2048,4,128]{2,1,0:T(4,128)(2,1)} %param.10, bf16[2048,4,128]{2,1,0:T(4,128)(2,1)} %param.9), kind=kLoop, calls=%fused_computation | loop fusion | bytes 8388608 | tf_op jit(solution)/shard_map/transpose | solution.py:446
  11.3 2.2 %attend.8 = bf16[528,128]{1,0:T(8,128)(2,1)S(1)} custom-call(bf16[1056,128]{1,0:T(8,128)(2,1)S(1)} %pack.1.q_ref, bf16[4,2048,128]{2,1,0:T(8,128)(2,1)S(1)} %get-tuple-element.64.k_ref, bf16[4,2048,128]{2,1,0:T(8,128)(2,1)S(1)} %get-tuple-element.63.v_ref, bf16[4,16,128]{2,1,0:T(8,128)(2,1)S(1)} %get-tuple-element.66.rest_0_, ...), custom_call_target="tpu_custom_call" | custom-call | flops 536870912 | bytes 2097152 | tf_op jit(solution)/shard_map/attend/pallas_call | solution.py:224
  13.6 3.8 %attend.9 = (bf16[528,128]{1,0:T(8,128)(2,1)S(1)}, bf16[1024,2048]{1,0:T(8,128)(2,1)S(1)}) custom-call(bf16[1056,128]{1,0:T(8,128)(2,1)S(1)} %pack.1.q_ref, bf16[4,2048,128]{2,1,0:T(8,128)(2,1)S(1)} %get-tuple-element.64.k_ref, bf16[4,2048,128]{2,1,0:T(8,128)(2,1)S(1)} %get-tuple-element.63.v_ref, bf16[4,16,128]{2,1,0:T(8,128)(2,1)S(1)} %get-tuple-element.66.rest_0_, ...), custom_call_target="tpu_custom_call" | custom-call | flops 536870912 | bytes 2097152 | tf_op jit(solution)/shard_map/attend/pallas_call | solution.py:224
  17.4 0.7 collective-permute-done.1.q_ref
  18.1 2.1 %attend.10 = bf16[528,128]{1,0:T(8,128)(2,1)S(1)} custom-call(bf16[1056,128]{1,0:T(8,128)(2,1)S(1)} %collective-permute-done.1.q_ref, bf16[4,2048,128]{2,1,0:T(8,128)(2,1)S(1)} %get-tuple-element.64.k_ref, bf16[4,2048,128]{2,1,0:T(8,128)(2,1)S(1)} %get-tuple-element.63.v_ref), custom_call_target="tpu_custom_call" | custom-call | flops 536870912 | bytes 2097152 | tf_op jit(solution)/shard_map/attend/pallas_call | solution.py:224
  20.3 0.4 collective-permute-done.q_ref
  20.6 0.4 collective-permute-start.2
  21.1 1.6 %collective-permute-start.3 = (bf16[528,128]{1,0:T(8,128)(2,1)S(1)}, bf16[528,128]{1,0:T(8,128)(2,1)S(1)}, u32[]{:S(2)}, u32[]{:S(2)}) collective-permute-start(bf16[528,128]{1,0:T(8,128)(2,1)S(1)} %attend.10), channel_id=1, source_target_pairs={{0,4},{4,0},{8,12},{12,8},{1,5},{5,1},{9,13},{13,9},{2,6},{6,2},{1... | collective-permute-start | bytes 405512 | tf_op jit(solution)/shard_map/ppermute | solution.py:426
  22.7 0.4 collective-permute-start.4
  23.1 2.1 %attend.11.refs_1_ = bf16[528,128]{1,0:T(8,128)(2,1)S(1)} custom-call(bf16[1056,128]{1,0:T(8,128)(2,1)S(1)} %collective-permute-done.1.q_ref, bf16[4,2048,128]{2,1,0:T(8,128)(2,1)S(1)} %get-tuple-element.64.k_ref, bf16[4,2048,128]{2,1,0:T(8,128)(2,1)S(1)} %get-tuple-element.63.v_ref), custom_call_target="tpu_custom_call" | custom-call | flops 536870912 | bytes 2097152 | tf_op jit(solution)/shard_map/attend/pallas_call | solution.py:224
  25.3 2.2 %attend.12 = bf16[528,128]{1,0:T(8,128)(2,1)S(1)} custom-call(bf16[1056,128]{1,0:T(8,128)(2,1)S(1)} %collective-permute-done.q_ref, bf16[4,2048,128]{2,1,0:T(8,128)(2,1)S(1)} %get-tuple-element.64.k_ref, bf16[4,2048,128]{2,1,0:T(8,128)(2,1)S(1)} %get-tuple-element.63.v_ref), custom_call_target="tpu_custom_call" | custom-call | flops 536870912 | bytes 2097152 | tf_op jit(solution)/shard_map/attend/pallas_call | solution.py:224
  27.4 4.9 %collective-permute-done.3.refs_2_ = bf16[528,128]{1,0:T(8,128)(2,1)S(1)} collective-permute-done((bf16[528,128]{1,0:T(8,128)(2,1)S(1)}, bf16[528,128]{1,0:T(8,128)(2,1)S(1)}, u32[]{:S(2)}, u32[]{:S(2)}) %collective-permute-start.3) | collective-permute-done | bytes 135200 | tf_op jit(solution)/shard_map/ppermute | solution.py:426
  32.3 1.4 %collective-permute-done.4.refs_3_ = bf16[528,128]{1,0:T(8,128)(2,1)S(1)} collective-permute-done((bf16[528,128]{1,0:T(8,128)(2,1)S(1)}, bf16[528,128]{1,0:T(8,128)(2,1)S(1)}, u32[]{:S(2)}, u32[]{:S(2)}) %collective-permute-start.4) | collective-permute-done | bytes 135200 | tf_op jit(solution)/shard_map/ppermute | solution.py:426
  33.8 0.5 combine.2.refs_0_
  34.2 1.3 %collective-permute-start.7 = (bf16[1056,128]{1,0:T(8,128)(2,1)S(1)}, bf16[1056,128]{1,0:T(8,128)(2,1)S(1)}, u32[]{:S(2)}, u32[]{:S(2)}) collective-permute-start(bf16[1056,128]{1,0:T(8,128)(2,1)S(1)} %combine.2.refs_0_), channel_id=1, source_target_pairs={{0,8},{4,12},{8,0},{12,4},{1,9},{5,13},{9,1},{13,5},{2,10},{6,14},... | collective-permute-start | bytes 811016 | tf_op jit(solution)/shard_map/ppermute | solution.py:426
  35.5 0.0 collective-permute-done.2.q_ref
  35.5 2.3 %attend.13 = bf16[528,128]{1,0:T(8,128)(2,1)S(1)} custom-call(bf16[1056,128]{1,0:T(8,128)(2,1)S(1)} %collective-permute-done.2.q_ref, bf16[4,2048,128]{2,1,0:T(8,128)(2,1)S(1)} %get-tuple-element.64.k_ref, bf16[4,2048,128]{2,1,0:T(8,128)(2,1)S(1)} %get-tuple-element.63.v_ref), custom_call_target="tpu_custom_call" | custom-call | flops 536870912 | bytes 2097152 | tf_op jit(solution)/shard_map/attend/pallas_call | solution.py:224
  37.8 1.8 %collective-permute-start.5 = (bf16[528,128]{1,0:T(8,128)(2,1)S(1)}, bf16[528,128]{1,0:T(8,128)(2,1)S(1)}, u32[]{:S(2)}, u32[]{:S(2)}) collective-permute-start(bf16[528,128]{1,0:T(8,128)(2,1)S(1)} %attend.13), channel_id=1, source_target_pairs={{0,4},{4,0},{8,12},{12,8},{1,5},{5,1},{9,13},{13,9},{2,6},{6,2},{1... | collective-permute-start | bytes 405512 | tf_op jit(solution)/shard_map/ppermute | solution.py:426
  39.6 0.3 collective-permute-start.6
  39.9 3.3 %attend.14 = (bf16[528,128]{1,0:T(8,128)(2,1)S(1)}, bf16[1024,2048]{1,0:T(8,128)(2,1)S(1)}) custom-call(bf16[1056,128]{1,0:T(8,128)(2,1)S(1)} %collective-permute-done.q_ref, bf16[4,2048,128]{2,1,0:T(8,128)(2,1)S(1)} %get-tuple-element.64.k_ref, bf16[4,2048,128]{2,1,0:T(8,128)(2,1)S(1)} %get-tuple-element.63.v_ref, bf16[8192,2048]{1,0:T(8,128)(2,1)} %w_ref.2), custom_call_target="tpu_custom_call" | custom-call | flops 536870912 | bytes 2097152 | tf_op jit(solution)/shard_map/attend/pallas_call | solution.py:224
  43.3 3.3 %attend.15 = (bf16[528,128]{1,0:T(8,128)(2,1)S(1)}, bf16[1024,2048]{1,0:T(8,128)(2,1)S(1)}) custom-call(bf16[1056,128]{1,0:T(8,128)(2,1)S(1)} %collective-permute-done.2.q_ref, bf16[4,2048,128]{2,1,0:T(8,128)(2,1)S(1)} %get-tuple-element.64.k_ref, bf16[4,2048,128]{2,1,0:T(8,128)(2,1)S(1)} %get-tuple-element.63.v_ref, bf16[8192,2048]{1,0:T(8,128)(2,1)} %w_ref.2), custom_call_target="tpu_custom_call" | custom-call | flops 536870912 | bytes 2097152 | tf_op jit(solution)/shard_map/attend/pallas_call | solution.py:224
  46.6 1.9 %collective-permute-done.5.refs_2_ = bf16[528,128]{1,0:T(8,128)(2,1)S(1)} collective-permute-done((bf16[528,128]{1,0:T(8,128)(2,1)S(1)}, bf16[528,128]{1,0:T(8,128)(2,1)S(1)}, u32[]{:S(2)}, u32[]{:S(2)}) %collective-permute-start.5) | collective-permute-done | bytes 135200 | tf_op jit(solution)/shard_map/ppermute | solution.py:426
  48.5 1.4 %collective-permute-done.6.refs_3_ = bf16[528,128]{1,0:T(8,128)(2,1)S(1)} collective-permute-done((bf16[528,128]{1,0:T(8,128)(2,1)S(1)}, bf16[528,128]{1,0:T(8,128)(2,1)S(1)}, u32[]{:S(2)}, u32[]{:S(2)}) %collective-permute-start.6) | collective-permute-done | bytes 135200 | tf_op jit(solution)/shard_map/ppermute | solution.py:426
  50.0 0.6 combine.3
  50.5 0.0 collective-permute-done.7.refs_1_
  50.5 0.6 merge.3.refs_0_
  51.2 0.1 collective-permute-start.9
  51.2 1.9 %collective-permute-start.15 = (bf16[544,128]{1,0:T(8,128)(2,1)S(1)}, bf16[544,128]{1,0:T(8,128)(2,1)S(1)}, u32[]{:S(2)}, u32[]{:S(2)}) collective-permute-start(bf16[544,128]{1,0:T(8,128)(2,1)S(1)} %get-tuple-element.47.refs_0_), channel_id=1, source_target_pairs={{0,8},{4,12},{8,0},{12,4},{1,9},{5,13},{9,1},{13,5},{2,10},{6,14},... | collective-permute-start | bytes 417800 | tf_op jit(solution)/shard_map/ppermute | solution.py:426
  53.2 1.1 %collective-permute-start.11 = (bf16[544,128]{1,0:T(8,128)(2,1)S(1)}, bf16[544,128]{1,0:T(8,128)(2,1)S(1)}, u32[]{:S(2)}, u32[]{:S(2)}) collective-permute-start(bf16[544,128]{1,0:T(8,128)(2,1)S(1)} %get-tuple-element.48.refs_2_), channel_id=1, source_target_pairs={{0,8},{4,12},{8,0},{12,4},{1,9},{5,13},{9,1},{13,5},{2,10},{6,14},... | collective-permute-start | bytes 417800 | tf_op jit(solution)/shard_map/ppermute | solution.py:426
  54.2 0.0 collective-permute-start.8
  54.2 7.9 %collective-permute-done.15.refs_1_ = bf16[544,128]{1,0:T(8,128)(2,1)S(1)} collective-permute-done((bf16[544,128]{1,0:T(8,128)(2,1)S(1)}, bf16[544,128]{1,0:T(8,128)(2,1)S(1)}, u32[]{:S(2)}, u32[]{:S(2)}) %collective-permute-start.15) | collective-permute-done | bytes 139296 | tf_op jit(solution)/shard_map/ppermute | solution.py:426
  62.1 0.3 merge.5.refs_4_
  62.5 0.1 collective-permute-start.17
  62.6 1.7 %collective-permute-done.9.refs_2_ = bf16[32,4096]{1,0:T(8,128)(2,1)S(1)} collective-permute-done((bf16[32,4096]{1,0:T(8,128)(2,1)S(1)}, bf16[32,4096]{1,0:T(8,128)(2,1)S(1)}, u32[]{:S(2)}, u32[]{:S(2)}) %collective-permute-start.9) | collective-permute-done | bytes 262176 | tf_op jit(solution)/shard_map/ppermute | solution.py:426
  64.3 0.0 collective-permute-start.10
  64.3 0.6 collective-permute-done.11.refs_1_
  64.9 0.3 merge.4.refs_4_
  65.3 0.1 collective-permute-start.13
  65.4 0.0 collective-permute-start.16
  65.4 2.1 %collective-permute-done.17.refs_6_ = bf16[32,2048]{1,0:T(8,128)(2,1)S(1)} collective-permute-done((bf16[32,2048]{1,0:T(8,128)(2,1)S(1)}, bf16[32,2048]{1,0:T(8,128)(2,1)S(1)}, u32[]{:S(2)}, u32[]{:S(2)}) %collective-permute-start.17) | collective-permute-done | bytes 131104 | tf_op jit(solution)/shard_map/ppermute | solution.py:426
  67.5 0.0 collective-permute-start.18
  67.5 3.5 %load.3 = (bf16[1024,2048]{1,0:T(8,128)(2,1)S(1)}, bf16[1024,2048]{1,0:T(8,128)(2,1)S(1)}) custom-call(bf16[8192,2048]{1,0:T(8,128)(2,1)} %w_ref.2), custom_call_target="tpu_custom_call" | custom-call | bytes 8388608 | tf_op jit(solution)/shard_map/load/pallas_call | solution.py:55
  71.0 3.5 %load.4 = (bf16[1024,2048]{1,0:T(8,128)(2,1)S(1)}, bf16[1024,2048]{1,0:T(8,128)(2,1)S(1)}) custom-call(bf16[8192,2048]{1,0:T(8,128)(2,1)} %w_ref.2), custom_call_target="tpu_custom_call" | custom-call | bytes 8388608 | tf_op jit(solution)/shard_map/load/pallas_call | solution.py:55
  74.5 0.0 collective-permute-done.8.refs_1_
  74.5 0.6 collective-permute-start.12
  75.1 0.0 collective-permute-done.13.refs_6_
  75.1 0.1 collective-permute-start.14
  75.2 0.0 collective-permute-done.10.refs_3_
  75.2 2.4 %project.3.refs_12_ = f32[128,2048]{1,0:T(8,128)S(1)} custom-call(bf16[32,4096]{1,0:T(8,128)(2,1)S(1)} %merge.3.refs_0_, bf16[32,4096]{1,0:T(8,128)(2,1)S(1)} %collective-permute-done.8.refs_1_, bf16[32,4096]{1,0:T(8,128)(2,1)S(1)} %collective-permute-done.9.refs_2_, bf16[32,4096]{1,0:T(8,128)(2,1)S(1)} %collective-permute-done.10.refs_3_, ...), custom_call_target="tpu_custom_call" | custom-call | flops 2147483648 | bytes 16777216 | tf_op jit(solution)/shard_map/project/pallas_call | solution.py:392
  77.6 2.2 %load.5.refs_11_ = bf16[1024,2048]{1,0:T(8,128)(2,1)S(1)} custom-call(bf16[8192,2048]{1,0:T(8,128)(2,1)} %w_ref.2), custom_call_target="tpu_custom_call" | custom-call | bytes 4194304 | tf_op jit(solution)/shard_map/load/pallas_call | solution.py:55
  79.8 0.0 collective-permute-done.12.refs_5_
  79.8 1.1 %project.4 = (f32[64,768]{1,0:T(8,128)S(1)}, bf16[64,768]{1,0:T(8,128)(2,1)S(1)}) custom-call(bf16[32,4096]{1,0:T(8,128)(2,1)S(1)} %merge.3.refs_0_, bf16[32,4096]{1,0:T(8,128)(2,1)S(1)} %collective-permute-done.8.refs_1_, bf16[32,4096]{1,0:T(8,128)(2,1)S(1)} %collective-permute-done.9.refs_2_, bf16[32,4096]{1,0:T(8,128)(2,1)S(1)} %collective-permute-done.10.refs_3_, ...), custom_call_target="tpu_custom_call" | custom-call | flops 805306368 | bytes 6291456 | tf_op jit(solution)/shard_map/project/pallas_call | solution.py:392
  80.9 2.0 %collective-permute-start.19 = (bf16[64,768]{1,0:T(8,128)(2,1)S(1)}, bf16[64,768]{1,0:T(8,128)(2,1)S(1)}, u32[]{:S(2)}, u32[]{:S(2)}) collective-permute-start(bf16[64,768]{1,0:T(8,128)(2,1)S(1)} %get-tuple-element.60), channel_id=1, source_target_pairs={{0,2},{2,0},{1,3},{3,1},{4,6},{6,4},{5,7},{7,5},{8,10},{10,8},{9,1... | collective-permute-start | bytes 294920 | tf_op jit(solution)/shard_map/ppermute | solution.py:633
  82.9 1.6 %project.5 = (f32[64,1280]{1,0:T(8,128)S(1)}, bf16[64,1280]{1,0:T(8,128)(2,1)S(1)}) custom-call(bf16[32,4096]{1,0:T(8,128)(2,1)S(1)} %merge.3.refs_0_, bf16[32,4096]{1,0:T(8,128)(2,1)S(1)} %collective-permute-done.8.refs_1_, bf16[32,4096]{1,0:T(8,128)(2,1)S(1)} %collective-permute-done.9.refs_2_, bf16[32,4096]{1,0:T(8,128)(2,1)S(1)} %collective-permute-done.10.refs_3_, ...), custom_call_target="tpu_custom_call" | custom-call | flops 1342177280 | bytes 10485760 | tf_op jit(solution)/shard_map/project/pallas_call | solution.py:392
  84.5 0.2 collective-permute-start.20
  84.7 1.6 %collective-permute-done.19 = bf16[64,768]{1,0:T(8,128)(2,1)S(1)} collective-permute-done((bf16[64,768]{1,0:T(8,128)(2,1)S(1)}, bf16[64,768]{1,0:T(8,128)(2,1)S(1)}, u32[]{:S(2)}, u32[]{:S(2)}) %collective-permute-start.19) | collective-permute-done | bytes 98336 | tf_op jit(solution)/shard_map/ppermute | solution.py:633
  86.3 4.5 %collective-permute-done.20 = bf16[64,1280]{1,0:T(8,128)(2,1)S(1)} collective-permute-done((bf16[64,1280]{1,0:T(8,128)(2,1)S(1)}, bf16[64,1280]{1,0:T(8,128)(2,1)S(1)}, u32[]{:S(2)}, u32[]{:S(2)}) %collective-permute-start.20) | collective-permute-done | bytes 163872 | tf_op jit(solution)/shard_map/ppermute | solution.py:633
  90.9 0.7 pad_maximum_fusion
  (9 shorter events, 0.1 us)
Async XLA Ops:
  0.7 0.7 copy-start
  2.8 8.5 %copy-start.1 = (bf16[16,4,128]{2,1,0:T(4,128)(2,1)S(1)}, bf16[16,4,128]{2,1,0:T(4,128)(2,1)}, u32[]{:S(2)}) copy-start(bf16[16,4,128]{2,1,0:T(4,128)(2,1)} %param.12) | copy-start | bytes 49156
  2.8 8.5 %copy-start.2 = (bf16[16,4,128]{2,1,0:T(4,128)(2,1)S(1)}, bf16[16,4,128]{2,1,0:T(4,128)(2,1)}, u32[]{:S(2)}) copy-start(bf16[16,4,128]{2,1,0:T(4,128)(2,1)} %param.11) | copy-start | bytes 49156
  2.8 15.3 %collective-permute-start.1 = (bf16[1056,128]{1,0:T(8,128)(2,1)S(1)}, bf16[1056,128]{1,0:T(8,128)(2,1)S(1)}, u32[]{:S(2)}, u32[]{:S(2)}) collective-permute-start(bf16[1056,128]{1,0:T(8,128)(2,1)S(1)} %pack.1.q_ref), channel_id=1, source_target_pairs={{0,4},{4,0},{8,12},{12,8},{1,5},{5,1},{9,13},{13,9},{2,6},{6,2},{1... | collective-permute-start | bytes 811016 | tf_op jit(solution)/shard_map/ppermute | solution.py:426
  6.0 14.7 %collective-permute-start = (bf16[1056,128]{1,0:T(8,128)(2,1)S(1)}, bf16[1056,128]{1,0:T(8,128)(2,1)S(1)}, u32[]{:S(2)}, u32[]{:S(2)}) collective-permute-start(bf16[1056,128]{1,0:T(8,128)(2,1)S(1)} %pack.1.q_ref), channel_id=1, source_target_pairs={{0,8},{4,12},{8,0},{12,4},{1,9},{5,13},{9,1},{13,5},{2,10},{6,14},... | collective-permute-start | bytes 811016 | tf_op jit(solution)/shard_map/ppermute | solution.py:426
  20.6 14.9 %collective-permute-start.2 = (bf16[1056,128]{1,0:T(8,128)(2,1)S(1)}, bf16[1056,128]{1,0:T(8,128)(2,1)S(1)}, u32[]{:S(2)}, u32[]{:S(2)}) collective-permute-start(bf16[1056,128]{1,0:T(8,128)(2,1)S(1)} %collective-permute-done.q_ref), channel_id=1, source_target_pairs={{0,4},{4,0},{8,12},{12,8},{1,5},{5,1},{9,13},{13,9},{2,6},{6,2},{1... | collective-permute-start | bytes 811016 | tf_op jit(solution)/shard_map/ppermute | solution.py:426
  21.1 11.2 %collective-permute-start.3 = (bf16[528,128]{1,0:T(8,128)(2,1)S(1)}, bf16[528,128]{1,0:T(8,128)(2,1)S(1)}, u32[]{:S(2)}, u32[]{:S(2)}) collective-permute-start(bf16[528,128]{1,0:T(8,128)(2,1)S(1)} %attend.10), channel_id=1, source_target_pairs={{0,4},{4,0},{8,12},{12,8},{1,5},{5,1},{9,13},{13,9},{2,6},{6,2},{1... | collective-permute-start | bytes 405512 | tf_op jit(solution)/shard_map/ppermute | solution.py:426
  22.7 11.1 %collective-permute-start.4 = (bf16[528,128]{1,0:T(8,128)(2,1)S(1)}, bf16[528,128]{1,0:T(8,128)(2,1)S(1)}, u32[]{:S(2)}, u32[]{:S(2)}) collective-permute-start(bf16[528,128]{1,0:T(8,128)(2,1)S(1)} %attend.8), channel_id=1, source_target_pairs={{0,4},{4,0},{8,12},{12,8},{1,5},{5,1},{9,13},{13,9},{2,6},{6,2},{1... | collective-permute-start | bytes 405512 | tf_op jit(solution)/shard_map/ppermute | solution.py:426
  34.2 16.3 %collective-permute-start.7 = (bf16[1056,128]{1,0:T(8,128)(2,1)S(1)}, bf16[1056,128]{1,0:T(8,128)(2,1)S(1)}, u32[]{:S(2)}, u32[]{:S(2)}) collective-permute-start(bf16[1056,128]{1,0:T(8,128)(2,1)S(1)} %combine.2.refs_0_), channel_id=1, source_target_pairs={{0,8},{4,12},{8,0},{12,4},{1,9},{5,13},{9,1},{13,5},{2,10},{6,14},... | collective-permute-start | bytes 811016 | tf_op jit(solution)/shard_map/ppermute | solution.py:426
  37.8 10.7 %collective-permute-start.5 = (bf16[528,128]{1,0:T(8,128)(2,1)S(1)}, bf16[528,128]{1,0:T(8,128)(2,1)S(1)}, u32[]{:S(2)}, u32[]{:S(2)}) collective-permute-start(bf16[528,128]{1,0:T(8,128)(2,1)S(1)} %attend.13), channel_id=1, source_target_pairs={{0,4},{4,0},{8,12},{12,8},{1,5},{5,1},{9,13},{13,9},{2,6},{6,2},{1... | collective-permute-start | bytes 405512 | tf_op jit(solution)/shard_map/ppermute | solution.py:426
  39.6 10.3 %collective-permute-start.6 = (bf16[528,128]{1,0:T(8,128)(2,1)S(1)}, bf16[528,128]{1,0:T(8,128)(2,1)S(1)}, u32[]{:S(2)}, u32[]{:S(2)}) collective-permute-start(bf16[528,128]{1,0:T(8,128)(2,1)S(1)} %attend.12), channel_id=1, source_target_pairs={{0,4},{4,0},{8,12},{12,8},{1,5},{5,1},{9,13},{13,9},{2,6},{6,2},{1... | collective-permute-start | bytes 405512 | tf_op jit(solution)/shard_map/ppermute | solution.py:426
  51.2 13.2 %collective-permute-start.9 = (bf16[32,4096]{1,0:T(8,128)(2,1)S(1)}, bf16[32,4096]{1,0:T(8,128)(2,1)S(1)}, u32[]{:S(2)}, u32[]{:S(2)}) collective-permute-start(bf16[32,4096]{1,0:T(8,128)(2,1)S(1)} %merge.3.refs_0_), channel_id=1, source_target_pairs={{0,4},{4,0},{8,12},{12,8},{1,5},{5,1},{9,13},{13,9},{2,6},{6,2},{1... | collective-permute-start | bytes 786440 | tf_op jit(solution)/shard_map/ppermute | solution.py:426
  51.2 10.9 %collective-permute-start.15 = (bf16[544,128]{1,0:T(8,128)(2,1)S(1)}, bf16[544,128]{1,0:T(8,128)(2,1)S(1)}, u32[]{:S(2)}, u32[]{:S(2)}) collective-permute-start(bf16[544,128]{1,0:T(8,128)(2,1)S(1)} %get-tuple-element.47.refs_0_), channel_id=1, source_target_pairs={{0,8},{4,12},{8,0},{12,4},{1,9},{5,13},{9,1},{13,5},{2,10},{6,14},... | collective-permute-start | bytes 417800 | tf_op jit(solution)/shard_map/ppermute | solution.py:426
  53.2 11.7 %collective-permute-start.11 = (bf16[544,128]{1,0:T(8,128)(2,1)S(1)}, bf16[544,128]{1,0:T(8,128)(2,1)S(1)}, u32[]{:S(2)}, u32[]{:S(2)}) collective-permute-start(bf16[544,128]{1,0:T(8,128)(2,1)S(1)} %get-tuple-element.48.refs_2_), channel_id=1, source_target_pairs={{0,8},{4,12},{8,0},{12,4},{1,9},{5,13},{9,1},{13,5},{2,10},{6,14},... | collective-permute-start | bytes 417800 | tf_op jit(solution)/shard_map/ppermute | solution.py:426
  54.2 20.2 %collective-permute-start.8 = (bf16[32,4096]{1,0:T(8,128)(2,1)S(1)}, bf16[32,4096]{1,0:T(8,128)(2,1)S(1)}, u32[]{:S(2)}, u32[]{:S(2)}) collective-permute-start(bf16[32,4096]{1,0:T(8,128)(2,1)S(1)} %merge.3.refs_0_), channel_id=1, source_target_pairs={{0,1},{1,0},{2,3},{3,2},{4,5},{5,4},{6,7},{7,6},{8,9},{9,8},{10,11... | collective-permute-start | bytes 786440 | tf_op jit(solution)/shard_map/ppermute | solution.py:576
  62.5 5.0 %collective-permute-start.17 = (bf16[32,2048]{1,0:T(8,128)(2,1)S(1)}, bf16[32,2048]{1,0:T(8,128)(2,1)S(1)}, u32[]{:S(2)}, u32[]{:S(2)}) collective-permute-start(bf16[32,2048]{1,0:T(8,128)(2,1)S(1)} %merge.5.refs_4_), channel_id=1, source_target_pairs={{0,4},{4,0},{8,12},{12,8},{1,5},{5,1},{9,13},{13,9},{2,6},{6,2},{1... | collective-permute-start | bytes 393224 | tf_op jit(solution)/shard_map/ppermute | solution.py:426
  64.3 10.8 %collective-permute-start.10 = (bf16[32,4096]{1,0:T(8,128)(2,1)S(1)}, bf16[32,4096]{1,0:T(8,128)(2,1)S(1)}, u32[]{:S(2)}, u32[]{:S(2)}) collective-permute-start(bf16[32,4096]{1,0:T(8,128)(2,1)S(1)} %collective-permute-done.9.refs_2_), channel_id=1, source_target_pairs={{0,1},{1,0},{2,3},{3,2},{4,5},{5,4},{6,7},{7,6},{8,9},{9,8},{10,11... | collective-permute-start | bytes 786440 | tf_op jit(solution)/shard_map/ppermute | solution.py:576
  65.3 9.8 %collective-permute-start.13 = (bf16[32,2048]{1,0:T(8,128)(2,1)S(1)}, bf16[32,2048]{1,0:T(8,128)(2,1)S(1)}, u32[]{:S(2)}, u32[]{:S(2)}) collective-permute-start(bf16[32,2048]{1,0:T(8,128)(2,1)S(1)} %merge.4.refs_4_), channel_id=1, source_target_pairs={{0,4},{4,0},{8,12},{12,8},{1,5},{5,1},{9,13},{13,9},{2,6},{6,2},{1... | collective-permute-start | bytes 393224 | tf_op jit(solution)/shard_map/ppermute | solution.py:426
  65.4 9.8 %collective-permute-start.16 = (bf16[32,2048]{1,0:T(8,128)(2,1)S(1)}, bf16[32,2048]{1,0:T(8,128)(2,1)S(1)}, u32[]{:S(2)}, u32[]{:S(2)}) collective-permute-start(bf16[32,2048]{1,0:T(8,128)(2,1)S(1)} %merge.5.refs_4_), channel_id=1, source_target_pairs={{0,1},{1,0},{2,3},{3,2},{4,5},{5,4},{6,7},{7,6},{8,9},{9,8},{10,11... | collective-permute-start | bytes 393224 | tf_op jit(solution)/shard_map/ppermute | solution.py:576
  67.5 7.6 %collective-permute-start.18 = (bf16[32,2048]{1,0:T(8,128)(2,1)S(1)}, bf16[32,2048]{1,0:T(8,128)(2,1)S(1)}, u32[]{:S(2)}, u32[]{:S(2)}) collective-permute-start(bf16[32,2048]{1,0:T(8,128)(2,1)S(1)} %collective-permute-done.17.refs_6_), channel_id=1, source_target_pairs={{0,1},{1,0},{2,3},{3,2},{4,5},{5,4},{6,7},{7,6},{8,9},{9,8},{10,11... | collective-permute-start | bytes 393224 | tf_op jit(solution)/shard_map/ppermute | solution.py:576
  74.5 5.3 %collective-permute-start.12 = (bf16[32,2048]{1,0:T(8,128)(2,1)S(1)}, bf16[32,2048]{1,0:T(8,128)(2,1)S(1)}, u32[]{:S(2)}, u32[]{:S(2)}) collective-permute-start(bf16[32,2048]{1,0:T(8,128)(2,1)S(1)} %merge.4.refs_4_), channel_id=1, source_target_pairs={{0,1},{1,0},{2,3},{3,2},{4,5},{5,4},{6,7},{7,6},{8,9},{9,8},{10,11... | collective-permute-start | bytes 393224 | tf_op jit(solution)/shard_map/ppermute | solution.py:576
  75.1 4.7 %collective-permute-start.14 = (bf16[32,2048]{1,0:T(8,128)(2,1)S(1)}, bf16[32,2048]{1,0:T(8,128)(2,1)S(1)}, u32[]{:S(2)}, u32[]{:S(2)}) collective-permute-start(bf16[32,2048]{1,0:T(8,128)(2,1)S(1)} %collective-permute-done.13.refs_6_), channel_id=1, source_target_pairs={{0,1},{1,0},{2,3},{3,2},{4,5},{5,4},{6,7},{7,6},{8,9},{9,8},{10,11... | collective-permute-start | bytes 393224 | tf_op jit(solution)/shard_map/ppermute | solution.py:576
  80.9 5.4 %collective-permute-start.19 = (bf16[64,768]{1,0:T(8,128)(2,1)S(1)}, bf16[64,768]{1,0:T(8,128)(2,1)S(1)}, u32[]{:S(2)}, u32[]{:S(2)}) collective-permute-start(bf16[64,768]{1,0:T(8,128)(2,1)S(1)} %get-tuple-element.60), channel_id=1, source_target_pairs={{0,2},{2,0},{1,3},{3,1},{4,6},{6,4},{5,7},{7,5},{8,10},{10,8},{9,1... | collective-permute-start | bytes 294920 | tf_op jit(solution)/shard_map/ppermute | solution.py:633
  84.5 6.3 %collective-permute-start.20 = (bf16[64,1280]{1,0:T(8,128)(2,1)S(1)}, bf16[64,1280]{1,0:T(8,128)(2,1)S(1)}, u32[]{:S(2)}, u32[]{:S(2)}) collective-permute-start(bf16[64,1280]{1,0:T(8,128)(2,1)S(1)} %get-tuple-element.62), channel_id=1, source_target_pairs={{0,2},{2,0},{1,3},{3,1},{4,6},{6,4},{5,7},{7,5},{8,10},{10,8},{9,1... | collective-permute-start | bytes 491528 | tf_op jit(solution)/shard_map/ppermute | solution.py:633
